TPU v7x, 256 devices: a whole 4x4x8 slice. The times are simulated.
256 devices in a mesh: pipe: 2 (over core), obs: 16 (over y, x), patch: 8 (over z).
Axes of the slice: x: 4, y: 4, z: 8, core: 2. Of those that a mesh axis runs over, the one named last changes fastest.
Arguments:
- patch_tokens: bfloat16 [4096, 2048], P('patch', 'obs'), may hold values from -40 to 40
- obs_tokens: bfloat16 [2048, 2048], P('patch', 'obs'), may hold values from -40 to 40
- footprint: int32 [32, 8], P('patch'), may hold values from 0 to 15, as said below
- list_counts: int32 [32], P('patch'), may hold values from 1 to 8
- footprint_bias: float32 [32, 8], P('patch'), may hold values from -4 to 290
- w_query: bfloat16 [2, 2048, 2048], P('pipe', None, 'obs'), may hold values from -0.125 to 0.125
- w_key: bfloat16 [2, 2048, 2048], P('pipe', None, 'obs'), may hold values from -0.125 to 0.125
- w_value: bfloat16 [2, 2048, 2048], P('pipe', None, 'obs'), may hold values from -0.125 to 0.125
- w_out: bfloat16 [2, 2048, 2048], P('pipe', 'obs'), may hold values from -0.125 to 0.125
- patch_gain: float32 [2, 2048], P('pipe'), may hold values from 0.1 to 1.9
- obs_gain: float32 [2, 2048], P('pipe'), may hold values from 0.1 to 1.9
Outputs:
- sections: bfloat16 [2, 4096, 2048], P('pipe', 'patch', 'obs')
Inputs may be any that keep to these rules, and one draw needn't show every extreme that they name: `footprint`: entries are global observation block indices. In each row the first list_counts entries (the live ones) are distinct, the rest are to be ignored. For a device along patch and any device along patch, all live entries of the first device's rows that lie in the second device's range of 2 blocks name one and the same block.
All inputs are finite; a program needn't handle non-finite values.
Results may differ from a plain program's by a relative error of at most 0.012.
Values may be sent and summed in bfloat16 or wider, within the bound.
No kernel may reach another device: no remote copies, remote signals or barrier semaphores. Data moves between devices by JAX's collectives and lax.ppermute only.
A program may use at most 64 MiB of HBM per device.

v0:
```python
import functools

import jax
import jax.numpy as jnp
from jax import lax
from jax.experimental import pallas as pl
from jax.experimental.pallas import tpu as pltpu
from jax.sharding import PartitionSpec as P


HS = 128
BLK = 128
SIDE = 4
EPS = 1e-05

SMEM = pl.BlockSpec(memory_space=pltpu.SMEM)
VMEM = pl.BlockSpec(memory_space=pltpu.VMEM)
ANY = pl.BlockSpec(memory_space=pl.ANY)
AROUND = (2, 1, 3)


def square_shift(first_axis, step):
    pairs = []
    for core in range(2):
        for row in range(SIDE):
            for col in range(SIDE):
                along_col = (core == 0) == first_axis
                new_row = row if along_col else (row + step) % SIDE
                new_col = (col + step) % SIDE if along_col else col
                base = core * SIDE * SIDE
                pairs.append((base + row * SIDE + col, base + new_row * SIDE + new_col))
    return pairs


def near(value, step):
    return lax.ppermute(value, ("pipe", "obs"), square_shift(True, step))


def far(value, step):
    return lax.ppermute(value, ("pipe", "obs"), square_shift(False, step))


def all_far(value):
    arrived = {step: far(value, step) for step in AROUND}
    return [value] + [arrived[step] for step in range(1, SIDE)]


def all_near(value):
    arrived = {step: near(value, step) for step in AROUND}
    return [value] + [arrived[step] for step in range(1, SIDE)]


def swapped(value):
    return lax.ppermute(value, "pipe", [(0, 1), (1, 0)])


def position():
    core = lax.axis_index("pipe")
    chip = lax.axis_index("obs")
    row = lax.div(chip, SIDE)
    col = lax.rem(chip, SIDE)
    near_at = jnp.where(core == 0, col, row)
    far_at = jnp.where(core == 0, row, col)
    near_stride = jnp.where(core == 0, 1, SIDE)
    far_stride = jnp.where(core == 0, SIDE, 1)
    return core, near_at, far_at, near_stride, far_stride


def wrapped(value):
    return lax.rem(value + SIDE, SIDE)


def tile_cols(block):
    return pl.ds(pl.multiple_of(block * HS, HS), HS)


def fetch(core, section, mine, theirs, target, sem, act):
    @pl.when(core == section)
    def _():
        act(pltpu.make_async_copy(mine, target, sem))

    @pl.when(core != section)
    def _():
        act(pltpu.make_async_copy(theirs, target, sem))


def start(copy):
    copy.start()


def wait(copy):
    copy.wait()


def normed_into(where, is_relative, pieces, gain, normed):
    _, near_at, far_at, near_stride, far_stride = where
    rows = normed.shape[0]
    squares = jnp.zeros((rows, HS), jnp.float32)
    for piece in pieces:
        for part in range(SIDE):
            widened = piece[part].astype(jnp.float32)
            squares = squares + widened * widened
    mean = jnp.sum(squares, axis=-1, keepdims=True) * (1.0 / (SIDE * SIDE * HS))
    inverse = lax.rsqrt(mean + EPS)
    for step, piece in enumerate(pieces):
        for part in range(SIDE):
            at = wrapped(near_at - part) if is_relative else part
            block = wrapped(far_at - step) * far_stride + at * near_stride
            scaled = (piece[part].astype(jnp.float32) * inverse) * gain[pl.ds(block, 1), :]
            normed[:, tile_cols(block)] = scaled.astype(jnp.bfloat16)


def chosen_gain(core, section, mine, theirs, index, gain):
    gain[...] = jnp.where(core == section, mine[index], theirs[index])


def key_value_kernel(
    section,
    o0,
    o1,
    o2,
    o3,
    gain_mine,
    gain_theirs,
    key_mine,
    key_theirs,
    value_mine,
    value_theirs,
    out,
    normed,
    weight,
    gain,
    sems,
):
    where = position()
    core = where[0]
    key_at, value_at = weight.at[:, :HS], weight.at[:, HS:]
    fetch(core, section, key_mine, key_theirs, key_at, sems.at[0], start)
    fetch(core, section, value_mine, value_theirs, value_at, sems.at[1], start)
    chosen_gain(core, section, gain_mine, gain_theirs, 1, gain)
    normed_into(where, True, (o0, o1, o2, o3), gain, normed)
    fetch(core, section, key_mine, key_theirs, key_at, sems.at[0], wait)
    fetch(core, section, value_mine, value_theirs, value_at, sems.at[1], wait)
    out[...] = jnp.dot(
        normed[...], weight[...], preferred_element_type=jnp.float32
    ).astype(jnp.bfloat16)


def attend_kernel(
    section,
    entries,
    counts,
    bias,
    x0,
    x1,
    x2,
    x3,
    kv_same,
    kv_other,
    gain_mine,
    gain_theirs,
    query_mine,
    query_theirs,
    out_mine,
    out_theirs,
    y0,
    y1,
    y2,
    y3,
    kept,
    normed,
    context,
    w_query,
    w_out,
    gain,
    sems,
):
    rows = normed.shape[0]
    slots = entries.shape[1]
    where = position()
    core, near_at, far_at, near_stride, far_stride = where
    place = lax.axis_index("patch")
    patch_count = kv_same.shape[0]
    fetch(core, section, query_mine, query_theirs, w_query, sems.at[0], start)
    fetch(core, section, out_mine, out_theirs, w_out, sems.at[1], start)
    chosen_gain(core, section, gain_mine, gain_theirs, 0, gain)
    normed_into(where, section == 0, (x0, x1, x2, x3), gain, normed)
    if section == 0:
        for part in range(SIDE):
            kept[part] = x0[wrapped(near_at - part)]
    fetch(core, section, query_mine, query_theirs, w_query, sems.at[0], wait)
    queries = (
        jnp.dot(normed[...], w_query[...], preferred_element_type=jnp.float32) * HS ** (-0.5)
    ).astype(jnp.bfloat16)
    blocks_here = rows // BLK
    for block in range(blocks_here):
        query = queries[block * BLK : (block + 1) * BLK]
        row = core * blocks_here + block
        live = counts[row]
        scores, values = [], []
        for slot in range(slots):
            entry = jnp.where(slot < live, entries[row, slot], 0)
            owner = lax.div(entry, 2)
            index = owner
            if section == 0:
                index = lax.rem(place - owner + patch_count, patch_count)
            is_same = (entry - owner * 2) == core
            both = jnp.where(is_same, kv_same[index], kv_other[index])
            score = lax.dot_general(
                query,
                both[:, :HS],
                (((1,), (1,)), ((), ())),
                preferred_element_type=jnp.float32,
            )
            scores.append(jnp.where(slot < live, score + bias[row, slot], -1e30))
            values.append(both[:, HS:])
        scores = jnp.concatenate(scores, axis=1)
        top = jnp.max(scores, axis=-1, keepdims=True)
        weights = jnp.exp(scores - top)
        weights = (weights / jnp.sum(weights, axis=-1, keepdims=True)).astype(jnp.bfloat16)
        context[block * BLK : (block + 1) * BLK, :] = jnp.dot(
            weights, jnp.concatenate(values, axis=0), preferred_element_type=jnp.float32
        ).astype(jnp.bfloat16)
    fetch(core, section, out_mine, out_theirs, w_out, sems.at[1], wait)
    ready = context[...]
    width = SIDE * HS
    for part in range(SIDE):
        normed[:, part * width : (part + 1) * width] = jnp.dot(
            ready, w_out[:, part * width : (part + 1) * width], preferred_element_type=jnp.float32
        ).astype(jnp.bfloat16)
    for step, out in enumerate((y0, y1, y2, y3)):
        for part in range(SIDE):
            block = wrapped(far_at + step) * far_stride + part * near_stride
            out[part] = normed[:, tile_cols(block)]


def key_values(section, pieces, gains, w_key, w_value):
    rows = pieces[0].shape[1]
    features = w_key[0].shape[0]
    return pl.pallas_call(
        functools.partial(key_value_kernel, section),
        out_shape=jax.ShapeDtypeStruct((rows, 2 * HS), jnp.bfloat16),
        in_specs=[VMEM] * 6 + [ANY] * 4,
        out_specs=VMEM,
        scratch_shapes=[
            pltpu.VMEM((rows, features), jnp.bfloat16),
            pltpu.VMEM((features, 2 * HS), jnp.bfloat16),
            pltpu.VMEM(gains[0].shape[1:], jnp.float32),
            pltpu.SemaphoreType.DMA((2,)),
        ],
        cost_estimate=pl.CostEstimate(
            flops=4 * rows * features * HS, bytes_accessed=6 * features * HS, transcendentals=0
        ),
        compiler_params=pltpu.CompilerParams(vmem_limit_bytes=8 << 20),
        name="key_values",
    )(*pieces, *gains, *w_key, *w_value)


def attend(section, lists, pieces, kv, gains, w_query, w_out):
    rows = pieces[0].shape[1]
    features = w_query[0].shape[0]
    piece = jax.ShapeDtypeStruct((SIDE, rows, HS), jnp.bfloat16)
    extra = piece if section == 0 else jax.ShapeDtypeStruct((8, HS), jnp.bfloat16)
    return pl.pallas_call(
        functools.partial(attend_kernel, section),
        out_shape=[piece] * SIDE + [extra],
        in_specs=[SMEM] * 3 + [VMEM] * 8 + [ANY] * 4,
        out_specs=[VMEM] * 5,
        scratch_shapes=[
            pltpu.VMEM((rows, features), jnp.bfloat16),
            pltpu.VMEM((rows, HS), jnp.bfloat16),
            pltpu.VMEM(w_query[0].shape, jnp.bfloat16),
            pltpu.VMEM(w_out[0].shape, jnp.bfloat16),
            pltpu.VMEM(gains[0].shape[1:], jnp.float32),
            pltpu.SemaphoreType.DMA((2,)),
        ],
        cost_estimate=pl.CostEstimate(
            flops=8 * rows * features * HS,
            bytes_accessed=16 * features * HS,
            transcendentals=rows * 1024,
        ),
        compiler_params=pltpu.CompilerParams(vmem_limit_bytes=12 << 20),
        name="attend",
    )(*lists, *pieces, *kv, *gains, *w_query, *w_out)


def added(first, others):
    total = first.astype(jnp.float32)
    for other in others:
        total = total + other.astype(jnp.float32)
    return total


def on_device(
    patch_tokens,
    obs_tokens,
    footprint,
    list_counts,
    footprint_bias,
    w_query,
    w_key,
    w_value,
    w_out,
    patch_gain,
    obs_gain,
):
    core, near_at, _, _, _ = position()
    patch_count = lax.axis_size("patch")
    patch_rows = patch_tokens.shape[0] // 2
    obs_rows = obs_tokens.shape[0] // 2
    lists = (footprint, list_counts, footprint_bias)

    my_obs = lax.dynamic_slice_in_dim(obs_tokens, core * obs_rows, obs_rows, 0)
    my_patch = lax.dynamic_slice_in_dim(patch_tokens, core * patch_rows, patch_rows, 0)
    group = jnp.stack(all_near(jnp.concatenate([my_obs, my_patch], axis=0)))
    obs_group, patch_group = group[:, :obs_rows], group[:, obs_rows:]

    gains = jnp.concatenate([patch_gain, obs_gain], axis=0).reshape(2, SIDE * SIDE, HS)
    gains, keys, values, queries, outs = [
        (mine, swapped(mine)) for mine in (gains, w_key[0], w_value[0], w_query[0], w_out[0])
    ]

    obs_pieces = all_far(obs_group)
    mine = key_values(0, obs_pieces, gains, keys, values)
    steps = sorted(range(1, patch_count), key=lambda step: -min(step, patch_count - step))
    arrived = {}
    for step in steps:
        pairs = [(at, (at + step) % patch_count) for at in range(patch_count)]
        arrived[step] = lax.ppermute(mine, "patch", pairs)
    same = jnp.stack([mine] + [arrived[step] for step in range(1, patch_count)])
    kv_zero = (same, swapped(same))
    patch_group, mine = lax.optimization_barrier((patch_group, mine))
    patch_pieces = all_far(patch_group)
    mine = key_values(1, obs_pieces, gains, keys, values)

    def reduced(parts):
        arrived = {step: far(parts[step], step) for step in AROUND}
        return added(parts[0], [arrived[step] for step in range(1, SIDE)]).astype(jnp.bfloat16)

    *parts, kept = attend(0, lists, patch_pieces, kv_zero, gains, queries, outs)
    mine, _ = lax.optimization_barrier((mine, kept))
    same = lax.all_to_all(jnp.broadcast_to(mine[None], (patch_count, *mine.shape)), "patch", 0, 0)
    kv_one = (same, swapped(same))

    total = reduced(parts)
    first, *others = all_near(total)
    after_zero = (kept.astype(jnp.float32) + added(first, others)).astype(jnp.bfloat16)

    *parts, _ = attend(1, lists, all_far(after_zero), kv_one, gains, queries, outs)
    total = reduced(parts)
    own_zero = lax.dynamic_index_in_dim(after_zero, near_at, 0, keepdims=False)
    own_total = lax.dynamic_index_in_dim(total, near_at, 0, keepdims=False)
    others = [
        near(lax.dynamic_index_in_dim(total, wrapped(near_at + step), 0, keepdims=False), step)
        for step in AROUND
    ]
    own_one = (own_zero.astype(jnp.float32) + added(own_total, others)).astype(jnp.bfloat16)

    arrived = swapped(jnp.where(core == 0, own_one, own_zero))
    upper = jnp.where(core == 0, own_zero, arrived)
    lower = jnp.where(core == 0, arrived, own_one)
    return jnp.concatenate([upper, lower], axis=0)[None]


def solution(mesh):
    in_specs = (
        P("patch", "obs"),
        P("patch", "obs"),
        P("patch", None),
        P("patch"),
        P("patch", None),
        P("pipe", None, "obs"),
        P("pipe", None, "obs"),
        P("pipe", None, "obs"),
        P("pipe", "obs", None),
        P("pipe", None),
        P("pipe", None),
    )
    out_specs = P("pipe", "patch", "obs")
    return jax.shard_map(
        on_device, mesh=mesh, in_specs=in_specs, out_specs=out_specs, check_vma=False
    )
```

profile of v0, /device:TPU:1, one launch (start us, length us, event | category | flops | bytes accessed | tf_op | source)
XLA Modules:
  0.0 156.8 jit_solution(4411519294991910472)
XLA Ops:
  0.0 3.2 %collective-permute-start.7 = (bf16[2048,128]{1,0:T(8,128)(2,1)}, bf16[2048,128]{1,0:T(8,128)(2,1)S(1)}, u32[]{:S(2)}, u32[]{:S(2)}) collective-permute-start(bf16[2048,128]{1,0:T(8,128)(2,1)} %bitcast.53), channel_id=1, source_target_pairs={{0,128},{128,0},{1,129},{129,1},{2,130},{130,2},{3,131},{131,3},{4... | collective-permute-start | bytes 1572872 | tf_op jit(solution)/shard_map/ppermute | solution.py:54
  4.1 1.4 collective-permute-start.1
  5.9 2.3 %collective-permute-start.2 = (bf16[384,128]{1,0:T(8,128)(2,1)S(1)}, bf16[384,128]{1,0:T(8,128)(2,1)S(1)}, u32[]{:S(2)}, u32[]{:S(2)}) collective-permute-start(bf16[384,128]{1,0:T(8,128)(2,1)S(1)} %get-tuple-element.33), channel_id=1, source_target_pairs={{0,24},{8,0},{16,8},{24,16},{32,56},{40,32},{48,40},{56,48},{64,88... | collective-permute-start | bytes 294920 | tf_op jit(solution)/shard_map/ppermute | solution.py:36
  10.8 1.9 %collective-permute-start.5 = (bf16[4,128,128]{2,1,0:T(8,128)(2,1)S(1)}, bf16[4,128,128]{2,1,0:T(8,128)(2,1)S(1)}, u32[]{:S(2)}, u32[]{:S(2)}) collective-permute-start(bf16[4,128,128]{2,1,0:T(8,128)(2,1)S(1)} %pad_maximum_fusion.1.o0), channel_id=1, source_target_pairs={{0,96},{8,104},{16,112},{24,120},{32,0},{40,8},{48,16},{56,24},{64... | collective-permute-start | bytes 393224 | tf_op jit(solution)/shard_map/ppermute | solution.py:40
  13.9 2.2 %collective-permute-done.5.o3 = bf16[4,128,128]{2,1,0:T(8,128)(2,1)S(1)} collective-permute-done((bf16[4,128,128]{2,1,0:T(8,128)(2,1)S(1)}, bf16[4,128,128]{2,1,0:T(8,128)(2,1)S(1)}, u32[]{:S(2)}, u32[]{:S(2)}) %collective-permute-start.5) | collective-permute-done | bytes 131104 | tf_op jit(solution)/shard_map/ppermute | solution.py:40
  16.0 2.8 %collective-permute-start.20 = (bf16[2048,128]{1,0:T(8,128)(2,1)S(1)}, bf16[2048,128]{1,0:T(8,128)(2,1)S(1)}, u32[]{:S(2)}, u32[]{:S(2)}) collective-permute-start(bf16[2048,128]{1,0:T(8,128)(2,1)S(1)} %bitcast.47), channel_id=1, source_target_pairs={{0,128},{128,0},{1,129},{129,1},{2,130},{130,2},{3,131},{131,3},{4... | collective-permute-start | bytes 1572872 | tf_op jit(solution)/shard_map/ppermute | solution.py:54
  18.9 2.6 %collective-permute-start.21 = (bf16[128,2048]{1,0:T(8,128)(2,1)S(1)}, bf16[128,2048]{1,0:T(8,128)(2,1)S(1)}, u32[]{:S(2)}, u32[]{:S(2)}) collective-permute-start(bf16[128,2048]{1,0:T(8,128)(2,1)S(1)} %bitcast.50), channel_id=1, source_target_pairs={{0,128},{128,0},{1,129},{129,1},{2,130},{130,2},{3,131},{131,3},{4... | collective-permute-start | bytes 1572872 | tf_op jit(solution)/shard_map/ppermute | solution.py:54
  24.5 5.7 %collective-permute-start.18 = (bf16[128,256]{1,0:T(8,128)(2,1)S(1)}, bf16[128,256]{1,0:T(8,128)(2,1)S(1)}, u32[]{:S(2)}, u32[]{:S(2)}) collective-permute-start(bf16[128,256]{1,0:T(8,128)(2,1)S(1)} %key_values.2), channel_id=1, source_target_pairs={{0,7},{1,0},{2,1},{3,2},{4,3},{5,4},{6,5},{7,6},{8,15},{9,8},{10,9... | collective-permute-start | bytes 196616 | tf_op jit(solution)/shard_map/ppermute | solution.py:329
  32.0 3.6 %collective-permute-done.12 = bf16[128,256]{1,0:T(8,128)(2,1)S(1)} collective-permute-done((bf16[128,256]{1,0:T(8,128)(2,1)S(1)}, bf16[128,256]{1,0:T(8,128)(2,1)S(1)}, u32[]{:S(2)}, u32[]{:S(2)}) %collective-permute-start.12) | collective-permute-done | bytes 65568 | tf_op jit(solution)/shard_map/ppermute | solution.py:329
  35.9 4.9 %collective-permute-done.13 = bf16[128,256]{1,0:T(8,128)(2,1)S(1)} collective-permute-done((bf16[128,256]{1,0:T(8,128)(2,1)S(1)}, bf16[128,256]{1,0:T(8,128)(2,1)S(1)}, u32[]{:S(2)}, u32[]{:S(2)}) %collective-permute-start.13) | collective-permute-done | bytes 65568 | tf_op jit(solution)/shard_map/ppermute | solution.py:329
  40.8 6.5 %collective-permute-done.14 = bf16[128,256]{1,0:T(8,128)(2,1)S(1)} collective-permute-done((bf16[128,256]{1,0:T(8,128)(2,1)S(1)}, bf16[128,256]{1,0:T(8,128)(2,1)S(1)}, u32[]{:S(2)}, u32[]{:S(2)}) %collective-permute-start.14) | collective-permute-done | bytes 65568 | tf_op jit(solution)/shard_map/ppermute | solution.py:329
  47.3 1.8 %collective-permute-start.15 = (bf16[128,256]{1,0:T(8,128)(2,1)S(1)}, bf16[128,256]{1,0:T(8,128)(2,1)S(1)}, u32[]{:S(2)}, u32[]{:S(2)}) collective-permute-start(bf16[128,256]{1,0:T(8,128)(2,1)S(1)} %key_values.2), channel_id=1, source_target_pairs={{0,4},{1,5},{2,6},{3,7},{4,0},{5,1},{6,2},{7,3},{8,12},{9,13},{10,... | collective-permute-start | bytes 196616 | tf_op jit(solution)/shard_map/ppermute | solution.py:329
  49.2 5.6 %collective-permute-done.15 = bf16[128,256]{1,0:T(8,128)(2,1)S(1)} collective-permute-done((bf16[128,256]{1,0:T(8,128)(2,1)S(1)}, bf16[128,256]{1,0:T(8,128)(2,1)S(1)}, u32[]{:S(2)}, u32[]{:S(2)}) %collective-permute-start.15) | collective-permute-done | bytes 65568 | tf_op jit(solution)/shard_map/ppermute | solution.py:329
  54.8 5.2 %collective-permute-done.16 = bf16[128,256]{1,0:T(8,128)(2,1)S(1)} collective-permute-done((bf16[128,256]{1,0:T(8,128)(2,1)S(1)}, bf16[128,256]{1,0:T(8,128)(2,1)S(1)}, u32[]{:S(2)}, u32[]{:S(2)}) %collective-permute-start.16) | collective-permute-done | bytes 65568 | tf_op jit(solution)/shard_map/ppermute | solution.py:329
  60.0 8.4 %collective-permute-start.19 = (bf16[8,128,256]{2,1,0:T(8,128)(2,1)S(1)}, bf16[8,128,256]{2,1,0:T(8,128)(2,1)S(1)}, u32[]{:S(2)}, u32[]{:S(2)}) collective-permute-start(bf16[8,128,256]{2,1,0:T(8,128)(2,1)S(1)} %bitcast_dynamic-update-slice_fusion.kv_same), channel_id=1, source_target_pairs={{0,128},{128,0},{1,129},{129,1},{2,130},{130,2},{3,131},{131,3},{4... | collective-permute-start | bytes 1572872 | tf_op jit(solution)/shard_map/ppermute | solution.py:54
  68.6 3.0 %collective-permute-start.11 = (bf16[4,256,128]{2,1,0:T(8,128)(2,1)S(1)}, bf16[4,256,128]{2,1,0:T(8,128)(2,1)S(1)}, u32[]{:S(2)}, u32[]{:S(2)}) collective-permute-start(bf16[4,256,128]{2,1,0:T(8,128)(2,1)S(1)} %slice.8.x0), channel_id=1, source_target_pairs={{0,96},{8,104},{16,112},{24,120},{32,0},{40,8},{48,16},{56,24},{64... | collective-permute-start | bytes 786440 | tf_op jit(solution)/shard_map/ppermute | solution.py:40
  73.1 4.6 %collective-permute-done.11.x3 = bf16[4,256,128]{2,1,0:T(8,128)(2,1)S(1)} collective-permute-done((bf16[4,256,128]{2,1,0:T(8,128)(2,1)S(1)}, bf16[4,256,128]{2,1,0:T(8,128)(2,1)S(1)}, u32[]{:S(2)}, u32[]{:S(2)}) %collective-permute-start.11) | collective-permute-done | bytes 262176 | tf_op jit(solution)/shard_map/ppermute | solution.py:40
  78.4 2.4 %collective-permute-done.9.x1 = bf16[4,256,128]{2,1,0:T(8,128)(2,1)S(1)} collective-permute-done((bf16[4,256,128]{2,1,0:T(8,128)(2,1)S(1)}, bf16[4,256,128]{2,1,0:T(8,128)(2,1)S(1)}, u32[]{:S(2)}, u32[]{:S(2)}) %collective-permute-start.9) | collective-permute-done | bytes 262176 | tf_op jit(solution)/shard_map/ppermute | solution.py:40
  80.8 3.7 %attend.2 = (bf16[4,256,128]{2,1,0:T(8,128)(2,1)S(1)}, bf16[4,256,128]{2,1,0:T(8,128)(2,1)S(1)}, bf16[4,256,128]{2,1,0:T(8,128)(2,1)S(1)}, bf16[4,256,128]{2,1,0:T(8,128)(2,1)S(1)}, bf16[4,256,128]{2,1,0:T(8,128)(2,1)S(1)}) custom-call(s32[4,8]{1,0:T(4,128)S(1)} %copy-done.7, s32[4]{0:T(128)S(1)} %copy-done.9, f32[4,8]{1,0:T(4,128)S(1)} %copy-done.8, ...), custom_call_target="tpu_custom_call" | custom-call | flops 536870912 | bytes 4194304 | tf_op jit(solution)/shard_map/attend/pallas_call | solution.py:264
  87.5 3.5 %all-to-all-start = ((bf16[8,128,256]{2,1,0:T(8,128)(2,1)}), bf16[8,128,256]{2,1,0:T(8,128)(2,1)S(1)}, u32[]{:S(2)}, u32[]{:S(2)}) async-start(bf16[8,128,256]{2,1,0:T(8,128)(2,1)} %broadcast_in_dim.4), calls=%async_computation | async-start | bytes 1048576 | tf_op jit(solution)/shard_map/all_to_all | solution.py:342
  91.1 2.1 %collective-permute-start.23 = (bf16[4,256,128]{2,1,0:T(8,128)(2,1)}, bf16[4,256,128]{2,1,0:T(8,128)(2,1)S(1)}, u32[]{:S(2)}, u32[]{:S(2)}) collective-permute-start(bf16[4,256,128]{2,1,0:T(8,128)(2,1)} %copy-done.11), channel_id=1, source_target_pairs={{0,64},{8,72},{16,80},{24,88},{32,96},{40,104},{48,112},{56,120},{... | collective-permute-start | bytes 786440 | tf_op jit(solution)/shard_map/ppermute | solution.py:40
  93.8 7.1 %collective-permute-done.22 = bf16[4,256,128]{2,1,0:T(8,128)(2,1)S(1)} collective-permute-done((bf16[4,256,128]{2,1,0:T(8,128)(2,1)}, bf16[4,256,128]{2,1,0:T(8,128)(2,1)S(1)}, u32[]{:S(2)}, u32[]{:S(2)}) %collective-permute-start.22) | collective-permute-done | bytes 262176 | tf_op jit(solution)/shard_map/ppermute | solution.py:40
  103.8 4.4 %all-to-all-done.kv_same = bf16[8,128,256]{2,1,0:T(8,128)(2,1)S(1)} async-done(((bf16[8,128,256]{2,1,0:T(8,128)(2,1)}), bf16[8,128,256]{2,1,0:T(8,128)(2,1)S(1)}, u32[]{:S(2)}, u32[]{:S(2)}) %all-to-all-start) | async-done | bytes 524320 | tf_op jit(solution)/shard_map/all_to_all | solution.py:342
  109.5 3.0 %collective-permute-done.25 = bf16[4,256,128]{2,1,0:T(8,128)(2,1)} collective-permute-done((bf16[4,256,128]{2,1,0:T(8,128)(2,1)}, bf16[4,256,128]{2,1,0:T(8,128)(2,1)}, u32[]{:S(2)}, u32[]{:S(2)}) %collective-permute-start.25) | collective-permute-done | bytes 262176 | tf_op jit(solution)/shard_map/ppermute | solution.py:36
  113.9 2.3 %collective-permute-start.30 = (bf16[4,256,128]{2,1,0:T(8,128)(2,1)S(1)}, bf16[4,256,128]{2,1,0:T(8,128)(2,1)S(1)}, u32[]{:S(2)}, u32[]{:S(2)}) collective-permute-start(bf16[4,256,128]{2,1,0:T(8,128)(2,1)S(1)} %add_convert_fusion.1.x0), channel_id=1, source_target_pairs={{0,96},{8,104},{16,112},{24,120},{32,0},{40,8},{48,16},{56,24},{64... | collective-permute-start | bytes 786440 | tf_op jit(solution)/shard_map/ppermute | solution.py:40
  116.8 5.4 %collective-permute-done.30.x3 = bf16[4,256,128]{2,1,0:T(8,128)(2,1)S(1)} collective-permute-done((bf16[4,256,128]{2,1,0:T(8,128)(2,1)S(1)}, bf16[4,256,128]{2,1,0:T(8,128)(2,1)S(1)}, u32[]{:S(2)}, u32[]{:S(2)}) %collective-permute-start.30) | collective-permute-done | bytes 262176 | tf_op jit(solution)/shard_map/ppermute | solution.py:40
  122.9 2.7 %collective-permute-done.28.x1 = bf16[4,256,128]{2,1,0:T(8,128)(2,1)S(1)} collective-permute-done((bf16[4,256,128]{2,1,0:T(8,128)(2,1)S(1)}, bf16[4,256,128]{2,1,0:T(8,128)(2,1)S(1)}, u32[]{:S(2)}, u32[]{:S(2)}) %collective-permute-start.28) | collective-permute-done | bytes 262176 | tf_op jit(solution)/shard_map/ppermute | solution.py:40
  125.7 4.4 %attend.3 = (bf16[4,256,128]{2,1,0:T(8,128)(2,1)S(1)}, bf16[4,256,128]{2,1,0:T(8,128)(2,1)}, bf16[4,256,128]{2,1,0:T(8,128)(2,1)}, bf16[4,256,128]{2,1,0:T(8,128)(2,1)}, bf16[8,128]{1,0:T(8,128)(2,1)}) custom-call(s32[4,8]{1,0:T(4,128)S(1)} %copy-done.7, s32[4]{0:T(128)S(1)} %copy-done.9, f32[4,8]{1,0:T(4,128)S(1)} %copy-done.8, ...), custom_call_target="tpu_custom_call" | custom-call | flops 536870912 | bytes 4194304 | tf_op jit(solution)/shard_map/attend/pallas_call | solution.py:264
  130.2 1.8 %collective-permute-start.33 = (bf16[4,256,128]{2,1,0:T(8,128)(2,1)}, bf16[4,256,128]{2,1,0:T(8,128)(2,1)S(1)}, u32[]{:S(2)}, u32[]{:S(2)}) collective-permute-start(bf16[4,256,128]{2,1,0:T(8,128)(2,1)} %get-tuple-element.25), channel_id=1, source_target_pairs={{0,64},{8,72},{16,80},{24,88},{32,96},{40,104},{48,112},{56,120},{... | collective-permute-start | bytes 786440 | tf_op jit(solution)/shard_map/ppermute | solution.py:40
  132.8 7.1 %collective-permute-done.32 = bf16[4,256,128]{2,1,0:T(8,128)(2,1)S(1)} collective-permute-done((bf16[4,256,128]{2,1,0:T(8,128)(2,1)}, bf16[4,256,128]{2,1,0:T(8,128)(2,1)S(1)}, u32[]{:S(2)}, u32[]{:S(2)}) %collective-permute-start.32) | collective-permute-done | bytes 262176 | tf_op jit(solution)/shard_map/ppermute | solution.py:40
  142.7 2.8 %collective-permute-done.35 = bf16[256,128]{1,0:T(8,128)(2,1)S(1)} collective-permute-done((bf16[256,128]{1,0:T(8,128)(2,1)S(1)}, bf16[256,128]{1,0:T(8,128)(2,1)S(1)}, u32[]{:S(2)}, u32[]{:S(2)}) %collective-permute-start.35) | collective-permute-done | bytes 65568 | tf_op jit(solution)/shard_map/ppermute | solution.py:36
  146.5 8.7 %collective-permute-start.38 = (bf16[256,128]{1,0:T(8,128)(2,1)S(1)}, bf16[256,128]{1,0:T(8,128)(2,1)S(1)}, u32[]{:S(2)}, u32[]{:S(2)}) collective-permute-start(bf16[256,128]{1,0:T(8,128)(2,1)S(1)} %get-tuple-element.27), channel_id=1, source_target_pairs={{0,128},{128,0},{1,129},{129,1},{2,130},{130,2},{3,131},{131,3},{4... | collective-permute-start | bytes 196616 | tf_op jit(solution)/shard_map/ppermute | solution.py:54
  (106 shorter events, 29.5 us)
Async XLA Ops:
  0.0 21.5 %collective-permute-start.7 = (bf16[2048,128]{1,0:T(8,128)(2,1)}, bf16[2048,128]{1,0:T(8,128)(2,1)S(1)}, u32[]{:S(2)}, u32[]{:S(2)}) collective-permute-start(bf16[2048,128]{1,0:T(8,128)(2,1)} %bitcast.53), channel_id=1, source_target_pairs={{0,128},{128,0},{1,129},{129,1},{2,130},{130,2},{3,131},{131,3},{4... | collective-permute-start | bytes 1572872 | tf_op jit(solution)/shard_map/ppermute | solution.py:54
  3.2 18.3 %collective-permute-start.8 = (bf16[2048,128]{1,0:T(8,128)(2,1)}, bf16[2048,128]{1,0:T(8,128)(2,1)S(1)}, u32[]{:S(2)}, u32[]{:S(2)}) collective-permute-start(bf16[2048,128]{1,0:T(8,128)(2,1)} %bitcast.56), channel_id=1, source_target_pairs={{0,128},{128,0},{1,129},{129,1},{2,130},{130,2},{3,131},{131,3},{4... | collective-permute-start | bytes 1572872 | tf_op jit(solution)/shard_map/ppermute | solution.py:54
  4.1 5.4 %collective-permute-start.1 = (bf16[384,128]{1,0:T(8,128)(2,1)S(1)}, bf16[384,128]{1,0:T(8,128)(2,1)S(1)}, u32[]{:S(2)}, u32[]{:S(2)}) collective-permute-start(bf16[384,128]{1,0:T(8,128)(2,1)S(1)} %get-tuple-element.33), channel_id=1, source_target_pairs={{0,16},{8,24},{16,0},{24,8},{32,48},{40,56},{48,32},{56,40},{64,80... | collective-permute-start | bytes 294920 | tf_op jit(solution)/shard_map/ppermute | solution.py:36
  5.5 5.3 %collective-permute-start = (bf16[384,128]{1,0:T(8,128)(2,1)S(1)}, bf16[384,128]{1,0:T(8,128)(2,1)S(1)}, u32[]{:S(2)}, u32[]{:S(2)}) collective-permute-start(bf16[384,128]{1,0:T(8,128)(2,1)S(1)} %get-tuple-element.33), channel_id=1, source_target_pairs={{0,8},{8,16},{16,24},{24,0},{32,40},{40,48},{48,56},{56,32},{64,72... | collective-permute-start | bytes 294920 | tf_op jit(solution)/shard_map/ppermute | solution.py:36
  12.7 6.1 %collective-permute-start.4 = (bf16[4,128,128]{2,1,0:T(8,128)(2,1)S(1)}, bf16[4,128,128]{2,1,0:T(8,128)(2,1)S(1)}, u32[]{:S(2)}, u32[]{:S(2)}) collective-permute-start(bf16[4,128,128]{2,1,0:T(8,128)(2,1)S(1)} %pad_maximum_fusion.1.o0), channel_id=1, source_target_pairs={{0,64},{8,72},{16,80},{24,88},{32,96},{40,104},{48,112},{56,120},{... | collective-permute-start | bytes 393224 | tf_op jit(solution)/shard_map/ppermute | solution.py:40
  13.2 8.3 %collective-permute-start.3 = (bf16[4,128,128]{2,1,0:T(8,128)(2,1)S(1)}, bf16[4,128,128]{2,1,0:T(8,128)(2,1)S(1)}, u32[]{:S(2)}, u32[]{:S(2)}) collective-permute-start(bf16[4,128,128]{2,1,0:T(8,128)(2,1)S(1)} %pad_maximum_fusion.1.o0), channel_id=1, source_target_pairs={{0,32},{8,40},{16,48},{24,56},{32,64},{40,72},{48,80},{56,88},{64,... | collective-permute-start | bytes 393224 | tf_op jit(solution)/shard_map/ppermute | solution.py:40
  16.0 55.5 %collective-permute-start.20 = (bf16[2048,128]{1,0:T(8,128)(2,1)S(1)}, bf16[2048,128]{1,0:T(8,128)(2,1)S(1)}, u32[]{:S(2)}, u32[]{:S(2)}) collective-permute-start(bf16[2048,128]{1,0:T(8,128)(2,1)S(1)} %bitcast.47), channel_id=1, source_target_pairs={{0,128},{128,0},{1,129},{129,1},{2,130},{130,2},{3,131},{131,3},{4... | collective-permute-start | bytes 1572872 | tf_op jit(solution)/shard_map/ppermute | solution.py:54
  18.9 54.2 %collective-permute-start.21 = (bf16[128,2048]{1,0:T(8,128)(2,1)S(1)}, bf16[128,2048]{1,0:T(8,128)(2,1)S(1)}, u32[]{:S(2)}, u32[]{:S(2)}) collective-permute-start(bf16[128,2048]{1,0:T(8,128)(2,1)S(1)} %bitcast.50), channel_id=1, source_target_pairs={{0,128},{128,0},{1,129},{129,1},{2,130},{130,2},{3,131},{131,3},{4... | collective-permute-start | bytes 1572872 | tf_op jit(solution)/shard_map/ppermute | solution.py:54
  24.5 35.5 %collective-permute-start.18 = (bf16[128,256]{1,0:T(8,128)(2,1)S(1)}, bf16[128,256]{1,0:T(8,128)(2,1)S(1)}, u32[]{:S(2)}, u32[]{:S(2)}) collective-permute-start(bf16[128,256]{1,0:T(8,128)(2,1)S(1)} %key_values.2), channel_id=1, source_target_pairs={{0,7},{1,0},{2,1},{3,2},{4,3},{5,4},{6,5},{7,6},{8,15},{9,8},{10,9... | collective-permute-start | bytes 196616 | tf_op jit(solution)/shard_map/ppermute | solution.py:329
  30.1 29.8 %collective-permute-start.17 = (bf16[128,256]{1,0:T(8,128)(2,1)S(1)}, bf16[128,256]{1,0:T(8,128)(2,1)S(1)}, u32[]{:S(2)}, u32[]{:S(2)}) collective-permute-start(bf16[128,256]{1,0:T(8,128)(2,1)S(1)} %key_values.2), channel_id=1, source_target_pairs={{0,6},{1,7},{2,0},{3,1},{4,2},{5,3},{6,4},{7,5},{8,14},{9,15},{10,... | collective-permute-start | bytes 196616 | tf_op jit(solution)/shard_map/ppermute | solution.py:329
  35.6 5.2 %collective-permute-start.13 = (bf16[128,256]{1,0:T(8,128)(2,1)S(1)}, bf16[128,256]{1,0:T(8,128)(2,1)S(1)}, u32[]{:S(2)}, u32[]{:S(2)}) collective-permute-start(bf16[128,256]{1,0:T(8,128)(2,1)S(1)} %key_values.2), channel_id=1, source_target_pairs={{0,2},{1,3},{2,4},{3,5},{4,6},{5,7},{6,0},{7,1},{8,10},{9,11},{10,... | collective-permute-start | bytes 196616 | tf_op jit(solution)/shard_map/ppermute | solution.py:329
  40.8 6.5 %collective-permute-start.14 = (bf16[128,256]{1,0:T(8,128)(2,1)S(1)}, bf16[128,256]{1,0:T(8,128)(2,1)S(1)}, u32[]{:S(2)}, u32[]{:S(2)}) collective-permute-start(bf16[128,256]{1,0:T(8,128)(2,1)S(1)} %key_values.2), channel_id=1, source_target_pairs={{0,3},{1,4},{2,5},{3,6},{4,7},{5,0},{6,1},{7,2},{8,11},{9,12},{10,... | collective-permute-start | bytes 196616 | tf_op jit(solution)/shard_map/ppermute | solution.py:329
  47.3 7.4 %collective-permute-start.15 = (bf16[128,256]{1,0:T(8,128)(2,1)S(1)}, bf16[128,256]{1,0:T(8,128)(2,1)S(1)}, u32[]{:S(2)}, u32[]{:S(2)}) collective-permute-start(bf16[128,256]{1,0:T(8,128)(2,1)S(1)} %key_values.2), channel_id=1, source_target_pairs={{0,4},{1,5},{2,6},{3,7},{4,0},{5,1},{6,2},{7,3},{8,12},{9,13},{10,... | collective-permute-start | bytes 196616 | tf_op jit(solution)/shard_map/ppermute | solution.py:329
  60.0 20.8 %collective-permute-start.19 = (bf16[8,128,256]{2,1,0:T(8,128)(2,1)S(1)}, bf16[8,128,256]{2,1,0:T(8,128)(2,1)S(1)}, u32[]{:S(2)}, u32[]{:S(2)}) collective-permute-start(bf16[8,128,256]{2,1,0:T(8,128)(2,1)S(1)} %bitcast_dynamic-update-slice_fusion.kv_same), channel_id=1, source_target_pairs={{0,128},{128,0},{1,129},{129,1},{2,130},{130,2},{3,131},{131,3},{4... | collective-permute-start | bytes 1572872 | tf_op jit(solution)/shard_map/ppermute | solution.py:54
  68.6 9.2 %collective-permute-start.11 = (bf16[4,256,128]{2,1,0:T(8,128)(2,1)S(1)}, bf16[4,256,128]{2,1,0:T(8,128)(2,1)S(1)}, u32[]{:S(2)}, u32[]{:S(2)}) collective-permute-start(bf16[4,256,128]{2,1,0:T(8,128)(2,1)S(1)} %slice.8.x0), channel_id=1, source_target_pairs={{0,96},{8,104},{16,112},{24,120},{32,0},{40,8},{48,16},{56,24},{64... | collective-permute-start | bytes 786440 | tf_op jit(solution)/shard_map/ppermute | solution.py:40
  71.6 6.8 %collective-permute-start.10 = (bf16[4,256,128]{2,1,0:T(8,128)(2,1)S(1)}, bf16[4,256,128]{2,1,0:T(8,128)(2,1)S(1)}, u32[]{:S(2)}, u32[]{:S(2)}) collective-permute-start(bf16[4,256,128]{2,1,0:T(8,128)(2,1)S(1)} %slice.8.x0), channel_id=1, source_target_pairs={{0,64},{8,72},{16,80},{24,88},{32,96},{40,104},{48,112},{56,120},{... | collective-permute-start | bytes 786440 | tf_op jit(solution)/shard_map/ppermute | solution.py:40
  71.6 9.2 %collective-permute-start.9 = (bf16[4,256,128]{2,1,0:T(8,128)(2,1)S(1)}, bf16[4,256,128]{2,1,0:T(8,128)(2,1)S(1)}, u32[]{:S(2)}, u32[]{:S(2)}) collective-permute-start(bf16[4,256,128]{2,1,0:T(8,128)(2,1)S(1)} %slice.8.x0), channel_id=1, source_target_pairs={{0,32},{8,40},{16,48},{24,56},{32,64},{40,72},{48,80},{56,88},{64,... | collective-permute-start | bytes 786440 | tf_op jit(solution)/shard_map/ppermute | solution.py:40
  87.5 20.7 %all-to-all-start = ((bf16[8,128,256]{2,1,0:T(8,128)(2,1)}), bf16[8,128,256]{2,1,0:T(8,128)(2,1)S(1)}, u32[]{:S(2)}, u32[]{:S(2)}) async-start(bf16[8,128,256]{2,1,0:T(8,128)(2,1)} %broadcast_in_dim.4), calls=%async_computation | async-start | bytes 1048576 | tf_op jit(solution)/shard_map/all_to_all | solution.py:342
  91.0 9.8 %collective-permute-start.22 = (bf16[4,256,128]{2,1,0:T(8,128)(2,1)}, bf16[4,256,128]{2,1,0:T(8,128)(2,1)S(1)}, u32[]{:S(2)}, u32[]{:S(2)}) collective-permute-start(bf16[4,256,128]{2,1,0:T(8,128)(2,1)} %copy-done.12), channel_id=1, source_target_pairs={{0,32},{8,40},{16,48},{24,56},{32,64},{40,72},{48,80},{56,88},{64,... | collective-permute-start | bytes 786440 | tf_op jit(solution)/shard_map/ppermute | solution.py:40
  91.1 9.7 %collective-permute-start.23 = (bf16[4,256,128]{2,1,0:T(8,128)(2,1)}, bf16[4,256,128]{2,1,0:T(8,128)(2,1)S(1)}, u32[]{:S(2)}, u32[]{:S(2)}) collective-permute-start(bf16[4,256,128]{2,1,0:T(8,128)(2,1)} %copy-done.11), channel_id=1, source_target_pairs={{0,64},{8,72},{16,80},{24,88},{32,96},{40,104},{48,112},{56,120},{... | collective-permute-start | bytes 786440 | tf_op jit(solution)/shard_map/ppermute | solution.py:40
  93.2 8.3 %collective-permute-start.24 = (bf16[4,256,128]{2,1,0:T(8,128)(2,1)}, bf16[4,256,128]{2,1,0:T(8,128)(2,1)S(1)}, u32[]{:S(2)}, u32[]{:S(2)}) collective-permute-start(bf16[4,256,128]{2,1,0:T(8,128)(2,1)} %copy-done.10), channel_id=1, source_target_pairs={{0,96},{8,104},{16,112},{24,120},{32,0},{40,8},{48,16},{56,24},{64... | collective-permute-start | bytes 786440 | tf_op jit(solution)/shard_map/ppermute | solution.py:40
  102.3 6.3 %collective-permute-start.27 = (bf16[4,256,128]{2,1,0:T(8,128)(2,1)}, bf16[4,256,128]{2,1,0:T(8,128)(2,1)S(1)}, u32[]{:S(2)}, u32[]{:S(2)}) collective-permute-start(bf16[4,256,128]{2,1,0:T(8,128)(2,1)} %add_convert_fusion.2), channel_id=1, source_target_pairs={{0,24},{8,0},{16,8},{24,16},{32,56},{40,32},{48,40},{56,48},{64,88... | collective-permute-start | bytes 786440 | tf_op jit(solution)/shard_map/ppermute | solution.py:36
  102.4 7.1 %collective-permute-start.26 = (bf16[4,256,128]{2,1,0:T(8,128)(2,1)}, bf16[4,256,128]{2,1,0:T(8,128)(2,1)}, u32[]{:S(2)}, u32[]{:S(2)}) collective-permute-start(bf16[4,256,128]{2,1,0:T(8,128)(2,1)} %add_convert_fusion.2), channel_id=1, source_target_pairs={{0,16},{8,24},{16,0},{24,8},{32,48},{40,56},{48,32},{56,40},{64,80... | collective-permute-start | bytes 786440 | tf_op jit(solution)/shard_map/ppermute | solution.py:36
  102.5 10.0 %collective-permute-start.25 = (bf16[4,256,128]{2,1,0:T(8,128)(2,1)}, bf16[4,256,128]{2,1,0:T(8,128)(2,1)}, u32[]{:S(2)}, u32[]{:S(2)}) collective-permute-start(bf16[4,256,128]{2,1,0:T(8,128)(2,1)} %add_convert_fusion.2), channel_id=1, source_target_pairs={{0,8},{8,16},{16,24},{24,0},{32,40},{40,48},{48,56},{56,32},{64,72... | collective-permute-start | bytes 786440 | tf_op jit(solution)/shard_map/ppermute | solution.py:36
  108.2 17.5 %collective-permute-start.31 = (bf16[8,128,256]{2,1,0:T(8,128)(2,1)S(1)}, bf16[8,128,256]{2,1,0:T(8,128)(2,1)S(1)}, u32[]{:S(2)}, u32[]{:S(2)}) collective-permute-start(bf16[8,128,256]{2,1,0:T(8,128)(2,1)S(1)} %all-to-all-done.kv_same), channel_id=1, source_target_pairs={{0,128},{128,0},{1,129},{129,1},{2,130},{130,2},{3,131},{131,3},{4... | collective-permute-start | bytes 1572872 | tf_op jit(solution)/shard_map/ppermute | solution.py:54
  113.9 8.4 %collective-permute-start.30 = (bf16[4,256,128]{2,1,0:T(8,128)(2,1)S(1)}, bf16[4,256,128]{2,1,0:T(8,128)(2,1)S(1)}, u32[]{:S(2)}, u32[]{:S(2)}) collective-permute-start(bf16[4,256,128]{2,1,0:T(8,128)(2,1)S(1)} %add_convert_fusion.1.x0), channel_id=1, source_target_pairs={{0,96},{8,104},{16,112},{24,120},{32,0},{40,8},{48,16},{56,24},{64... | collective-permute-start | bytes 786440 | tf_op jit(solution)/shard_map/ppermute | solution.py:40
  116.1 6.8 %collective-permute-start.29 = (bf16[4,256,128]{2,1,0:T(8,128)(2,1)S(1)}, bf16[4,256,128]{2,1,0:T(8,128)(2,1)S(1)}, u32[]{:S(2)}, u32[]{:S(2)}) collective-permute-start(bf16[4,256,128]{2,1,0:T(8,128)(2,1)S(1)} %add_convert_fusion.1.x0), channel_id=1, source_target_pairs={{0,64},{8,72},{16,80},{24,88},{32,96},{40,104},{48,112},{56,120},{... | collective-permute-start | bytes 786440 | tf_op jit(solution)/shard_map/ppermute | solution.py:40
  116.1 9.5 %collective-permute-start.28 = (bf16[4,256,128]{2,1,0:T(8,128)(2,1)S(1)}, bf16[4,256,128]{2,1,0:T(8,128)(2,1)S(1)}, u32[]{:S(2)}, u32[]{:S(2)}) collective-permute-start(bf16[4,256,128]{2,1,0:T(8,128)(2,1)S(1)} %add_convert_fusion.1.x0), channel_id=1, source_target_pairs={{0,32},{8,40},{16,48},{24,56},{32,64},{40,72},{48,80},{56,88},{64,... | collective-permute-start | bytes 786440 | tf_op jit(solution)/shard_map/ppermute | solution.py:40
  130.1 9.8 %collective-permute-start.32 = (bf16[4,256,128]{2,1,0:T(8,128)(2,1)}, bf16[4,256,128]{2,1,0:T(8,128)(2,1)S(1)}, u32[]{:S(2)}, u32[]{:S(2)}) collective-permute-start(bf16[4,256,128]{2,1,0:T(8,128)(2,1)} %get-tuple-element.24), channel_id=1, source_target_pairs={{0,32},{8,40},{16,48},{24,56},{32,64},{40,72},{48,80},{56,88},{64,... | collective-permute-start | bytes 786440 | tf_op jit(solution)/shard_map/ppermute | solution.py:40
  130.2 9.7 %collective-permute-start.33 = (bf16[4,256,128]{2,1,0:T(8,128)(2,1)}, bf16[4,256,128]{2,1,0:T(8,128)(2,1)S(1)}, u32[]{:S(2)}, u32[]{:S(2)}) collective-permute-start(bf16[4,256,128]{2,1,0:T(8,128)(2,1)} %get-tuple-element.25), channel_id=1, source_target_pairs={{0,64},{8,72},{16,80},{24,88},{32,96},{40,104},{48,112},{56,120},{... | collective-permute-start | bytes 786440 | tf_op jit(solution)/shard_map/ppermute | solution.py:40
  132.0 8.6 %collective-permute-start.34 = (bf16[4,256,128]{2,1,0:T(8,128)(2,1)}, bf16[4,256,128]{2,1,0:T(8,128)(2,1)S(1)}, u32[]{:S(2)}, u32[]{:S(2)}) collective-permute-start(bf16[4,256,128]{2,1,0:T(8,128)(2,1)} %get-tuple-element.26), channel_id=1, source_target_pairs={{0,96},{8,104},{16,112},{24,120},{32,0},{40,8},{48,16},{56,24},{64... | collective-permute-start | bytes 786440 | tf_op jit(solution)/shard_map/ppermute | solution.py:40
  146.5 9.6 %collective-permute-start.38 = (bf16[256,128]{1,0:T(8,128)(2,1)S(1)}, bf16[256,128]{1,0:T(8,128)(2,1)S(1)}, u32[]{:S(2)}, u32[]{:S(2)}) collective-permute-start(bf16[256,128]{1,0:T(8,128)(2,1)S(1)} %get-tuple-element.27), channel_id=1, source_target_pairs={{0,128},{128,0},{1,129},{129,1},{2,130},{130,2},{3,131},{131,3},{4... | collective-permute-start | bytes 196616 | tf_op jit(solution)/shard_map/ppermute | solution.py:54
  (23 other events, 137.0 us)
where the time goes:
time: 157 us
  waiting for transfers between devices  73.4 us (47%)
  starting transfers between devices  63.4 us (40%)
  Pallas kernels  9.78 us (6%)
  local copies, waits for them, and re-layouts  6 us (4%)
  other arithmetic  3.89 us (2%)
    ppermute x15, waiting for transfers between devices, far(): return lax.ppermute(value, ('pipe', 'obs'), square_shift(False, step))  34.1 us
    ppermute x8, starting transfers between devices, swapped(): return lax.ppermute(value, 'pipe', [(0, 1), (1, 0)])  27.6 us
    ppermute x7, waiting for transfers between devices, on_device(): arrived[step] = lax.ppermute(mine, 'patch', pairs)  25.8 us
    ppermute x15, starting transfers between devices, far(): return lax.ppermute(value, ('pipe', 'obs'), square_shift(False, step))  15.2 us
    ppermute x7, starting transfers between devices, on_device(): arrived[step] = lax.ppermute(mine, 'patch', pairs)  9.68 us
    ppermute x9, waiting for transfers between devices, near(): return lax.ppermute(value, ('pipe', 'obs'), square_shift(True, step))  8.21 us
    pallas_call x2, Pallas kernels, attend(): pl.pallas_call(functools.partial(attend_kernel, section), out_shape=[piec...  8.11 us
    ppermute x9, starting transfers between devices, near(): return lax.ppermute(value, ('pipe', 'obs'), square_shift(True, step))  7.49 us
  transfers between devices with their start and end apart: 40, of which 24 were waited for; matrix products, arithmetic and copies ran while one was open for 2% of the time, Pallas kernels for 1%

commit v1 on v0

--- a/solution.py
+++ b/solution.py
@@ -74,14 +74,13 @@
     return pl.ds(pl.multiple_of(block * HS, HS), HS)
 
 
-def fetch(core, section, mine, theirs, target, sem, act):
-    @pl.when(core == section)
-    def _():
-        act(pltpu.make_async_copy(mine, target, sem))
-
-    @pl.when(core != section)
-    def _():
-        act(pltpu.make_async_copy(theirs, target, sem))
+def for_core(core, copies, act):
+    for number in range(2):
+
+        @pl.when(core == number)
+        def _(number=number):
+            for copy in copies(number):
+                act(copy)
 
 
 def start(copy):
@@ -92,8 +91,17 @@
     copy.wait()
 
 
-def normed_into(where, is_relative, pieces, gain, normed):
+def placed(where, is_relative):
     _, near_at, far_at, near_stride, far_stride = where
+
+    def block(step, part):
+        at = wrapped(near_at - part) if is_relative else part
+        return wrapped(far_at - step) * far_stride + at * near_stride
+
+    return block
+
+
+def normed_into(block_of, pieces, gain, normed):
     rows = normed.shape[0]
     squares = jnp.zeros((rows, HS), jnp.float32)
     for piece in pieces:
@@ -104,8 +112,7 @@
     inverse = lax.rsqrt(mean + EPS)
     for step, piece in enumerate(pieces):
         for part in range(SIDE):
-            at = wrapped(near_at - part) if is_relative else part
-            block = wrapped(far_at - step) * far_stride + at * near_stride
+            block = block_of(step, part)
             scaled = (piece[part].astype(jnp.float32) * inverse) * gain[pl.ds(block, 1), :]
             normed[:, tile_cols(block)] = scaled.astype(jnp.bfloat16)
 
@@ -126,7 +133,8 @@
     key_theirs,
     value_mine,
     value_theirs,
-    out,
+    keep,
+    give,
     normed,
     weight,
     gain,
@@ -134,16 +142,21 @@
 ):
     where = position()
     core = where[0]
-    key_at, value_at = weight.at[:, :HS], weight.at[:, HS:]
-    fetch(core, section, key_mine, key_theirs, key_at, sems.at[0], start)
-    fetch(core, section, value_mine, value_theirs, value_at, sems.at[1], start)
+
+    def copies(number):
+        key = key_mine if number == section else key_theirs
+        value = value_mine if number == section else value_theirs
+        halves = (weight.at[:, :HS], weight.at[:, HS:])
+        yield pltpu.make_async_copy(key, halves[number], sems.at[0])
+        yield pltpu.make_async_copy(value, halves[1 - number], sems.at[1])
+
+    for_core(core, copies, start)
     chosen_gain(core, section, gain_mine, gain_theirs, 1, gain)
-    normed_into(where, True, (o0, o1, o2, o3), gain, normed)
-    fetch(core, section, key_mine, key_theirs, key_at, sems.at[0], wait)
-    fetch(core, section, value_mine, value_theirs, value_at, sems.at[1], wait)
-    out[...] = jnp.dot(
-        normed[...], weight[...], preferred_element_type=jnp.float32
-    ).astype(jnp.bfloat16)
+    normed_into(placed(where, True), (o0, o1, o2, o3), gain, normed)
+    for_core(core, copies, wait)
+    both = jnp.dot(normed[...], weight[...], preferred_element_type=jnp.float32)
+    keep[...] = both[:, :HS].astype(jnp.bfloat16)
+    give[...] = both[:, HS:].astype(jnp.bfloat16)
 
 
 def attend_kernel(
@@ -155,8 +168,8 @@
     x1,
     x2,
     x3,
-    kv_same,
-    kv_other,
+    kv_mine,
+    kv_theirs,
     gain_mine,
     gain_theirs,
     query_mine,
@@ -179,16 +192,25 @@
     slots = entries.shape[1]
     where = position()
     core, near_at, far_at, near_stride, far_stride = where
-    place = lax.axis_index("patch")
-    patch_count = kv_same.shape[0]
-    fetch(core, section, query_mine, query_theirs, w_query, sems.at[0], start)
-    fetch(core, section, out_mine, out_theirs, w_out, sems.at[1], start)
+
+    def query_copy(number):
+        yield pltpu.make_async_copy(
+            query_mine if number == section else query_theirs, w_query, sems.at[0]
+        )
+
+    def out_copy(number):
+        yield pltpu.make_async_copy(
+            out_mine if number == section else out_theirs, w_out, sems.at[1]
+        )
+
+    for_core(core, query_copy, start)
+    for_core(core, out_copy, start)
     chosen_gain(core, section, gain_mine, gain_theirs, 0, gain)
-    normed_into(where, section == 0, (x0, x1, x2, x3), gain, normed)
+    normed_into(placed(where, section == 0), (x0, x1, x2, x3), gain, normed)
     if section == 0:
         for part in range(SIDE):
             kept[part] = x0[wrapped(near_at - part)]
-    fetch(core, section, query_mine, query_theirs, w_query, sems.at[0], wait)
+    for_core(core, query_copy, wait)
     queries = (
         jnp.dot(normed[...], w_query[...], preferred_element_type=jnp.float32) * HS ** (-0.5)
     ).astype(jnp.bfloat16)
@@ -199,21 +221,16 @@
         live = counts[row]
         scores, values = [], []
         for slot in range(slots):
-            entry = jnp.where(slot < live, entries[row, slot], 0)
-            owner = lax.div(entry, 2)
-            index = owner
-            if section == 0:
-                index = lax.rem(place - owner + patch_count, patch_count)
-            is_same = (entry - owner * 2) == core
-            both = jnp.where(is_same, kv_same[index], kv_other[index])
+            owner = jnp.where(slot < live, lax.div(entries[row, slot], 2), 0)
+            mine, theirs = kv_mine[owner], kv_theirs[owner]
             score = lax.dot_general(
                 query,
-                both[:, :HS],
+                jnp.where(core == 0, mine, theirs),
                 (((1,), (1,)), ((), ())),
                 preferred_element_type=jnp.float32,
             )
             scores.append(jnp.where(slot < live, score + bias[row, slot], -1e30))
-            values.append(both[:, HS:])
+            values.append(jnp.where(core == 0, theirs, mine))
         scores = jnp.concatenate(scores, axis=1)
         top = jnp.max(scores, axis=-1, keepdims=True)
         weights = jnp.exp(scores - top)
@@ -221,7 +238,7 @@
         context[block * BLK : (block + 1) * BLK, :] = jnp.dot(
             weights, jnp.concatenate(values, axis=0), preferred_element_type=jnp.float32
         ).astype(jnp.bfloat16)
-    fetch(core, section, out_mine, out_theirs, w_out, sems.at[1], wait)
+    for_core(core, out_copy, wait)
     ready = context[...]
     width = SIDE * HS
     for part in range(SIDE):
@@ -239,9 +256,9 @@
     features = w_key[0].shape[0]
     return pl.pallas_call(
         functools.partial(key_value_kernel, section),
-        out_shape=jax.ShapeDtypeStruct((rows, 2 * HS), jnp.bfloat16),
+        out_shape=[jax.ShapeDtypeStruct((rows, HS), jnp.bfloat16)] * 2,
         in_specs=[VMEM] * 6 + [ANY] * 4,
-        out_specs=VMEM,
+        out_specs=[VMEM] * 2,
         scratch_shapes=[
             pltpu.VMEM((rows, features), jnp.bfloat16),
             pltpu.VMEM((features, 2 * HS), jnp.bfloat16),
@@ -314,39 +331,48 @@
     my_patch = lax.dynamic_slice_in_dim(patch_tokens, core * patch_rows, patch_rows, 0)
     group = jnp.stack(all_near(jnp.concatenate([my_obs, my_patch], axis=0)))
     obs_group, patch_group = group[:, :obs_rows], group[:, obs_rows:]
+    obs_pieces = all_far(obs_group)
+
+    live = jnp.arange(footprint.shape[1])[None, :] < list_counts[:, None]
+    owners = jnp.arange(patch_count)[:, None, None]
+    named = live[None] & (footprint[None] // 2 == owners)
+    needed = jnp.max(jnp.where(named, footprint[None] % 2, 0), axis=(1, 2)).astype(jnp.int32)
+    needs = lax.all_to_all(
+        jnp.broadcast_to(needed[:, None, None], (patch_count, 8, HS)), "patch", 0, 0
+    )[:, :1]
 
     gains = jnp.concatenate([patch_gain, obs_gain], axis=0).reshape(2, SIDE * SIDE, HS)
     gains, keys, values, queries, outs = [
         (mine, swapped(mine)) for mine in (gains, w_key[0], w_value[0], w_query[0], w_out[0])
     ]
 
-    obs_pieces = all_far(obs_group)
-    mine = key_values(0, obs_pieces, gains, keys, values)
-    steps = sorted(range(1, patch_count), key=lambda step: -min(step, patch_count - step))
-    arrived = {}
-    for step in steps:
-        pairs = [(at, (at + step) % patch_count) for at in range(patch_count)]
-        arrived[step] = lax.ppermute(mine, "patch", pairs)
-    same = jnp.stack([mine] + [arrived[step] for step in range(1, patch_count)])
-    kv_zero = (same, swapped(same))
-    patch_group, mine = lax.optimization_barrier((patch_group, mine))
+    def chosen(section):
+        keep, give = key_values(section, obs_pieces, gains, keys, values)
+        return keep, swapped(give), needs
+
+    def exchanged(keep, given, needs):
+        pieces = jnp.where(needs == core, keep[None], given[None])
+        mine = lax.all_to_all(pieces, "patch", 0, 0)
+        return mine, swapped(mine)
+
+    kv_zero = exchanged(*chosen(0))
     patch_pieces = all_far(patch_group)
-    mine = key_values(1, obs_pieces, gains, keys, values)
+    pieces_one = chosen(1)
 
     def reduced(parts):
         arrived = {step: far(parts[step], step) for step in AROUND}
         return added(parts[0], [arrived[step] for step in range(1, SIDE)]).astype(jnp.bfloat16)
 
     *parts, kept = attend(0, lists, patch_pieces, kv_zero, gains, queries, outs)
-    mine, _ = lax.optimization_barrier((mine, kept))
-    same = lax.all_to_all(jnp.broadcast_to(mine[None], (patch_count, *mine.shape)), "patch", 0, 0)
-    kv_one = (same, swapped(same))
+    pieces_one, _ = lax.optimization_barrier((pieces_one, kept))
+    kv_one = exchanged(*pieces_one)
 
     total = reduced(parts)
     first, *others = all_near(total)
     after_zero = (kept.astype(jnp.float32) + added(first, others)).astype(jnp.bfloat16)
 
-    *parts, _ = attend(1, lists, all_far(after_zero), kv_one, gains, queries, outs)
+    pieces = all_far(after_zero)
+    *parts, _ = attend(1, lists, pieces, kv_one, gains, queries, outs)
     total = reduced(parts)
     own_zero = lax.dynamic_index_in_dim(after_zero, near_at, 0, keepdims=False)
     own_total = lax.dynamic_index_in_dim(total, near_at, 0, keepdims=False)

time: 157 us -> 131 us (0.83)
  the two profiles are of different devices: /device:TPU:1 before, /device:TPU:47 now
where the time goes in v1:
time: 131 us
  starting transfers between devices  57.8 us (44%)
  waiting for transfers between devices  32.1 us (25%)
  blocking collectives  13.5 us (10%)
  Pallas kernels  11.6 us (9%)
  local copies, waits for them, and re-layouts  9.18 us (7%)
  other arithmetic  5.96 us (5%)
    ppermute x10, starting transfers between devices, swapped(): return lax.ppermute(value, 'pipe', [(0, 1), (1, 0)])  24.8 us
    ppermute x15, waiting for transfers between devices, far(): return lax.ppermute(value, ('pipe', 'obs'), square_shift(False, step))  23.8 us
    all_to_all x1, blocking collectives, on_device(): lax.all_to_all(jnp.broadcast_to(needed[:, None, None], (patch_count, 8, H...  13.5 us
    ppermute x9, starting transfers between devices, near(): return lax.ppermute(value, ('pipe', 'obs'), square_shift(True, step))  12.6 us
    ppermute x15, starting transfers between devices, far(): return lax.ppermute(value, ('pipe', 'obs'), square_shift(False, step))  10.8 us
    pallas_call x2, Pallas kernels, attend(): pl.pallas_call(functools.partial(attend_kernel, section), out_shape=[piec...  9.69 us
    all_to_all x2, starting transfers between devices, exchanged(): mine = lax.all_to_all(pieces, 'patch', 0, 0)  9.58 us
    unnamed x63, local copies, waits for them, and re-layouts  8.36 us
  transfers between devices with their start and end apart: 36, of which 18 were waited for; matrix products, arithmetic and copies ran while one was open for 4% of the time, Pallas kernels for 5%

profile of v1, /device:TPU:47, one launch (start us, length us, event | category | flops | bytes accessed | tf_op | source)
XLA Modules:
  0.0 130.6 jit_solution(2524346482906413662)
XLA Ops:
  1.8 1.4 %collective-permute-start = (bf16[384,128]{1,0:T(8,128)(2,1)S(1)}, bf16[384,128]{1,0:T(8,128)(2,1)S(1)}, u32[]{:S(2)}, u32[]{:S(2)}) collective-permute-start(bf16[384,128]{1,0:T(8,128)(2,1)S(1)} %get-tuple-element.43), channel_id=1, source_target_pairs={{0,8},{8,16},{16,24},{24,0},{32,40},{40,48},{48,56},{56,32},{64,72... | collective-permute-start | bytes 294920 | tf_op jit(solution)/shard_map/ppermute | solution.py:36
  4.0 2.0 %collective-permute-start.2 = (bf16[384,128]{1,0:T(8,128)(2,1)S(1)}, bf16[384,128]{1,0:T(8,128)(2,1)S(1)}, u32[]{:S(2)}, u32[]{:S(2)}) collective-permute-start(bf16[384,128]{1,0:T(8,128)(2,1)S(1)} %get-tuple-element.43), channel_id=1, source_target_pairs={{0,24},{8,0},{16,8},{24,16},{32,56},{40,32},{48,40},{56,48},{64,88... | collective-permute-start | bytes 294920 | tf_op jit(solution)/shard_map/ppermute | solution.py:36
  7.1 1.3 %collective-permute-done.1 = bf16[384,128]{1,0:T(8,128)(2,1)S(1)} collective-permute-done((bf16[384,128]{1,0:T(8,128)(2,1)S(1)}, bf16[384,128]{1,0:T(8,128)(2,1)S(1)}, u32[]{:S(2)}, u32[]{:S(2)}) %collective-permute-start.1) | collective-permute-done | bytes 98336 | tf_op jit(solution)/shard_map/ppermute | solution.py:36
  9.2 2.0 %collective-permute-start.7 = (bf16[4,128,128]{2,1,0:T(8,128)(2,1)S(1)}, bf16[4,128,128]{2,1,0:T(8,128)(2,1)S(1)}, u32[]{:S(2)}, u32[]{:S(2)}) collective-permute-start(bf16[4,128,128]{2,1,0:T(8,128)(2,1)S(1)} %pad_maximum_fusion.1.o0), channel_id=1, source_target_pairs={{0,64},{8,72},{16,80},{24,88},{32,96},{40,104},{48,112},{56,120},{... | collective-permute-start | bytes 393224 | tf_op jit(solution)/shard_map/ppermute | solution.py:40
  11.4 13.5 %all_to_all.15 = s32[8,8,128]{2,1,0:T(8,128)S(1)} all-to-all(s32[8,8,128]{2,1,0:T(8,128)S(1)} %broadcast_in_dim.76), channel_id=1, replica_groups=mesh['pipe'=2,'obs'=16,'patch'=8] {'patch'}, dimensions={0} | all-to-all | bytes 65536 | tf_op jit(solution)/shard_map/all_to_all | solution.py:340
  26.7 6.5 %collective-permute-start.12 = (bf16[128,128]{1,0:T(8,128)(2,1)S(1)}, bf16[128,128]{1,0:T(8,128)(2,1)S(1)}, u32[]{:S(2)}, u32[]{:S(2)}) collective-permute-start(bf16[128,128]{1,0:T(8,128)(2,1)S(1)} %get-tuple-element.22), channel_id=1, source_target_pairs={{0,128},{128,0},{1,129},{129,1},{2,130},{130,2},{3,131},{131,3},{4... | collective-permute-start | bytes 98312 | tf_op jit(solution)/shard_map/ppermute | solution.py:54
  34.8 5.1 %all-to-all-start.1 = ((bf16[8,128,128]{2,1,0:T(8,128)(2,1)}), bf16[8,128,128]{2,1,0:T(8,128)(2,1)}, u32[]{:S(2)}, u32[]{:S(2)}) async-start(bf16[8,128,128]{2,1,0:T(8,128)(2,1)} %broadcast_select_fusion.1), calls=%async_computation.1 | async-start | bytes 524288 | tf_op jit(solution)/shard_map/all_to_all | solution.py:355
  41.7 1.1 collective-permute-start.4
  42.9 4.3 %collective-permute-done.3.x1 = bf16[4,256,128]{2,1,0:T(8,128)(2,1)S(1)} collective-permute-done((bf16[4,256,128]{2,1,0:T(8,128)(2,1)}, bf16[4,256,128]{2,1,0:T(8,128)(2,1)S(1)}, u32[]{:S(2)}, u32[]{:S(2)}) %collective-permute-start.3) | collective-permute-done | bytes 262176 | tf_op jit(solution)/shard_map/ppermute | solution.py:40
  47.9 1.1 all-to-all-done.1.kv_mine
  49.1 2.6 %collective-permute-start.13 = (bf16[8,128,128]{2,1,0:T(8,128)(2,1)}, bf16[8,128,128]{2,1,0:T(8,128)(2,1)S(1)}, u32[]{:S(2)}, u32[]{:S(2)}) collective-permute-start(bf16[8,128,128]{2,1,0:T(8,128)(2,1)} %all-to-all-done.1.kv_mine), channel_id=1, source_target_pairs={{0,128},{128,0},{1,129},{129,1},{2,130},{130,2},{3,131},{131,3},{4... | collective-permute-start | bytes 786440 | tf_op jit(solution)/shard_map/ppermute | solution.py:54
  58.0 5.0 %attend.2 = (bf16[4,256,128]{2,1,0:T(8,128)(2,1)S(1)}, bf16[4,256,128]{2,1,0:T(8,128)(2,1)}, bf16[4,256,128]{2,1,0:T(8,128)(2,1)}, bf16[4,256,128]{2,1,0:T(8,128)(2,1)S(1)}, bf16[4,256,128]{2,1,0:T(8,128)(2,1)S(1)}) custom-call(s32[4,8]{1,0:T(4,128)S(1)} %copy-done.20, s32[4]{0:T(128)S(1)} %copy-done.25, f32[4,8]{1,0:T(4,128)S(1)} %copy-done.22, ...), custom_call_target="tpu_custom_call" | custom-call | flops 536870912 | bytes 4194304 | tf_op jit(solution)/shard_map/attend/pallas_call | solution.py:281
  63.5 1.1 collective-permute-start.17
  65.4 4.5 %all-to-all-start.2 = ((bf16[8,128,128]{2,1,0:T(8,128)(2,1)}), bf16[8,128,128]{2,1,0:T(8,128)(2,1)S(1)}, u32[]{:S(2)}, u32[]{:S(2)}) async-start(bf16[8,128,128]{2,1,0:T(8,128)(2,1)} %broadcast_select_fusion), calls=%async_computation.2 | async-start | bytes 524288 | tf_op jit(solution)/shard_map/all_to_all | solution.py:355
  70.6 2.7 %collective-permute-done.18 = bf16[4,256,128]{2,1,0:T(8,128)(2,1)} collective-permute-done((bf16[4,256,128]{2,1,0:T(8,128)(2,1)S(1)}, bf16[4,256,128]{2,1,0:T(8,128)(2,1)}, u32[]{:S(2)}, u32[]{:S(2)}) %collective-permute-start.18) | collective-permute-done | bytes 262176 | tf_op jit(solution)/shard_map/ppermute | solution.py:40
  73.3 2.0 %add_convert_fusion.2 = bf16[4,256,128]{2,1,0:T(8,128)(2,1)} fusion(bf16[4,256,128]{2,1,0:T(8,128)(2,1)} %collective-permute-done.18, bf16[4,256,128]{2,1,0:T(8,128)(2,1)} %collective-permute-done.17, bf16[4,256,128]{2,1,0:T(8,128)(2,1)} %collective-permute-done.16, bf16[4,256,128]{2,1,0:T(8,128)(2,1)S(1)} %get-tuple-element.24), kind=kLoop, calls=%fused_computation.2 | loop fusion | flops 1048576 | bytes 1310720 | tf_op jit(solution)/shard_map/convert_element_type | solution.py:364
  75.3 4.1 %collective-permute-start.20 = (bf16[4,256,128]{2,1,0:T(8,128)(2,1)}, bf16[4,256,128]{2,1,0:T(8,128)(2,1)}, u32[]{:S(2)}, u32[]{:S(2)}) collective-permute-start(bf16[4,256,128]{2,1,0:T(8,128)(2,1)} %add_convert_fusion.2), channel_id=1, source_target_pairs={{0,16},{8,24},{16,0},{24,8},{32,48},{40,56},{48,32},{56,40},{64,80... | collective-permute-start | bytes 786440 | tf_op jit(solution)/shard_map/ppermute | solution.py:36
  79.4 5.3 %collective-permute-start.26 = (bf16[8,128,128]{2,1,0:T(8,128)(2,1)S(1)}, bf16[8,128,128]{2,1,0:T(8,128)(2,1)S(1)}, u32[]{:S(2)}, u32[]{:S(2)}) collective-permute-start(bf16[8,128,128]{2,1,0:T(8,128)(2,1)S(1)} %all-to-all-done.2.kv_mine), channel_id=1, source_target_pairs={{0,128},{128,0},{1,129},{129,1},{2,130},{130,2},{3,131},{131,3},{4... | collective-permute-start | bytes 786440 | tf_op jit(solution)/shard_map/ppermute | solution.py:54
  84.7 1.9 %collective-permute-done.21 = bf16[4,256,128]{2,1,0:T(8,128)(2,1)} collective-permute-done((bf16[4,256,128]{2,1,0:T(8,128)(2,1)}, bf16[4,256,128]{2,1,0:T(8,128)(2,1)}, u32[]{:S(2)}, u32[]{:S(2)}) %collective-permute-start.21) | collective-permute-done | bytes 262176 | tf_op jit(solution)/shard_map/ppermute | solution.py:36
  86.6 1.4 %add_convert_fusion.1.x0 = bf16[4,256,128]{2,1,0:T(8,128)(2,1)S(1)} fusion(bf16[4,256,128]{2,1,0:T(8,128)(2,1)} %collective-permute-done.21, bf16[4,256,128]{2,1,0:T(8,128)(2,1)} %collective-permute-done.20, bf16[4,256,128]{2,1,0:T(8,128)(2,1)} %collective-permute-done.19, bf16[4,256,128]{2,1,0:T(8,128)(2,1)} %add_convert_fusion.2, ...), kind=kLoop, calls=%fused_computation.1 | loop fusion | flops 1310720 | bytes 1572864 | tf_op jit(solution)/shard_map/convert_element_type | solution.py:372
  87.9 1.2 collective-permute-start.22
  91.0 2.3 %collective-permute-done.22.x1 = bf16[4,256,128]{2,1,0:T(8,128)(2,1)S(1)} collective-permute-done((bf16[4,256,128]{2,1,0:T(8,128)(2,1)S(1)}, bf16[4,256,128]{2,1,0:T(8,128)(2,1)S(1)}, u32[]{:S(2)}, u32[]{:S(2)}) %collective-permute-start.22) | collective-permute-done | bytes 262176 | tf_op jit(solution)/shard_map/ppermute | solution.py:40
  93.2 2.7 %collective-permute-done.23.x2 = bf16[4,256,128]{2,1,0:T(8,128)(2,1)S(1)} collective-permute-done((bf16[4,256,128]{2,1,0:T(8,128)(2,1)S(1)}, bf16[4,256,128]{2,1,0:T(8,128)(2,1)S(1)}, u32[]{:S(2)}, u32[]{:S(2)}) %collective-permute-start.23) | collective-permute-done | bytes 262176 | tf_op jit(solution)/shard_map/ppermute | solution.py:40
  96.0 2.8 %collective-permute-done.24.x3 = bf16[4,256,128]{2,1,0:T(8,128)(2,1)S(1)} collective-permute-done((bf16[4,256,128]{2,1,0:T(8,128)(2,1)S(1)}, bf16[4,256,128]{2,1,0:T(8,128)(2,1)S(1)}, u32[]{:S(2)}, u32[]{:S(2)}) %collective-permute-start.24) | collective-permute-done | bytes 262176 | tf_op jit(solution)/shard_map/ppermute | solution.py:40
  98.8 4.7 %attend.3 = (bf16[4,256,128]{2,1,0:T(8,128)(2,1)S(1)}, bf16[4,256,128]{2,1,0:T(8,128)(2,1)}, bf16[4,256,128]{2,1,0:T(8,128)(2,1)}, bf16[4,256,128]{2,1,0:T(8,128)(2,1)}, bf16[8,128]{1,0:T(8,128)(2,1)}) custom-call(s32[4,8]{1,0:T(4,128)S(1)} %copy-done.21, s32[4]{0:T(128)S(1)} %copy-done.25, f32[4,8]{1,0:T(4,128)S(1)} %copy-done.23, ...), custom_call_target="tpu_custom_call" | custom-call | flops 536870912 | bytes 4194304 | tf_op jit(solution)/shard_map/attend/pallas_call | solution.py:281
  104.1 1.1 collective-permute-start.28
  105.7 3.4 %collective-permute-done.27 = bf16[4,256,128]{2,1,0:T(8,128)(2,1)S(1)} collective-permute-done((bf16[4,256,128]{2,1,0:T(8,128)(2,1)}, bf16[4,256,128]{2,1,0:T(8,128)(2,1)S(1)}, u32[]{:S(2)}, u32[]{:S(2)}) %collective-permute-start.27) | collective-permute-done | bytes 262176 | tf_op jit(solution)/shard_map/ppermute | solution.py:40
  109.0 2.1 %collective-permute-done.28 = bf16[4,256,128]{2,1,0:T(8,128)(2,1)S(1)} collective-permute-done((bf16[4,256,128]{2,1,0:T(8,128)(2,1)}, bf16[4,256,128]{2,1,0:T(8,128)(2,1)S(1)}, u32[]{:S(2)}, u32[]{:S(2)}) %collective-permute-start.28) | collective-permute-done | bytes 262176 | tf_op jit(solution)/shard_map/ppermute | solution.py:40
  111.1 2.8 %collective-permute-done.29 = bf16[4,256,128]{2,1,0:T(8,128)(2,1)S(1)} collective-permute-done((bf16[4,256,128]{2,1,0:T(8,128)(2,1)}, bf16[4,256,128]{2,1,0:T(8,128)(2,1)S(1)}, u32[]{:S(2)}, u32[]{:S(2)}) %collective-permute-start.29) | collective-permute-done | bytes 262176 | tf_op jit(solution)/shard_map/ppermute | solution.py:40
  114.1 2.9 %collective-permute-start.30 = (bf16[256,128]{1,0:T(8,128)(2,1)S(1)}, bf16[256,128]{1,0:T(8,128)(2,1)S(1)}, u32[]{:S(2)}, u32[]{:S(2)}) collective-permute-start(bf16[256,128]{1,0:T(8,128)(2,1)S(1)} %get-tuple-element.39), channel_id=1, source_target_pairs={{0,16},{8,24},{16,0},{24,8},{32,48},{40,56},{48,32},{56,40},{64,80... | collective-permute-start | bytes 196616 | tf_op jit(solution)/shard_map/ppermute | solution.py:36
  117.0 1.5 %collective-permute-start.32 = (bf16[256,128]{1,0:T(8,128)(2,1)S(1)}, bf16[256,128]{1,0:T(8,128)(2,1)S(1)}, u32[]{:S(2)}, u32[]{:S(2)}) collective-permute-start(bf16[256,128]{1,0:T(8,128)(2,1)S(1)} %get-tuple-element.40), channel_id=1, source_target_pairs={{0,24},{8,0},{16,8},{24,16},{32,56},{40,32},{48,40},{56,48},{64,88... | collective-permute-start | bytes 196616 | tf_op jit(solution)/shard_map/ppermute | solution.py:36
  120.4 8.6 %collective-permute-start.33 = (bf16[256,128]{1,0:T(8,128)(2,1)S(1)}, bf16[256,128]{1,0:T(8,128)(2,1)S(1)}, u32[]{:S(2)}, u32[]{:S(2)}) collective-permute-start(bf16[256,128]{1,0:T(8,128)(2,1)S(1)} %get-tuple-element.37), channel_id=1, source_target_pairs={{0,128},{128,0},{1,129},{129,1},{2,130},{130,2},{3,131},{131,3},{4... | collective-permute-start | bytes 196616 | tf_op jit(solution)/shard_map/ppermute | solution.py:54
  (131 shorter events, 25.4 us)
Async XLA Ops:
  1.8 4.8 %collective-permute-start = (bf16[384,128]{1,0:T(8,128)(2,1)S(1)}, bf16[384,128]{1,0:T(8,128)(2,1)S(1)}, u32[]{:S(2)}, u32[]{:S(2)}) collective-permute-start(bf16[384,128]{1,0:T(8,128)(2,1)S(1)} %get-tuple-element.43), channel_id=1, source_target_pairs={{0,8},{8,16},{16,24},{24,0},{32,40},{40,48},{48,56},{56,32},{64,72... | collective-permute-start | bytes 294920 | tf_op jit(solution)/shard_map/ppermute | solution.py:36
  3.1 5.3 %collective-permute-start.1 = (bf16[384,128]{1,0:T(8,128)(2,1)S(1)}, bf16[384,128]{1,0:T(8,128)(2,1)S(1)}, u32[]{:S(2)}, u32[]{:S(2)}) collective-permute-start(bf16[384,128]{1,0:T(8,128)(2,1)S(1)} %get-tuple-element.43), channel_id=1, source_target_pairs={{0,16},{8,24},{16,0},{24,8},{32,48},{40,56},{48,32},{56,40},{64,80... | collective-permute-start | bytes 294920 | tf_op jit(solution)/shard_map/ppermute | solution.py:36
  5.9 19.0 %collective-permute-start.10 = (bf16[2048,128]{1,0:T(8,128)(2,1)}, bf16[2048,128]{1,0:T(8,128)(2,1)S(1)}, u32[]{:S(2)}, u32[]{:S(2)}) collective-permute-start(bf16[2048,128]{1,0:T(8,128)(2,1)} %bitcast.42), channel_id=1, source_target_pairs={{0,128},{128,0},{1,129},{129,1},{2,130},{130,2},{3,131},{131,3},{4... | collective-permute-start | bytes 1572872 | tf_op jit(solution)/shard_map/ppermute | solution.py:54
  5.9 19.0 %collective-permute-start.11 = (bf16[2048,128]{1,0:T(8,128)(2,1)}, bf16[2048,128]{1,0:T(8,128)(2,1)S(1)}, u32[]{:S(2)}, u32[]{:S(2)}) collective-permute-start(bf16[2048,128]{1,0:T(8,128)(2,1)} %bitcast.45), channel_id=1, source_target_pairs={{0,128},{128,0},{1,129},{129,1},{2,130},{130,2},{3,131},{131,3},{4... | collective-permute-start | bytes 1572872 | tf_op jit(solution)/shard_map/ppermute | solution.py:54
  8.7 16.2 %collective-permute-start.6 = (bf16[4,128,128]{2,1,0:T(8,128)(2,1)S(1)}, bf16[4,128,128]{2,1,0:T(8,128)(2,1)S(1)}, u32[]{:S(2)}, u32[]{:S(2)}) collective-permute-start(bf16[4,128,128]{2,1,0:T(8,128)(2,1)S(1)} %pad_maximum_fusion.1.o0), channel_id=1, source_target_pairs={{0,32},{8,40},{16,48},{24,56},{32,64},{40,72},{48,80},{56,88},{64,... | collective-permute-start | bytes 393224 | tf_op jit(solution)/shard_map/ppermute | solution.py:40
  9.2 15.7 %collective-permute-start.7 = (bf16[4,128,128]{2,1,0:T(8,128)(2,1)S(1)}, bf16[4,128,128]{2,1,0:T(8,128)(2,1)S(1)}, u32[]{:S(2)}, u32[]{:S(2)}) collective-permute-start(bf16[4,128,128]{2,1,0:T(8,128)(2,1)S(1)} %pad_maximum_fusion.1.o0), channel_id=1, source_target_pairs={{0,64},{8,72},{16,80},{24,88},{32,96},{40,104},{48,112},{56,120},{... | collective-permute-start | bytes 393224 | tf_op jit(solution)/shard_map/ppermute | solution.py:40
  11.2 13.7 %collective-permute-start.8 = (bf16[4,128,128]{2,1,0:T(8,128)(2,1)S(1)}, bf16[4,128,128]{2,1,0:T(8,128)(2,1)S(1)}, u32[]{:S(2)}, u32[]{:S(2)}) collective-permute-start(bf16[4,128,128]{2,1,0:T(8,128)(2,1)S(1)} %pad_maximum_fusion.1.o0), channel_id=1, source_target_pairs={{0,96},{8,104},{16,112},{24,120},{32,0},{40,8},{48,16},{56,24},{64... | collective-permute-start | bytes 393224 | tf_op jit(solution)/shard_map/ppermute | solution.py:40
  26.7 7.3 %collective-permute-start.12 = (bf16[128,128]{1,0:T(8,128)(2,1)S(1)}, bf16[128,128]{1,0:T(8,128)(2,1)S(1)}, u32[]{:S(2)}, u32[]{:S(2)}) collective-permute-start(bf16[128,128]{1,0:T(8,128)(2,1)S(1)} %get-tuple-element.22), channel_id=1, source_target_pairs={{0,128},{128,0},{1,129},{129,1},{2,130},{130,2},{3,131},{131,3},{4... | collective-permute-start | bytes 98312 | tf_op jit(solution)/shard_map/ppermute | solution.py:54
  34.8 14.3 %all-to-all-start.1 = ((bf16[8,128,128]{2,1,0:T(8,128)(2,1)}), bf16[8,128,128]{2,1,0:T(8,128)(2,1)}, u32[]{:S(2)}, u32[]{:S(2)}) async-start(bf16[8,128,128]{2,1,0:T(8,128)(2,1)} %broadcast_select_fusion.1), calls=%async_computation.1 | async-start | bytes 524288 | tf_op jit(solution)/shard_map/all_to_all | solution.py:355
  39.9 17.6 %collective-permute-start.14 = (bf16[2048,128]{1,0:T(8,128)(2,1)S(1)}, bf16[2048,128]{1,0:T(8,128)(2,1)S(1)}, u32[]{:S(2)}, u32[]{:S(2)}) collective-permute-start(bf16[2048,128]{1,0:T(8,128)(2,1)S(1)} %bitcast.36), channel_id=1, source_target_pairs={{0,128},{128,0},{1,129},{129,1},{2,130},{130,2},{3,131},{131,3},{4... | collective-permute-start | bytes 1572872 | tf_op jit(solution)/shard_map/ppermute | solution.py:54
  41.4 5.8 %collective-permute-start.3 = (bf16[4,256,128]{2,1,0:T(8,128)(2,1)}, bf16[4,256,128]{2,1,0:T(8,128)(2,1)S(1)}, u32[]{:S(2)}, u32[]{:S(2)}) collective-permute-start(bf16[4,256,128]{2,1,0:T(8,128)(2,1)} %slice.12.x0), channel_id=1, source_target_pairs={{0,32},{8,40},{16,48},{24,56},{32,64},{40,72},{48,80},{56,88},{64,... | collective-permute-start | bytes 786440 | tf_op jit(solution)/shard_map/ppermute | solution.py:40
  41.7 15.8 %collective-permute-start.15 = (bf16[128,2048]{1,0:T(8,128)(2,1)S(1)}, bf16[128,2048]{1,0:T(8,128)(2,1)S(1)}, u32[]{:S(2)}, u32[]{:S(2)}) collective-permute-start(bf16[128,2048]{1,0:T(8,128)(2,1)S(1)} %bitcast.39), channel_id=1, source_target_pairs={{0,128},{128,0},{1,129},{129,1},{2,130},{130,2},{3,131},{131,3},{4... | collective-permute-start | bytes 1572872 | tf_op jit(solution)/shard_map/ppermute | solution.py:54
  41.7 15.7 %collective-permute-start.4 = (bf16[4,256,128]{2,1,0:T(8,128)(2,1)}, bf16[4,256,128]{2,1,0:T(8,128)(2,1)}, u32[]{:S(2)}, u32[]{:S(2)}) collective-permute-start(bf16[4,256,128]{2,1,0:T(8,128)(2,1)} %slice.12.x0), channel_id=1, source_target_pairs={{0,64},{8,72},{16,80},{24,88},{32,96},{40,104},{48,112},{56,120},{... | collective-permute-start | bytes 786440 | tf_op jit(solution)/shard_map/ppermute | solution.py:40
  42.8 14.7 %collective-permute-start.5 = (bf16[4,256,128]{2,1,0:T(8,128)(2,1)}, bf16[4,256,128]{2,1,0:T(8,128)(2,1)}, u32[]{:S(2)}, u32[]{:S(2)}) collective-permute-start(bf16[4,256,128]{2,1,0:T(8,128)(2,1)} %slice.12.x0), channel_id=1, source_target_pairs={{0,96},{8,104},{16,112},{24,120},{32,0},{40,8},{48,16},{56,24},{64... | collective-permute-start | bytes 786440 | tf_op jit(solution)/shard_map/ppermute | solution.py:40
  49.1 8.4 %collective-permute-start.13 = (bf16[8,128,128]{2,1,0:T(8,128)(2,1)}, bf16[8,128,128]{2,1,0:T(8,128)(2,1)S(1)}, u32[]{:S(2)}, u32[]{:S(2)}) collective-permute-start(bf16[8,128,128]{2,1,0:T(8,128)(2,1)} %all-to-all-done.1.kv_mine), channel_id=1, source_target_pairs={{0,128},{128,0},{1,129},{129,1},{2,130},{130,2},{3,131},{131,3},{4... | collective-permute-start | bytes 786440 | tf_op jit(solution)/shard_map/ppermute | solution.py:54
  57.4 5.7 %collective-permute-start.25 = (bf16[128,128]{1,0:T(8,128)(2,1)S(1)}, bf16[128,128]{1,0:T(8,128)(2,1)S(1)}, u32[]{:S(2)}, u32[]{:S(2)}) collective-permute-start(bf16[128,128]{1,0:T(8,128)(2,1)S(1)} %get-tuple-element.29), channel_id=1, source_target_pairs={{0,128},{128,0},{1,129},{129,1},{2,130},{130,2},{3,131},{131,3},{4... | collective-permute-start | bytes 98312 | tf_op jit(solution)/shard_map/ppermute | solution.py:54
  63.1 6.8 %collective-permute-start.16 = (bf16[4,256,128]{2,1,0:T(8,128)(2,1)}, bf16[4,256,128]{2,1,0:T(8,128)(2,1)}, u32[]{:S(2)}, u32[]{:S(2)}) collective-permute-start(bf16[4,256,128]{2,1,0:T(8,128)(2,1)} %get-tuple-element.25), channel_id=1, source_target_pairs={{0,32},{8,40},{16,48},{24,56},{32,64},{40,72},{48,80},{56,88},{64,... | collective-permute-start | bytes 786440 | tf_op jit(solution)/shard_map/ppermute | solution.py:40
  63.5 7.1 %collective-permute-start.17 = (bf16[4,256,128]{2,1,0:T(8,128)(2,1)}, bf16[4,256,128]{2,1,0:T(8,128)(2,1)}, u32[]{:S(2)}, u32[]{:S(2)}) collective-permute-start(bf16[4,256,128]{2,1,0:T(8,128)(2,1)} %get-tuple-element.26), channel_id=1, source_target_pairs={{0,64},{8,72},{16,80},{24,88},{32,96},{40,104},{48,112},{56,120},{... | collective-permute-start | bytes 786440 | tf_op jit(solution)/shard_map/ppermute | solution.py:40
  64.5 8.8 %collective-permute-start.18 = (bf16[4,256,128]{2,1,0:T(8,128)(2,1)S(1)}, bf16[4,256,128]{2,1,0:T(8,128)(2,1)}, u32[]{:S(2)}, u32[]{:S(2)}) collective-permute-start(bf16[4,256,128]{2,1,0:T(8,128)(2,1)S(1)} %get-tuple-element.27), channel_id=1, source_target_pairs={{0,96},{8,104},{16,112},{24,120},{32,0},{40,8},{48,16},{56,24},{64... | collective-permute-start | bytes 786440 | tf_op jit(solution)/shard_map/ppermute | solution.py:40
  65.4 13.9 %all-to-all-start.2 = ((bf16[8,128,128]{2,1,0:T(8,128)(2,1)}), bf16[8,128,128]{2,1,0:T(8,128)(2,1)S(1)}, u32[]{:S(2)}, u32[]{:S(2)}) async-start(bf16[8,128,128]{2,1,0:T(8,128)(2,1)} %broadcast_select_fusion), calls=%async_computation.2 | async-start | bytes 524288 | tf_op jit(solution)/shard_map/all_to_all | solution.py:355
  75.3 9.4 %collective-permute-start.19 = (bf16[4,256,128]{2,1,0:T(8,128)(2,1)}, bf16[4,256,128]{2,1,0:T(8,128)(2,1)}, u32[]{:S(2)}, u32[]{:S(2)}) collective-permute-start(bf16[4,256,128]{2,1,0:T(8,128)(2,1)} %add_convert_fusion.2), channel_id=1, source_target_pairs={{0,8},{8,16},{16,24},{24,0},{32,40},{40,48},{48,56},{56,32},{64,72... | collective-permute-start | bytes 786440 | tf_op jit(solution)/shard_map/ppermute | solution.py:36
  75.3 9.4 %collective-permute-start.20 = (bf16[4,256,128]{2,1,0:T(8,128)(2,1)}, bf16[4,256,128]{2,1,0:T(8,128)(2,1)}, u32[]{:S(2)}, u32[]{:S(2)}) collective-permute-start(bf16[4,256,128]{2,1,0:T(8,128)(2,1)} %add_convert_fusion.2), channel_id=1, source_target_pairs={{0,16},{8,24},{16,0},{24,8},{32,48},{40,56},{48,32},{56,40},{64,80... | collective-permute-start | bytes 786440 | tf_op jit(solution)/shard_map/ppermute | solution.py:36
  79.4 7.2 %collective-permute-start.21 = (bf16[4,256,128]{2,1,0:T(8,128)(2,1)}, bf16[4,256,128]{2,1,0:T(8,128)(2,1)}, u32[]{:S(2)}, u32[]{:S(2)}) collective-permute-start(bf16[4,256,128]{2,1,0:T(8,128)(2,1)} %add_convert_fusion.2), channel_id=1, source_target_pairs={{0,24},{8,0},{16,8},{24,16},{32,56},{40,32},{48,40},{56,48},{64,88... | collective-permute-start | bytes 786440 | tf_op jit(solution)/shard_map/ppermute | solution.py:36
  79.4 11.6 %collective-permute-start.26 = (bf16[8,128,128]{2,1,0:T(8,128)(2,1)S(1)}, bf16[8,128,128]{2,1,0:T(8,128)(2,1)S(1)}, u32[]{:S(2)}, u32[]{:S(2)}) collective-permute-start(bf16[8,128,128]{2,1,0:T(8,128)(2,1)S(1)} %all-to-all-done.2.kv_mine), channel_id=1, source_target_pairs={{0,128},{128,0},{1,129},{129,1},{2,130},{130,2},{3,131},{131,3},{4... | collective-permute-start | bytes 786440 | tf_op jit(solution)/shard_map/ppermute | solution.py:54
  87.9 5.3 %collective-permute-start.22 = (bf16[4,256,128]{2,1,0:T(8,128)(2,1)S(1)}, bf16[4,256,128]{2,1,0:T(8,128)(2,1)S(1)}, u32[]{:S(2)}, u32[]{:S(2)}) collective-permute-start(bf16[4,256,128]{2,1,0:T(8,128)(2,1)S(1)} %add_convert_fusion.1.x0), channel_id=1, source_target_pairs={{0,32},{8,40},{16,48},{24,56},{32,64},{40,72},{48,80},{56,88},{64,... | collective-permute-start | bytes 786440 | tf_op jit(solution)/shard_map/ppermute | solution.py:40
  89.2 6.8 %collective-permute-start.23 = (bf16[4,256,128]{2,1,0:T(8,128)(2,1)S(1)}, bf16[4,256,128]{2,1,0:T(8,128)(2,1)S(1)}, u32[]{:S(2)}, u32[]{:S(2)}) collective-permute-start(bf16[4,256,128]{2,1,0:T(8,128)(2,1)S(1)} %add_convert_fusion.1.x0), channel_id=1, source_target_pairs={{0,64},{8,72},{16,80},{24,88},{32,96},{40,104},{48,112},{56,120},{... | collective-permute-start | bytes 786440 | tf_op jit(solution)/shard_map/ppermute | solution.py:40
  90.2 8.6 %collective-permute-start.24 = (bf16[4,256,128]{2,1,0:T(8,128)(2,1)S(1)}, bf16[4,256,128]{2,1,0:T(8,128)(2,1)S(1)}, u32[]{:S(2)}, u32[]{:S(2)}) collective-permute-start(bf16[4,256,128]{2,1,0:T(8,128)(2,1)S(1)} %add_convert_fusion.1.x0), channel_id=1, source_target_pairs={{0,96},{8,104},{16,112},{24,120},{32,0},{40,8},{48,16},{56,24},{64... | collective-permute-start | bytes 786440 | tf_op jit(solution)/shard_map/ppermute | solution.py:40
  103.5 5.5 %collective-permute-start.27 = (bf16[4,256,128]{2,1,0:T(8,128)(2,1)}, bf16[4,256,128]{2,1,0:T(8,128)(2,1)S(1)}, u32[]{:S(2)}, u32[]{:S(2)}) collective-permute-start(bf16[4,256,128]{2,1,0:T(8,128)(2,1)} %get-tuple-element.34), channel_id=1, source_target_pairs={{0,32},{8,40},{16,48},{24,56},{32,64},{40,72},{48,80},{56,88},{64,... | collective-permute-start | bytes 786440 | tf_op jit(solution)/shard_map/ppermute | solution.py:40
  104.1 7.0 %collective-permute-start.28 = (bf16[4,256,128]{2,1,0:T(8,128)(2,1)}, bf16[4,256,128]{2,1,0:T(8,128)(2,1)S(1)}, u32[]{:S(2)}, u32[]{:S(2)}) collective-permute-start(bf16[4,256,128]{2,1,0:T(8,128)(2,1)} %get-tuple-element.35), channel_id=1, source_target_pairs={{0,64},{8,72},{16,80},{24,88},{32,96},{40,104},{48,112},{56,120},{... | collective-permute-start | bytes 786440 | tf_op jit(solution)/shard_map/ppermute | solution.py:40
  105.1 8.8 %collective-permute-start.29 = (bf16[4,256,128]{2,1,0:T(8,128)(2,1)}, bf16[4,256,128]{2,1,0:T(8,128)(2,1)S(1)}, u32[]{:S(2)}, u32[]{:S(2)}) collective-permute-start(bf16[4,256,128]{2,1,0:T(8,128)(2,1)} %get-tuple-element.36), channel_id=1, source_target_pairs={{0,96},{8,104},{16,112},{24,120},{32,0},{40,8},{48,16},{56,24},{64... | collective-permute-start | bytes 786440 | tf_op jit(solution)/shard_map/ppermute | solution.py:40
  114.1 5.4 %collective-permute-start.30 = (bf16[256,128]{1,0:T(8,128)(2,1)S(1)}, bf16[256,128]{1,0:T(8,128)(2,1)S(1)}, u32[]{:S(2)}, u32[]{:S(2)}) collective-permute-start(bf16[256,128]{1,0:T(8,128)(2,1)S(1)} %get-tuple-element.39), channel_id=1, source_target_pairs={{0,16},{8,24},{16,0},{24,8},{32,48},{40,56},{48,32},{56,40},{64,80... | collective-permute-start | bytes 196616 | tf_op jit(solution)/shard_map/ppermute | solution.py:36
  120.4 9.5 %collective-permute-start.33 = (bf16[256,128]{1,0:T(8,128)(2,1)S(1)}, bf16[256,128]{1,0:T(8,128)(2,1)S(1)}, u32[]{:S(2)}, u32[]{:S(2)}) collective-permute-start(bf16[256,128]{1,0:T(8,128)(2,1)S(1)} %get-tuple-element.37), channel_id=1, source_target_pairs={{0,128},{128,0},{1,129},{129,1},{2,130},{130,2},{3,131},{131,3},{4... | collective-permute-start | bytes 196616 | tf_op jit(solution)/shard_map/ppermute | solution.py:54
  (35 other events, 210.3 us)

commit v2 on v0

--- a/solution.py
+++ b/solution.py
@@ -92,8 +92,21 @@
     copy.wait()
 
 
-def normed_into(where, is_relative, pieces, gain, normed):
+def natural(step, part):
+    return step * SIDE + part
+
+
+def placed(where, is_relative):
     _, near_at, far_at, near_stride, far_stride = where
+
+    def block(step, part):
+        at = wrapped(near_at - part) if is_relative else part
+        return wrapped(far_at - step) * far_stride + at * near_stride
+
+    return block
+
+
+def normed_into(block_of, pieces, gain, normed):
     rows = normed.shape[0]
     squares = jnp.zeros((rows, HS), jnp.float32)
     for piece in pieces:
@@ -104,8 +117,7 @@
     inverse = lax.rsqrt(mean + EPS)
     for step, piece in enumerate(pieces):
         for part in range(SIDE):
-            at = wrapped(near_at - part) if is_relative else part
-            block = wrapped(far_at - step) * far_stride + at * near_stride
+            block = block_of(step, part)
             scaled = (piece[part].astype(jnp.float32) * inverse) * gain[pl.ds(block, 1), :]
             normed[:, tile_cols(block)] = scaled.astype(jnp.bfloat16)
 
@@ -116,10 +128,7 @@
 
 def key_value_kernel(
     section,
-    o0,
-    o1,
-    o2,
-    o3,
+    obs,
     gain_mine,
     gain_theirs,
     key_mine,
@@ -132,13 +141,13 @@
     gain,
     sems,
 ):
-    where = position()
-    core = where[0]
+    core = lax.axis_index("pipe")
     key_at, value_at = weight.at[:, :HS], weight.at[:, HS:]
     fetch(core, section, key_mine, key_theirs, key_at, sems.at[0], start)
     fetch(core, section, value_mine, value_theirs, value_at, sems.at[1], start)
     chosen_gain(core, section, gain_mine, gain_theirs, 1, gain)
-    normed_into(where, True, (o0, o1, o2, o3), gain, normed)
+    pieces = [obs.at[step * SIDE : (step + 1) * SIDE] for step in range(SIDE)]
+    normed_into(natural, pieces, gain, normed)
     fetch(core, section, key_mine, key_theirs, key_at, sems.at[0], wait)
     fetch(core, section, value_mine, value_theirs, value_at, sems.at[1], wait)
     out[...] = jnp.dot(
@@ -184,7 +193,7 @@
     fetch(core, section, query_mine, query_theirs, w_query, sems.at[0], start)
     fetch(core, section, out_mine, out_theirs, w_out, sems.at[1], start)
     chosen_gain(core, section, gain_mine, gain_theirs, 0, gain)
-    normed_into(where, section == 0, (x0, x1, x2, x3), gain, normed)
+    normed_into(placed(where, section == 0), (x0, x1, x2, x3), gain, normed)
     if section == 0:
         for part in range(SIDE):
             kept[part] = x0[wrapped(near_at - part)]
@@ -201,9 +210,7 @@
         for slot in range(slots):
             entry = jnp.where(slot < live, entries[row, slot], 0)
             owner = lax.div(entry, 2)
-            index = owner
-            if section == 0:
-                index = lax.rem(place - owner + patch_count, patch_count)
+            index = lax.rem(place - owner + patch_count, patch_count)
             is_same = (entry - owner * 2) == core
             both = jnp.where(is_same, kv_same[index], kv_other[index])
             score = lax.dot_general(
@@ -217,7 +224,7 @@
         scores = jnp.concatenate(scores, axis=1)
         top = jnp.max(scores, axis=-1, keepdims=True)
         weights = jnp.exp(scores - top)
-        weights = (weights / jnp.sum(weights, axis=-1, keepdims=True)).astype(jnp.bfloat16)
+        weights = (weights * (1.0 / jnp.sum(weights, axis=-1, keepdims=True))).astype(jnp.bfloat16)
         context[block * BLK : (block + 1) * BLK, :] = jnp.dot(
             weights, jnp.concatenate(values, axis=0), preferred_element_type=jnp.float32
         ).astype(jnp.bfloat16)
@@ -234,13 +241,13 @@
             out[part] = normed[:, tile_cols(block)]
 
 
-def key_values(section, pieces, gains, w_key, w_value):
-    rows = pieces[0].shape[1]
+def key_values(section, obs, gains, w_key, w_value):
+    rows = obs.shape[1]
     features = w_key[0].shape[0]
     return pl.pallas_call(
         functools.partial(key_value_kernel, section),
         out_shape=jax.ShapeDtypeStruct((rows, 2 * HS), jnp.bfloat16),
-        in_specs=[VMEM] * 6 + [ANY] * 4,
+        in_specs=[VMEM] * 3 + [ANY] * 4,
         out_specs=VMEM,
         scratch_shapes=[
             pltpu.VMEM((rows, features), jnp.bfloat16),
@@ -253,7 +260,7 @@
         ),
         compiler_params=pltpu.CompilerParams(vmem_limit_bytes=8 << 20),
         name="key_values",
-    )(*pieces, *gains, *w_key, *w_value)
+    )(obs, *gains, *w_key, *w_value)
 
 
 def attend(section, lists, pieces, kv, gains, w_query, w_out):
@@ -311,27 +318,33 @@
     lists = (footprint, list_counts, footprint_bias)
 
     my_obs = lax.dynamic_slice_in_dim(obs_tokens, core * obs_rows, obs_rows, 0)
+    obs = lax.all_to_all(
+        jnp.broadcast_to(my_obs[None], (lax.axis_size("obs"), *my_obs.shape)), "obs", 0, 0
+    )
     my_patch = lax.dynamic_slice_in_dim(patch_tokens, core * patch_rows, patch_rows, 0)
-    group = jnp.stack(all_near(jnp.concatenate([my_obs, my_patch], axis=0)))
-    obs_group, patch_group = group[:, :obs_rows], group[:, obs_rows:]
+    patch_group = jnp.stack(all_near(my_patch))
 
     gains = jnp.concatenate([patch_gain, obs_gain], axis=0).reshape(2, SIDE * SIDE, HS)
     gains, keys, values, queries, outs = [
         (mine, swapped(mine)) for mine in (gains, w_key[0], w_value[0], w_query[0], w_out[0])
     ]
 
-    obs_pieces = all_far(obs_group)
-    mine = key_values(0, obs_pieces, gains, keys, values)
-    steps = sorted(range(1, patch_count), key=lambda step: -min(step, patch_count - step))
-    arrived = {}
-    for step in steps:
-        pairs = [(at, (at + step) % patch_count) for at in range(patch_count)]
-        arrived[step] = lax.ppermute(mine, "patch", pairs)
+    mine = key_values(0, obs, gains, keys, values)
+
+    def to_patch(value, steps):
+        return {
+            step: lax.ppermute(
+                value, "patch", [(at, (at + step) % patch_count) for at in range(patch_count)]
+            )
+            for step in steps
+        }
+
+    arrived = to_patch(mine, (4, 3, 5)) | to_patch(mine, (2, 6, 1, 7))
     same = jnp.stack([mine] + [arrived[step] for step in range(1, patch_count)])
     kv_zero = (same, swapped(same))
     patch_group, mine = lax.optimization_barrier((patch_group, mine))
     patch_pieces = all_far(patch_group)
-    mine = key_values(1, obs_pieces, gains, keys, values)
+    mine = key_values(1, obs, gains, keys, values)
 
     def reduced(parts):
         arrived = {step: far(parts[step], step) for step in AROUND}
@@ -339,27 +352,49 @@
 
     *parts, kept = attend(0, lists, patch_pieces, kv_zero, gains, queries, outs)
     mine, _ = lax.optimization_barrier((mine, kept))
-    same = lax.all_to_all(jnp.broadcast_to(mine[None], (patch_count, *mine.shape)), "patch", 0, 0)
+    arrived = to_patch(mine, (4, 1)) | to_patch(mine, (3, 5))
+    arrived |= to_patch(mine, (2, 6, 7))
+    same = jnp.stack([mine] + [arrived[step] for step in range(1, patch_count)])
     kv_one = (same, swapped(same))
 
     total = reduced(parts)
     first, *others = all_near(total)
     after_zero = (kept.astype(jnp.float32) + added(first, others)).astype(jnp.bfloat16)
 
-    *parts, _ = attend(1, lists, all_far(after_zero), kv_one, gains, queries, outs)
+    pieces = all_far(after_zero)
+    own_zero = lax.dynamic_index_in_dim(after_zero, near_at, 0, keepdims=False)
+    other_zero = swapped(own_zero)
+    halves_zero = (
+        jnp.where(core == 0, own_zero, other_zero),
+        jnp.where(core == 0, other_zero, own_zero),
+    )
+    *parts, _ = attend(1, lists, pieces, kv_one, gains, queries, outs)
     total = reduced(parts)
-    own_zero = lax.dynamic_index_in_dim(after_zero, near_at, 0, keepdims=False)
-    own_total = lax.dynamic_index_in_dim(total, near_at, 0, keepdims=False)
-    others = [
-        near(lax.dynamic_index_in_dim(total, wrapped(near_at + step), 0, keepdims=False), step)
-        for step in AROUND
+
+    sent = lax.optimization_barrier(
+        tuple(
+            lax.dynamic_index_in_dim(total, wrapped(near_at + step), 0, keepdims=False)
+            for step in range(SIDE)
+        )
+    )
+
+    def to_last(core_from, step):
+        pairs = [pair for pair in square_shift(True, step) if pair[0] // SIDE**2 == core_from]
+        pairs = [(source, target % SIDE**2 + SIDE**2) for source, target in pairs]
+        return lax.ppermute(sent[step], ("pipe", "obs"), pairs)
+
+    own_total = sent[0]
+    on_chip = to_last(0, 0)
+    from_one = [to_last(1, step) for step in AROUND]
+    from_zero = [on_chip] + [to_last(0, step) for step in AROUND]
+    sums = (added(from_zero[0], from_zero[1:]), added(own_total, from_one))
+    result = [
+        jnp.where(
+            core == 0, before, (before.astype(jnp.float32) + extra).astype(jnp.bfloat16)
+        )
+        for before, extra in zip(halves_zero, sums)
     ]
-    own_one = (own_zero.astype(jnp.float32) + added(own_total, others)).astype(jnp.bfloat16)
-
-    arrived = swapped(jnp.where(core == 0, own_one, own_zero))
-    upper = jnp.where(core == 0, own_zero, arrived)
-    lower = jnp.where(core == 0, arrived, own_one)
-    return jnp.concatenate([upper, lower], axis=0)[None]
+    return jnp.concatenate(result, axis=0)[None]
 
 
 def solution(mesh):

time: 157 us -> 183 us (1.17)
  the two profiles are of different devices: /device:TPU:1 before, /device:TPU:2 now
where the time goes in v2:
time: 183 us; the launch traced here: 180 us
  waiting for transfers between devices  96.2 us (53%)
  starting transfers between devices  68.9 us (38%)
  Pallas kernels  10.4 us (6%)
  local copies, waits for them, and re-layouts  2.89 us (2%)
    ppermute x14, waiting for transfers between devices, to_patch(): lax.ppermute(value, 'patch', [(at, (at + step) % patch_count) for at in r...  45.1 us
    ppermute x12, waiting for transfers between devices, far(): return lax.ppermute(value, ('pipe', 'obs'), square_shift(False, step))  32.3 us
    ppermute x14, starting transfers between devices, to_patch(): lax.ppermute(value, 'patch', [(at, (at + step) % patch_count) for at in r...  22.3 us
    ppermute x12, starting transfers between devices, far(): return lax.ppermute(value, ('pipe', 'obs'), square_shift(False, step))  14 us
    ppermute x7, starting transfers between devices, to_last(): return lax.ppermute(sent[step], ('pipe', 'obs'), pairs)  12.1 us
    ppermute x6, starting transfers between devices, near(): return lax.ppermute(value, ('pipe', 'obs'), square_shift(True, step))  10.9 us
    ppermute x6, waiting for transfers between devices, near(): return lax.ppermute(value, ('pipe', 'obs'), square_shift(True, step))  10.1 us
    pallas_call x2, Pallas kernels, attend(): pl.pallas_call(functools.partial(attend_kernel, section), out_shape=[piec...  8.13 us
  transfers between devices with their start and end apart: 48, of which 25 were waited for; matrix products, arithmetic and copies ran while one was open for 1% of the time, Pallas kernels for 1%

profile of v2, /device:TPU:2, one launch (start us, length us, event | category | flops | bytes accessed | tf_op | source)
XLA Modules:
  0.0 180.1 jit_solution(16503245083322973879)
XLA Ops:
  2.2 7.6 %all-to-all-start = ((bf16[16,128,128]{2,1,0:T(8,128)(2,1)}), bf16[16,128,128]{2,1,0:T(8,128)(2,1)S(1)}, u32[]{:S(2)}, u32[]{:S(2)}) async-start(bf16[16,128,128]{2,1,0:T(8,128)(2,1)} %broadcast_in_dim.4), calls=%async_computation | async-start | bytes 1048576 | tf_op jit(solution)/shard_map/all_to_all | solution.py:321
  13.3 6.9 %all-to-all-done.obs = bf16[16,128,128]{2,1,0:T(8,128)(2,1)S(1)} async-done(((bf16[16,128,128]{2,1,0:T(8,128)(2,1)}), bf16[16,128,128]{2,1,0:T(8,128)(2,1)S(1)}, u32[]{:S(2)}, u32[]{:S(2)}) %all-to-all-start) | async-done | bytes 524320 | tf_op jit(solution)/shard_map/all_to_all | solution.py:321
  22.1 5.9 %collective-permute-start.15 = (bf16[128,256]{1,0:T(8,128)(2,1)S(1)}, bf16[128,256]{1,0:T(8,128)(2,1)S(1)}, u32[]{:S(2)}, u32[]{:S(2)}) collective-permute-start(bf16[128,256]{1,0:T(8,128)(2,1)S(1)} %key_values.2), channel_id=1, source_target_pairs={{0,7},{1,0},{2,1},{3,2},{4,3},{5,4},{6,5},{7,6},{8,15},{9,8},{10,9... | collective-permute-start | bytes 196616 | tf_op jit(solution)/shard_map/ppermute | solution.py:336
  28.0 5.5 %collective-permute-done.9 = bf16[128,256]{1,0:T(8,128)(2,1)S(1)} collective-permute-done((bf16[128,256]{1,0:T(8,128)(2,1)S(1)}, bf16[128,256]{1,0:T(8,128)(2,1)S(1)}, u32[]{:S(2)}, u32[]{:S(2)}) %collective-permute-start.9) | collective-permute-done | bytes 65568 | tf_op jit(solution)/shard_map/ppermute | solution.py:336
  33.5 6.4 %collective-permute-done.10 = bf16[128,256]{1,0:T(8,128)(2,1)S(1)} collective-permute-done((bf16[128,256]{1,0:T(8,128)(2,1)S(1)}, bf16[128,256]{1,0:T(8,128)(2,1)S(1)}, u32[]{:S(2)}, u32[]{:S(2)}) %collective-permute-start.10) | collective-permute-done | bytes 65568 | tf_op jit(solution)/shard_map/ppermute | solution.py:336
  39.9 7.3 %collective-permute-done.11 = bf16[128,256]{1,0:T(8,128)(2,1)S(1)} collective-permute-done((bf16[128,256]{1,0:T(8,128)(2,1)S(1)}, bf16[128,256]{1,0:T(8,128)(2,1)S(1)}, u32[]{:S(2)}, u32[]{:S(2)}) %collective-permute-start.11) | collective-permute-done | bytes 65568 | tf_op jit(solution)/shard_map/ppermute | solution.py:336
  49.5 5.8 %collective-permute-done.12 = bf16[128,256]{1,0:T(8,128)(2,1)S(1)} collective-permute-done((bf16[128,256]{1,0:T(8,128)(2,1)S(1)}, bf16[128,256]{1,0:T(8,128)(2,1)S(1)}, u32[]{:S(2)}, u32[]{:S(2)}) %collective-permute-start.12) | collective-permute-done | bytes 65568 | tf_op jit(solution)/shard_map/ppermute | solution.py:336
  55.4 2.5 %collective-permute-start.13 = (bf16[128,256]{1,0:T(8,128)(2,1)S(1)}, bf16[128,256]{1,0:T(8,128)(2,1)S(1)}, u32[]{:S(2)}, u32[]{:S(2)}) collective-permute-start(bf16[128,256]{1,0:T(8,128)(2,1)S(1)} %key_values.2), channel_id=1, source_target_pairs={{0,5},{1,6},{2,7},{3,0},{4,1},{5,2},{6,3},{7,4},{8,13},{9,14},{10,... | collective-permute-start | bytes 196616 | tf_op jit(solution)/shard_map/ppermute | solution.py:336
  57.9 4.2 %collective-permute-done.13 = bf16[128,256]{1,0:T(8,128)(2,1)S(1)} collective-permute-done((bf16[128,256]{1,0:T(8,128)(2,1)S(1)}, bf16[128,256]{1,0:T(8,128)(2,1)S(1)}, u32[]{:S(2)}, u32[]{:S(2)}) %collective-permute-start.13) | collective-permute-done | bytes 65568 | tf_op jit(solution)/shard_map/ppermute | solution.py:336
  63.1 4.3 %collective-permute-done.14 = bf16[128,256]{1,0:T(8,128)(2,1)S(1)} collective-permute-done((bf16[128,256]{1,0:T(8,128)(2,1)S(1)}, bf16[128,256]{1,0:T(8,128)(2,1)S(1)}, u32[]{:S(2)}, u32[]{:S(2)}) %collective-permute-start.14) | collective-permute-done | bytes 65568 | tf_op jit(solution)/shard_map/ppermute | solution.py:336
  67.5 3.2 %collective-permute-start = (bf16[256,128]{1,0:T(8,128)(2,1)S(1)}, bf16[256,128]{1,0:T(8,128)(2,1)S(1)}, u32[]{:S(2)}, u32[]{:S(2)}) collective-permute-start(bf16[256,128]{1,0:T(8,128)(2,1)S(1)} %constant_dynamic-slice_fusion.1), channel_id=1, source_target_pairs={{0,8},{8,16},{16,24},{24,0},{32,40},{40,48},{48,56},{56,32},{64,72... | collective-permute-start | bytes 196616 | tf_op jit(solution)/shard_map/ppermute | solution.py:36
  72.5 2.4 %collective-permute-done.2 = bf16[256,128]{1,0:T(8,128)(2,1)S(1)} collective-permute-done((bf16[256,128]{1,0:T(8,128)(2,1)S(1)}, bf16[256,128]{1,0:T(8,128)(2,1)S(1)}, u32[]{:S(2)}, u32[]{:S(2)}) %collective-permute-start.2) | collective-permute-done | bytes 65568 | tf_op jit(solution)/shard_map/ppermute | solution.py:36
  79.1 2.5 %collective-permute-done.8.x3 = bf16[4,256,128]{2,1,0:T(8,128)(2,1)S(1)} collective-permute-done((bf16[4,256,128]{2,1,0:T(8,128)(2,1)S(1)}, bf16[4,256,128]{2,1,0:T(8,128)(2,1)S(1)}, u32[]{:S(2)}, u32[]{:S(2)}) %collective-permute-start.8) | collective-permute-done | bytes 262176 | tf_op jit(solution)/shard_map/ppermute | solution.py:40
  81.6 2.5 %collective-permute-done.7.x2 = bf16[4,256,128]{2,1,0:T(8,128)(2,1)S(1)} collective-permute-done((bf16[4,256,128]{2,1,0:T(8,128)(2,1)S(1)}, bf16[4,256,128]{2,1,0:T(8,128)(2,1)S(1)}, u32[]{:S(2)}, u32[]{:S(2)}) %collective-permute-start.7) | collective-permute-done | bytes 262176 | tf_op jit(solution)/shard_map/ppermute | solution.py:40
  84.1 2.7 %collective-permute-done.6.x1 = bf16[4,256,128]{2,1,0:T(8,128)(2,1)S(1)} collective-permute-done((bf16[4,256,128]{2,1,0:T(8,128)(2,1)S(1)}, bf16[4,256,128]{2,1,0:T(8,128)(2,1)S(1)}, u32[]{:S(2)}, u32[]{:S(2)}) %collective-permute-start.6) | collective-permute-done | bytes 262176 | tf_op jit(solution)/shard_map/ppermute | solution.py:40
  86.8 3.7 %attend.2 = (bf16[4,256,128]{2,1,0:T(8,128)(2,1)S(1)}, bf16[4,256,128]{2,1,0:T(8,128)(2,1)S(1)}, bf16[4,256,128]{2,1,0:T(8,128)(2,1)S(1)}, bf16[4,256,128]{2,1,0:T(8,128)(2,1)S(1)}, bf16[4,256,128]{2,1,0:T(8,128)(2,1)S(1)}) custom-call(s32[4,8]{1,0:T(4,128)S(1)} %copy-done.6, s32[4]{0:T(128)S(1)} %copy-done.8, f32[4,8]{1,0:T(4,128)S(1)} %copy-done.7, ...), custom_call_target="tpu_custom_call" | custom-call | flops 536870912 | bytes 4194304 | tf_op jit(solution)/shard_map/attend/pallas_call | solution.py:271
  90.6 3.1 %collective-permute-start.33 = (bf16[128,256]{1,0:T(8,128)(2,1)S(1)}, bf16[128,256]{1,0:T(8,128)(2,1)S(1)}, u32[]{:S(2)}, u32[]{:S(2)}) collective-permute-start(bf16[128,256]{1,0:T(8,128)(2,1)S(1)} %key_values.3), channel_id=1, source_target_pairs={{0,5},{1,6},{2,7},{3,0},{4,1},{5,2},{6,3},{7,4},{8,13},{9,14},{10,... | collective-permute-start | bytes 196616 | tf_op jit(solution)/shard_map/ppermute | solution.py:336
  93.7 3.4 %collective-permute-start.32 = (bf16[128,256]{1,0:T(8,128)(2,1)S(1)}, bf16[128,256]{1,0:T(8,128)(2,1)S(1)}, u32[]{:S(2)}, u32[]{:S(2)}) collective-permute-start(bf16[128,256]{1,0:T(8,128)(2,1)S(1)} %key_values.3), channel_id=1, source_target_pairs={{0,4},{1,5},{2,6},{3,7},{4,0},{5,1},{6,2},{7,3},{8,12},{9,13},{10,... | collective-permute-start | bytes 196616 | tf_op jit(solution)/shard_map/ppermute | solution.py:336
  97.1 3.3 %collective-permute-start.31 = (bf16[128,256]{1,0:T(8,128)(2,1)S(1)}, bf16[128,256]{1,0:T(8,128)(2,1)S(1)}, u32[]{:S(2)}, u32[]{:S(2)}) collective-permute-start(bf16[128,256]{1,0:T(8,128)(2,1)S(1)} %key_values.3), channel_id=1, source_target_pairs={{0,3},{1,4},{2,5},{3,6},{4,7},{5,0},{6,1},{7,2},{8,11},{9,12},{10,... | collective-permute-start | bytes 196616 | tf_op jit(solution)/shard_map/ppermute | solution.py:336
  100.4 5.6 %collective-permute-done.29 = bf16[128,256]{1,0:T(8,128)(2,1)S(1)} collective-permute-done((bf16[128,256]{1,0:T(8,128)(2,1)S(1)}, bf16[128,256]{1,0:T(8,128)(2,1)S(1)}, u32[]{:S(2)}, u32[]{:S(2)}) %collective-permute-start.29) | collective-permute-done | bytes 65568 | tf_op jit(solution)/shard_map/ppermute | solution.py:336
  106.4 6.0 %collective-permute-done.30 = bf16[128,256]{1,0:T(8,128)(2,1)S(1)} collective-permute-done((bf16[128,256]{1,0:T(8,128)(2,1)S(1)}, bf16[128,256]{1,0:T(8,128)(2,1)S(1)}, u32[]{:S(2)}, u32[]{:S(2)}) %collective-permute-start.30) | collective-permute-done | bytes 65568 | tf_op jit(solution)/shard_map/ppermute | solution.py:336
  112.5 4.6 %collective-permute-start.20 = (bf16[4,256,128]{2,1,0:T(8,128)(2,1)S(1)}, bf16[4,256,128]{2,1,0:T(8,128)(2,1)S(1)}, u32[]{:S(2)}, u32[]{:S(2)}) collective-permute-start(bf16[4,256,128]{2,1,0:T(8,128)(2,1)S(1)} %get-tuple-element.24), channel_id=1, source_target_pairs={{0,64},{8,72},{16,80},{24,88},{32,96},{40,104},{48,112},{56,120},{... | collective-permute-start | bytes 786440 | tf_op jit(solution)/shard_map/ppermute | solution.py:40
  117.5 2.6 %collective-permute-done.19 = bf16[4,256,128]{2,1,0:T(8,128)(2,1)S(1)} collective-permute-done((bf16[4,256,128]{2,1,0:T(8,128)(2,1)S(1)}, bf16[4,256,128]{2,1,0:T(8,128)(2,1)S(1)}, u32[]{:S(2)}, u32[]{:S(2)}) %collective-permute-start.19) | collective-permute-done | bytes 262176 | tf_op jit(solution)/shard_map/ppermute | solution.py:40
  120.0 4.1 %collective-permute-done.20 = bf16[4,256,128]{2,1,0:T(8,128)(2,1)S(1)} collective-permute-done((bf16[4,256,128]{2,1,0:T(8,128)(2,1)S(1)}, bf16[4,256,128]{2,1,0:T(8,128)(2,1)S(1)}, u32[]{:S(2)}, u32[]{:S(2)}) %collective-permute-start.20) | collective-permute-done | bytes 262176 | tf_op jit(solution)/shard_map/ppermute | solution.py:40
  124.3 2.8 %collective-permute-start.24 = (bf16[4,256,128]{2,1,0:T(8,128)(2,1)S(1)}, bf16[4,256,128]{2,1,0:T(8,128)(2,1)S(1)}, u32[]{:S(2)}, u32[]{:S(2)}) collective-permute-start(bf16[4,256,128]{2,1,0:T(8,128)(2,1)S(1)} %add_convert_fusion.2), channel_id=1, source_target_pairs={{0,24},{8,0},{16,8},{24,16},{32,56},{40,32},{48,40},{56,48},{64,88... | collective-permute-start | bytes 786440 | tf_op jit(solution)/shard_map/ppermute | solution.py:36
  131.0 4.0 %collective-permute-done.23 = bf16[4,256,128]{2,1,0:T(8,128)(2,1)S(1)} collective-permute-done((bf16[4,256,128]{2,1,0:T(8,128)(2,1)S(1)}, bf16[4,256,128]{2,1,0:T(8,128)(2,1)S(1)}, u32[]{:S(2)}, u32[]{:S(2)}) %collective-permute-start.23) | collective-permute-done | bytes 262176 | tf_op jit(solution)/shard_map/ppermute | solution.py:36
  136.0 2.4 %collective-permute-start.28 = (bf16[4,256,128]{2,1,0:T(8,128)(2,1)S(1)}, bf16[4,256,128]{2,1,0:T(8,128)(2,1)S(1)}, u32[]{:S(2)}, u32[]{:S(2)}) collective-permute-start(bf16[4,256,128]{2,1,0:T(8,128)(2,1)S(1)} %add_convert_fusion.1.x0), channel_id=1, source_target_pairs={{0,96},{8,104},{16,112},{24,120},{32,0},{40,8},{48,16},{56,24},{64... | collective-permute-start | bytes 786440 | tf_op jit(solution)/shard_map/ppermute | solution.py:40
  139.4 5.8 %collective-permute-done.28.x3 = bf16[4,256,128]{2,1,0:T(8,128)(2,1)S(1)} collective-permute-done((bf16[4,256,128]{2,1,0:T(8,128)(2,1)S(1)}, bf16[4,256,128]{2,1,0:T(8,128)(2,1)S(1)}, u32[]{:S(2)}, u32[]{:S(2)}) %collective-permute-start.28) | collective-permute-done | bytes 262176 | tf_op jit(solution)/shard_map/ppermute | solution.py:40
  146.4 2.7 %collective-permute-done.26.x1 = bf16[4,256,128]{2,1,0:T(8,128)(2,1)S(1)} collective-permute-done((bf16[4,256,128]{2,1,0:T(8,128)(2,1)S(1)}, bf16[4,256,128]{2,1,0:T(8,128)(2,1)S(1)}, u32[]{:S(2)}, u32[]{:S(2)}) %collective-permute-start.26) | collective-permute-done | bytes 262176 | tf_op jit(solution)/shard_map/ppermute | solution.py:40
  149.1 4.4 %attend.3 = (bf16[4,256,128]{2,1,0:T(8,128)(2,1)S(1)}, bf16[4,256,128]{2,1,0:T(8,128)(2,1)}, bf16[4,256,128]{2,1,0:T(8,128)(2,1)}, bf16[4,256,128]{2,1,0:T(8,128)(2,1)S(1)}, bf16[8,128]{1,0:T(8,128)(2,1)}) custom-call(s32[4,8]{1,0:T(4,128)S(1)} %copy-done.6, s32[4]{0:T(128)S(1)} %copy-done.8, f32[4,8]{1,0:T(4,128)S(1)} %copy-done.7, ...), custom_call_target="tpu_custom_call" | custom-call | flops 536870912 | bytes 4194304 | tf_op jit(solution)/shard_map/attend/pallas_call | solution.py:271
  156.9 7.3 %collective-permute-done.37 = bf16[4,256,128]{2,1,0:T(8,128)(2,1)S(1)} collective-permute-done((bf16[4,256,128]{2,1,0:T(8,128)(2,1)}, bf16[4,256,128]{2,1,0:T(8,128)(2,1)S(1)}, u32[]{:S(2)}, u32[]{:S(2)}) %collective-permute-start.37) | collective-permute-done | bytes 262176 | tf_op jit(solution)/shard_map/ppermute | solution.py:40
  171.8 5.7 %collective-permute-start.43 = (bf16[256,128]{1,0:T(8,128)(2,1)S(1)}, bf16[256,128]{1,0:T(8,128)(2,1)S(1)}, u32[]{:S(2)}, u32[]{:S(2)}) collective-permute-start(bf16[256,128]{1,0:T(8,128)(2,1)S(1)} %get-tuple-element.34), channel_id=1, source_target_pairs={{0,152},{8,128},{16,136},{24,144},{32,184},{40,160},{48,168},{56,1... | collective-permute-start | bytes 196616 | tf_op jit(solution)/shard_map/ppermute | solution.py:384
  (120 shorter events, 38.7 us)
Async XLA Ops:
  0.0 20.2 %collective-permute-start.4 = (bf16[2048,128]{1,0:T(8,128)(2,1)}, bf16[2048,128]{1,0:T(8,128)(2,1)}, u32[]{:S(2)}, u32[]{:S(2)}) collective-permute-start(bf16[2048,128]{1,0:T(8,128)(2,1)} %bitcast.66), channel_id=1, source_target_pairs={{0,128},{128,0},{1,129},{129,1},{2,130},{130,2},{3,131},{131,3},{4... | collective-permute-start | bytes 1572872 | tf_op jit(solution)/shard_map/ppermute | solution.py:54
  0.0 20.2 %collective-permute-start.5 = (bf16[2048,128]{1,0:T(8,128)(2,1)}, bf16[2048,128]{1,0:T(8,128)(2,1)}, u32[]{:S(2)}, u32[]{:S(2)}) collective-permute-start(bf16[2048,128]{1,0:T(8,128)(2,1)} %bitcast.69), channel_id=1, source_target_pairs={{0,128},{128,0},{1,129},{129,1},{2,130},{130,2},{3,131},{131,3},{4... | collective-permute-start | bytes 1572872 | tf_op jit(solution)/shard_map/ppermute | solution.py:54
  2.2 18.0 %all-to-all-start = ((bf16[16,128,128]{2,1,0:T(8,128)(2,1)}), bf16[16,128,128]{2,1,0:T(8,128)(2,1)S(1)}, u32[]{:S(2)}, u32[]{:S(2)}) async-start(bf16[16,128,128]{2,1,0:T(8,128)(2,1)} %broadcast_in_dim.4), calls=%async_computation | async-start | bytes 1048576 | tf_op jit(solution)/shard_map/all_to_all | solution.py:321
  10.0 60.6 %collective-permute-start.1 = (bf16[256,128]{1,0:T(8,128)(2,1)S(1)}, bf16[256,128]{1,0:T(8,128)(2,1)S(1)}, u32[]{:S(2)}, u32[]{:S(2)}) collective-permute-start(bf16[256,128]{1,0:T(8,128)(2,1)S(1)} %constant_dynamic-slice_fusion.1), channel_id=1, source_target_pairs={{0,16},{8,24},{16,0},{24,8},{32,48},{40,56},{48,32},{56,40},{64,80... | collective-permute-start | bytes 196616 | tf_op jit(solution)/shard_map/ppermute | solution.py:36
  12.1 64.1 %collective-permute-start.17 = (bf16[2048,128]{1,0:T(8,128)(2,1)S(1)}, bf16[2048,128]{1,0:T(8,128)(2,1)S(1)}, u32[]{:S(2)}, u32[]{:S(2)}) collective-permute-start(bf16[2048,128]{1,0:T(8,128)(2,1)S(1)} %bitcast.60), channel_id=1, source_target_pairs={{0,128},{128,0},{1,129},{129,1},{2,130},{130,2},{3,131},{131,3},{4... | collective-permute-start | bytes 1572872 | tf_op jit(solution)/shard_map/ppermute | solution.py:54
  13.2 65.9 %collective-permute-start.18 = (bf16[128,2048]{1,0:T(8,128)(2,1)S(1)}, bf16[128,2048]{1,0:T(8,128)(2,1)S(1)}, u32[]{:S(2)}, u32[]{:S(2)}) collective-permute-start(bf16[128,2048]{1,0:T(8,128)(2,1)S(1)} %bitcast.63), channel_id=1, source_target_pairs={{0,128},{128,0},{1,129},{129,1},{2,130},{130,2},{3,131},{131,3},{4... | collective-permute-start | bytes 1572872 | tf_op jit(solution)/shard_map/ppermute | solution.py:54
  22.1 45.3 %collective-permute-start.15 = (bf16[128,256]{1,0:T(8,128)(2,1)S(1)}, bf16[128,256]{1,0:T(8,128)(2,1)S(1)}, u32[]{:S(2)}, u32[]{:S(2)}) collective-permute-start(bf16[128,256]{1,0:T(8,128)(2,1)S(1)} %key_values.2), channel_id=1, source_target_pairs={{0,7},{1,0},{2,1},{3,2},{4,3},{5,4},{6,5},{7,6},{8,15},{9,8},{10,9... | collective-permute-start | bytes 196616 | tf_op jit(solution)/shard_map/ppermute | solution.py:336
  47.2 8.2 %collective-permute-start.12 = (bf16[128,256]{1,0:T(8,128)(2,1)S(1)}, bf16[128,256]{1,0:T(8,128)(2,1)S(1)}, u32[]{:S(2)}, u32[]{:S(2)}) collective-permute-start(bf16[128,256]{1,0:T(8,128)(2,1)S(1)} %key_values.2), channel_id=1, source_target_pairs={{0,4},{1,5},{2,6},{3,7},{4,0},{5,1},{6,2},{7,3},{8,12},{9,13},{10,... | collective-permute-start | bytes 196616 | tf_op jit(solution)/shard_map/ppermute | solution.py:336
  67.4 19.4 %collective-permute-start.16 = (bf16[8,128,256]{2,1,0:T(8,128)(2,1)S(1)}, bf16[8,128,256]{2,1,0:T(8,128)(2,1)S(1)}, u32[]{:S(2)}, u32[]{:S(2)}) collective-permute-start(bf16[8,128,256]{2,1,0:T(8,128)(2,1)S(1)} %bitcast_dynamic-update-slice_fusion.8.kv_same), channel_id=1, source_target_pairs={{0,128},{128,0},{1,129},{129,1},{2,130},{130,2},{3,131},{131,3},{4... | collective-permute-start | bytes 1572872 | tf_op jit(solution)/shard_map/ppermute | solution.py:54
  76.1 8.0 %collective-permute-start.7 = (bf16[4,256,128]{2,1,0:T(8,128)(2,1)S(1)}, bf16[4,256,128]{2,1,0:T(8,128)(2,1)S(1)}, u32[]{:S(2)}, u32[]{:S(2)}) collective-permute-start(bf16[4,256,128]{2,1,0:T(8,128)(2,1)S(1)} %pad_maximum_fusion.x0), channel_id=1, source_target_pairs={{0,64},{8,72},{16,80},{24,88},{32,96},{40,104},{48,112},{56,120},{... | collective-permute-start | bytes 786440 | tf_op jit(solution)/shard_map/ppermute | solution.py:40
  76.2 10.6 %collective-permute-start.6 = (bf16[4,256,128]{2,1,0:T(8,128)(2,1)S(1)}, bf16[4,256,128]{2,1,0:T(8,128)(2,1)S(1)}, u32[]{:S(2)}, u32[]{:S(2)}) collective-permute-start(bf16[4,256,128]{2,1,0:T(8,128)(2,1)S(1)} %pad_maximum_fusion.x0), channel_id=1, source_target_pairs={{0,32},{8,40},{16,48},{24,56},{32,64},{40,72},{48,80},{56,88},{64,... | collective-permute-start | bytes 786440 | tf_op jit(solution)/shard_map/ppermute | solution.py:40
  90.5 39.3 %collective-permute-start.35 = (bf16[128,256]{1,0:T(8,128)(2,1)S(1)}, bf16[128,256]{1,0:T(8,128)(2,1)S(1)}, u32[]{:S(2)}, u32[]{:S(2)}) collective-permute-start(bf16[128,256]{1,0:T(8,128)(2,1)S(1)} %key_values.3), channel_id=1, source_target_pairs={{0,7},{1,0},{2,1},{3,2},{4,3},{5,4},{6,5},{7,6},{8,15},{9,8},{10,9... | collective-permute-start | bytes 196616 | tf_op jit(solution)/shard_map/ppermute | solution.py:336
  90.6 26.6 %collective-permute-start.33 = (bf16[128,256]{1,0:T(8,128)(2,1)S(1)}, bf16[128,256]{1,0:T(8,128)(2,1)S(1)}, u32[]{:S(2)}, u32[]{:S(2)}) collective-permute-start(bf16[128,256]{1,0:T(8,128)(2,1)S(1)} %key_values.3), channel_id=1, source_target_pairs={{0,5},{1,6},{2,7},{3,0},{4,1},{5,2},{6,3},{7,4},{8,13},{9,14},{10,... | collective-permute-start | bytes 196616 | tf_op jit(solution)/shard_map/ppermute | solution.py:336
  93.7 23.4 %collective-permute-start.32 = (bf16[128,256]{1,0:T(8,128)(2,1)S(1)}, bf16[128,256]{1,0:T(8,128)(2,1)S(1)}, u32[]{:S(2)}, u32[]{:S(2)}) collective-permute-start(bf16[128,256]{1,0:T(8,128)(2,1)S(1)} %key_values.3), channel_id=1, source_target_pairs={{0,4},{1,5},{2,6},{3,7},{4,0},{5,1},{6,2},{7,3},{8,12},{9,13},{10,... | collective-permute-start | bytes 196616 | tf_op jit(solution)/shard_map/ppermute | solution.py:336
  97.1 15.4 %collective-permute-start.31 = (bf16[128,256]{1,0:T(8,128)(2,1)S(1)}, bf16[128,256]{1,0:T(8,128)(2,1)S(1)}, u32[]{:S(2)}, u32[]{:S(2)}) collective-permute-start(bf16[128,256]{1,0:T(8,128)(2,1)S(1)} %key_values.3), channel_id=1, source_target_pairs={{0,3},{1,4},{2,5},{3,6},{4,7},{5,0},{6,1},{7,2},{8,11},{9,12},{10,... | collective-permute-start | bytes 196616 | tf_op jit(solution)/shard_map/ppermute | solution.py:336
  112.5 7.6 %collective-permute-start.19 = (bf16[4,256,128]{2,1,0:T(8,128)(2,1)S(1)}, bf16[4,256,128]{2,1,0:T(8,128)(2,1)S(1)}, u32[]{:S(2)}, u32[]{:S(2)}) collective-permute-start(bf16[4,256,128]{2,1,0:T(8,128)(2,1)S(1)} %get-tuple-element.23), channel_id=1, source_target_pairs={{0,32},{8,40},{16,48},{24,56},{32,64},{40,72},{48,80},{56,88},{64,... | collective-permute-start | bytes 786440 | tf_op jit(solution)/shard_map/ppermute | solution.py:40
  112.5 11.7 %collective-permute-start.20 = (bf16[4,256,128]{2,1,0:T(8,128)(2,1)S(1)}, bf16[4,256,128]{2,1,0:T(8,128)(2,1)S(1)}, u32[]{:S(2)}, u32[]{:S(2)}) collective-permute-start(bf16[4,256,128]{2,1,0:T(8,128)(2,1)S(1)} %get-tuple-element.24), channel_id=1, source_target_pairs={{0,64},{8,72},{16,80},{24,88},{32,96},{40,104},{48,112},{56,120},{... | collective-permute-start | bytes 786440 | tf_op jit(solution)/shard_map/ppermute | solution.py:40
  117.2 12.6 %collective-permute-start.34 = (bf16[128,256]{1,0:T(8,128)(2,1)S(1)}, bf16[128,256]{1,0:T(8,128)(2,1)S(1)}, u32[]{:S(2)}, u32[]{:S(2)}) collective-permute-start(bf16[128,256]{1,0:T(8,128)(2,1)S(1)} %key_values.3), channel_id=1, source_target_pairs={{0,6},{1,7},{2,0},{3,1},{4,2},{5,3},{6,4},{7,5},{8,14},{9,15},{10,... | collective-permute-start | bytes 196616 | tf_op jit(solution)/shard_map/ppermute | solution.py:336
  127.1 7.9 %collective-permute-start.23 = (bf16[4,256,128]{2,1,0:T(8,128)(2,1)S(1)}, bf16[4,256,128]{2,1,0:T(8,128)(2,1)S(1)}, u32[]{:S(2)}, u32[]{:S(2)}) collective-permute-start(bf16[4,256,128]{2,1,0:T(8,128)(2,1)S(1)} %add_convert_fusion.2), channel_id=1, source_target_pairs={{0,16},{8,24},{16,0},{24,8},{32,48},{40,56},{48,32},{56,40},{64,80... | collective-permute-start | bytes 786440 | tf_op jit(solution)/shard_map/ppermute | solution.py:36
  127.6 8.2 %collective-permute-start.22 = (bf16[4,256,128]{2,1,0:T(8,128)(2,1)S(1)}, bf16[4,256,128]{2,1,0:T(8,128)(2,1)S(1)}, u32[]{:S(2)}, u32[]{:S(2)}) collective-permute-start(bf16[4,256,128]{2,1,0:T(8,128)(2,1)S(1)} %add_convert_fusion.2), channel_id=1, source_target_pairs={{0,8},{8,16},{16,24},{24,0},{32,40},{40,48},{48,56},{56,32},{64,72... | collective-permute-start | bytes 786440 | tf_op jit(solution)/shard_map/ppermute | solution.py:36
  129.9 9.5 %collective-permute-start.36 = (bf16[8,128,256]{2,1,0:T(8,128)(2,1)S(1)}, bf16[8,128,256]{2,1,0:T(8,128)(2,1)S(1)}, u32[]{:S(2)}, u32[]{:S(2)}) collective-permute-start(bf16[8,128,256]{2,1,0:T(8,128)(2,1)S(1)} %bitcast_dynamic-update-slice_fusion.kv_same), channel_id=1, source_target_pairs={{0,128},{128,0},{1,129},{129,1},{2,130},{130,2},{3,131},{131,3},{4... | collective-permute-start | bytes 1572872 | tf_op jit(solution)/shard_map/ppermute | solution.py:54
  136.0 9.1 %collective-permute-start.28 = (bf16[4,256,128]{2,1,0:T(8,128)(2,1)S(1)}, bf16[4,256,128]{2,1,0:T(8,128)(2,1)S(1)}, u32[]{:S(2)}, u32[]{:S(2)}) collective-permute-start(bf16[4,256,128]{2,1,0:T(8,128)(2,1)S(1)} %add_convert_fusion.1.x0), channel_id=1, source_target_pairs={{0,96},{8,104},{16,112},{24,120},{32,0},{40,8},{48,16},{56,24},{64... | collective-permute-start | bytes 786440 | tf_op jit(solution)/shard_map/ppermute | solution.py:40
  138.4 8.0 %collective-permute-start.27 = (bf16[4,256,128]{2,1,0:T(8,128)(2,1)S(1)}, bf16[4,256,128]{2,1,0:T(8,128)(2,1)S(1)}, u32[]{:S(2)}, u32[]{:S(2)}) collective-permute-start(bf16[4,256,128]{2,1,0:T(8,128)(2,1)S(1)} %add_convert_fusion.1.x0), channel_id=1, source_target_pairs={{0,64},{8,72},{16,80},{24,88},{32,96},{40,104},{48,112},{56,120},{... | collective-permute-start | bytes 786440 | tf_op jit(solution)/shard_map/ppermute | solution.py:40
  139.1 10.0 %collective-permute-start.26 = (bf16[4,256,128]{2,1,0:T(8,128)(2,1)S(1)}, bf16[4,256,128]{2,1,0:T(8,128)(2,1)S(1)}, u32[]{:S(2)}, u32[]{:S(2)}) collective-permute-start(bf16[4,256,128]{2,1,0:T(8,128)(2,1)S(1)} %add_convert_fusion.1.x0), channel_id=1, source_target_pairs={{0,32},{8,40},{16,48},{24,56},{32,64},{40,72},{48,80},{56,88},{64,... | collective-permute-start | bytes 786440 | tf_op jit(solution)/shard_map/ppermute | solution.py:40
  153.5 10.7 %collective-permute-start.37 = (bf16[4,256,128]{2,1,0:T(8,128)(2,1)}, bf16[4,256,128]{2,1,0:T(8,128)(2,1)S(1)}, u32[]{:S(2)}, u32[]{:S(2)}) collective-permute-start(bf16[4,256,128]{2,1,0:T(8,128)(2,1)} %get-tuple-element.28), channel_id=1, source_target_pairs={{0,32},{8,40},{16,48},{24,56},{32,64},{40,72},{48,80},{56,88},{64,... | collective-permute-start | bytes 786440 | tf_op jit(solution)/shard_map/ppermute | solution.py:40
  153.6 10.6 %collective-permute-start.38 = (bf16[4,256,128]{2,1,0:T(8,128)(2,1)}, bf16[4,256,128]{2,1,0:T(8,128)(2,1)S(1)}, u32[]{:S(2)}, u32[]{:S(2)}) collective-permute-start(bf16[4,256,128]{2,1,0:T(8,128)(2,1)} %get-tuple-element.29), channel_id=1, source_target_pairs={{0,64},{8,72},{16,80},{24,88},{32,96},{40,104},{48,112},{56,120},{... | collective-permute-start | bytes 786440 | tf_op jit(solution)/shard_map/ppermute | solution.py:40
  155.7 9.4 %collective-permute-start.39 = (bf16[4,256,128]{2,1,0:T(8,128)(2,1)S(1)}, bf16[4,256,128]{2,1,0:T(8,128)(2,1)S(1)}, u32[]{:S(2)}, u32[]{:S(2)}) collective-permute-start(bf16[4,256,128]{2,1,0:T(8,128)(2,1)S(1)} %get-tuple-element.30), channel_id=1, source_target_pairs={{0,96},{8,104},{16,112},{24,120},{32,0},{40,8},{48,16},{56,24},{64... | collective-permute-start | bytes 786440 | tf_op jit(solution)/shard_map/ppermute | solution.py:40
  156.9 12.8 %collective-permute-start.25 = (bf16[256,128]{1,0:T(8,128)(2,1)S(1)}, bf16[256,128]{1,0:T(8,128)(2,1)S(1)}, u32[]{:S(2)}, u32[]{:S(2)}) collective-permute-start(bf16[256,128]{1,0:T(8,128)(2,1)S(1)} %dynamic-slice_bitcast_fusion.4), channel_id=1, source_target_pairs={{0,128},{128,0},{1,129},{129,1},{2,130},{130,2},{3,131},{131,3},{4... | collective-permute-start | bytes 196616 | tf_op jit(solution)/shard_map/ppermute | solution.py:54
  167.3 10.2 %collective-permute-start.41 = (bf16[256,128]{1,0:T(8,128)(2,1)S(1)}, bf16[256,128]{1,0:T(8,128)(2,1)S(1)}, u32[]{:S(2)}, u32[]{:S(2)}) collective-permute-start(bf16[256,128]{1,0:T(8,128)(2,1)S(1)} %get-tuple-element.32), channel_id=1, source_target_pairs={{0,144},{8,152},{16,128},{24,136},{32,176},{40,184},{48,160},{56,1... | collective-permute-start | bytes 196616 | tf_op jit(solution)/shard_map/ppermute | solution.py:384
  169.1 8.4 %collective-permute-start.45 = (bf16[256,128]{1,0:T(8,128)(2,1)S(1)}, bf16[256,128]{1,0:T(8,128)(2,1)S(1)}, u32[]{:S(2)}, u32[]{:S(2)}) collective-permute-start(bf16[256,128]{1,0:T(8,128)(2,1)S(1)} %get-tuple-element.33), channel_id=1, source_target_pairs={{128,160},{136,168},{144,176},{152,184},{160,192},{168,200},{176,2... | collective-permute-start | bytes 196616 | tf_op jit(solution)/shard_map/ppermute | solution.py:384
  169.8 7.7 %collective-permute-start.42 = (bf16[256,128]{1,0:T(8,128)(2,1)S(1)}, bf16[256,128]{1,0:T(8,128)(2,1)S(1)}, u32[]{:S(2)}, u32[]{:S(2)}) collective-permute-start(bf16[256,128]{1,0:T(8,128)(2,1)S(1)} %get-tuple-element.33), channel_id=1, source_target_pairs={{0,136},{8,144},{16,152},{24,128},{32,168},{40,176},{48,184},{56,1... | collective-permute-start | bytes 196616 | tf_op jit(solution)/shard_map/ppermute | solution.py:384
  171.8 7.6 %collective-permute-start.43 = (bf16[256,128]{1,0:T(8,128)(2,1)S(1)}, bf16[256,128]{1,0:T(8,128)(2,1)S(1)}, u32[]{:S(2)}, u32[]{:S(2)}) collective-permute-start(bf16[256,128]{1,0:T(8,128)(2,1)S(1)} %get-tuple-element.34), channel_id=1, source_target_pairs={{0,152},{8,128},{16,136},{24,144},{32,184},{40,160},{48,168},{56,1... | collective-permute-start | bytes 196616 | tf_op jit(solution)/shard_map/ppermute | solution.py:384
  (27 other events, 217.0 us)

commit v3 on v0

--- a/solution.py
+++ b/solution.py
@@ -92,20 +92,33 @@
     copy.wait()
 
 
-def normed_into(where, is_relative, pieces, gain, normed):
+def placed(where, is_relative):
     _, near_at, far_at, near_stride, far_stride = where
+
+    def block(step, part):
+        at = wrapped(near_at - part) if is_relative else part
+        return wrapped(far_at - step) * far_stride + at * near_stride
+
+    return block
+
+
+def normed_into(block_of, pieces, gain, normed):
     rows = normed.shape[0]
-    squares = jnp.zeros((rows, HS), jnp.float32)
-    for piece in pieces:
-        for part in range(SIDE):
+
+    def add_squares(part, squares):
+        for piece in pieces:
             widened = piece[part].astype(jnp.float32)
             squares = squares + widened * widened
+        return squares
+
+    squares = lax.fori_loop(0, SIDE, add_squares, jnp.zeros((rows, HS), jnp.float32))
     mean = jnp.sum(squares, axis=-1, keepdims=True) * (1.0 / (SIDE * SIDE * HS))
     inverse = lax.rsqrt(mean + EPS)
-    for step, piece in enumerate(pieces):
-        for part in range(SIDE):
-            at = wrapped(near_at - part) if is_relative else part
-            block = wrapped(far_at - step) * far_stride + at * near_stride
+
+    @pl.loop(0, SIDE)
+    def _(part):
+        for step, piece in enumerate(pieces):
+            block = block_of(step, part)
             scaled = (piece[part].astype(jnp.float32) * inverse) * gain[pl.ds(block, 1), :]
             normed[:, tile_cols(block)] = scaled.astype(jnp.bfloat16)
 
@@ -138,7 +151,7 @@
     fetch(core, section, key_mine, key_theirs, key_at, sems.at[0], start)
     fetch(core, section, value_mine, value_theirs, value_at, sems.at[1], start)
     chosen_gain(core, section, gain_mine, gain_theirs, 1, gain)
-    normed_into(where, True, (o0, o1, o2, o3), gain, normed)
+    normed_into(placed(where, True), (o0, o1, o2, o3), gain, normed)
     fetch(core, section, key_mine, key_theirs, key_at, sems.at[0], wait)
     fetch(core, section, value_mine, value_theirs, value_at, sems.at[1], wait)
     out[...] = jnp.dot(
@@ -184,26 +197,30 @@
     fetch(core, section, query_mine, query_theirs, w_query, sems.at[0], start)
     fetch(core, section, out_mine, out_theirs, w_out, sems.at[1], start)
     chosen_gain(core, section, gain_mine, gain_theirs, 0, gain)
-    normed_into(where, section == 0, (x0, x1, x2, x3), gain, normed)
+    normed_into(placed(where, section == 0), (x0, x1, x2, x3), gain, normed)
     if section == 0:
-        for part in range(SIDE):
+
+        @pl.loop(0, SIDE)
+        def _(part):
             kept[part] = x0[wrapped(near_at - part)]
+
     fetch(core, section, query_mine, query_theirs, w_query, sems.at[0], wait)
-    queries = (
+    context[...] = (
         jnp.dot(normed[...], w_query[...], preferred_element_type=jnp.float32) * HS ** (-0.5)
     ).astype(jnp.bfloat16)
     blocks_here = rows // BLK
-    for block in range(blocks_here):
-        query = queries[block * BLK : (block + 1) * BLK]
+
+    @pl.loop(0, blocks_here)
+    def _(block):
+        here = pl.ds(pl.multiple_of(block * BLK, BLK), BLK)
+        query = context[here, :]
         row = core * blocks_here + block
         live = counts[row]
         scores, values = [], []
         for slot in range(slots):
             entry = jnp.where(slot < live, entries[row, slot], 0)
             owner = lax.div(entry, 2)
-            index = owner
-            if section == 0:
-                index = lax.rem(place - owner + patch_count, patch_count)
+            index = lax.rem(place - owner + patch_count, patch_count)
             is_same = (entry - owner * 2) == core
             both = jnp.where(is_same, kv_same[index], kv_other[index])
             score = lax.dot_general(
@@ -217,19 +234,25 @@
         scores = jnp.concatenate(scores, axis=1)
         top = jnp.max(scores, axis=-1, keepdims=True)
         weights = jnp.exp(scores - top)
-        weights = (weights / jnp.sum(weights, axis=-1, keepdims=True)).astype(jnp.bfloat16)
-        context[block * BLK : (block + 1) * BLK, :] = jnp.dot(
+        weights = (weights * (1.0 / jnp.sum(weights, axis=-1, keepdims=True))).astype(jnp.bfloat16)
+        context[here, :] = jnp.dot(
             weights, jnp.concatenate(values, axis=0), preferred_element_type=jnp.float32
         ).astype(jnp.bfloat16)
+
     fetch(core, section, out_mine, out_theirs, w_out, sems.at[1], wait)
     ready = context[...]
     width = SIDE * HS
-    for part in range(SIDE):
-        normed[:, part * width : (part + 1) * width] = jnp.dot(
-            ready, w_out[:, part * width : (part + 1) * width], preferred_element_type=jnp.float32
+
+    @pl.loop(0, SIDE)
+    def _(part):
+        cols = pl.ds(pl.multiple_of(part * width, width), width)
+        normed[:, cols] = jnp.dot(
+            ready, w_out[:, cols], preferred_element_type=jnp.float32
         ).astype(jnp.bfloat16)
-    for step, out in enumerate((y0, y1, y2, y3)):
-        for part in range(SIDE):
+
+    @pl.loop(0, SIDE)
+    def _(part):
+        for step, out in enumerate((y0, y1, y2, y3)):
             block = wrapped(far_at + step) * far_stride + part * near_stride
             out[part] = normed[:, tile_cols(block)]
 
@@ -322,11 +345,16 @@
 
     obs_pieces = all_far(obs_group)
     mine = key_values(0, obs_pieces, gains, keys, values)
-    steps = sorted(range(1, patch_count), key=lambda step: -min(step, patch_count - step))
-    arrived = {}
-    for step in steps:
-        pairs = [(at, (at + step) % patch_count) for at in range(patch_count)]
-        arrived[step] = lax.ppermute(mine, "patch", pairs)
+
+    def to_patch(value, steps):
+        return {
+            step: lax.ppermute(
+                value, "patch", [(at, (at + step) % patch_count) for at in range(patch_count)]
+            )
+            for step in steps
+        }
+
+    arrived = to_patch(mine, (4, 3, 5)) | to_patch(mine, (2, 6, 1, 7))
     same = jnp.stack([mine] + [arrived[step] for step in range(1, patch_count)])
     kv_zero = (same, swapped(same))
     patch_group, mine = lax.optimization_barrier((patch_group, mine))
@@ -339,14 +367,17 @@
 
     *parts, kept = attend(0, lists, patch_pieces, kv_zero, gains, queries, outs)
     mine, _ = lax.optimization_barrier((mine, kept))
-    same = lax.all_to_all(jnp.broadcast_to(mine[None], (patch_count, *mine.shape)), "patch", 0, 0)
+    arrived = to_patch(mine, (4, 1)) | to_patch(mine, (3, 5))
+    arrived |= to_patch(mine, (2, 6, 7))
+    same = jnp.stack([mine] + [arrived[step] for step in range(1, patch_count)])
     kv_one = (same, swapped(same))
 
     total = reduced(parts)
     first, *others = all_near(total)
     after_zero = (kept.astype(jnp.float32) + added(first, others)).astype(jnp.bfloat16)
 
-    *parts, _ = attend(1, lists, all_far(after_zero), kv_one, gains, queries, outs)
+    pieces = all_far(after_zero)
+    *parts, _ = attend(1, lists, pieces, kv_one, gains, queries, outs)
     total = reduced(parts)
     own_zero = lax.dynamic_index_in_dim(after_zero, near_at, 0, keepdims=False)
     own_total = lax.dynamic_index_in_dim(total, near_at, 0, keepdims=False)

time: 157 us -> 173 us (1.10)
  the two profiles are of different devices: /device:TPU:1 before, /device:TPU:2 now
where the time goes in v3:
time: 173 us; the launch traced here: 170 us
  waiting for transfers between devices  100 us (58%)
  starting transfers between devices  52.5 us (30%)
  Pallas kernels  11.7 us (7%)
  local copies, waits for them, and re-layouts  3.11 us (2%)
  other arithmetic  2.01 us (1%)
    ppermute x14, waiting for transfers between devices, to_patch(): lax.ppermute(value, 'patch', [(at, (at + step) % patch_count) for at in r...  48.3 us
    ppermute x15, waiting for transfers between devices, far(): return lax.ppermute(value, ('pipe', 'obs'), square_shift(False, step))  39 us
    ppermute x14, starting transfers between devices, to_patch(): lax.ppermute(value, 'patch', [(at, (at + step) % patch_count) for at in r...  18.4 us
    ppermute x15, starting transfers between devices, far(): return lax.ppermute(value, ('pipe', 'obs'), square_shift(False, step))  18.2 us
    ppermute x9, starting transfers between devices, near(): return lax.ppermute(value, ('pipe', 'obs'), square_shift(True, step))  14.7 us
    ppermute x9, waiting for transfers between devices, near(): return lax.ppermute(value, ('pipe', 'obs'), square_shift(True, step))  11.6 us
    pallas_call x2, Pallas kernels, attend(): pl.pallas_call(functools.partial(attend_kernel, section), out_shape=[piec...  9.79 us
  transfers between devices with their start and end apart: 46, of which 30 were waited for; matrix products, arithmetic and copies ran while one was open for 1% of the time, Pallas kernels for 1%

profile of v3, /device:TPU:2, one launch (start us, length us, event | category | flops | bytes accessed | tf_op | source)
XLA Modules:
  0.0 169.8 jit_solution(14234592723064889506)
XLA Ops:
  1.4 2.2 %collective-permute-start.1 = (bf16[384,128]{1,0:T(8,128)(2,1)S(1)}, bf16[384,128]{1,0:T(8,128)(2,1)S(1)}, u32[]{:S(2)}, u32[]{:S(2)}) collective-permute-start(bf16[384,128]{1,0:T(8,128)(2,1)S(1)} %get-tuple-element.33), channel_id=1, source_target_pairs={{0,16},{8,24},{16,0},{24,8},{32,48},{40,56},{48,32},{56,40},{64,80... | collective-permute-start | bytes 294920 | tf_op jit(solution)/shard_map/ppermute | solution.py:36
  9.8 2.0 %collective-permute-start.5 = (bf16[4,128,128]{2,1,0:T(8,128)(2,1)S(1)}, bf16[4,128,128]{2,1,0:T(8,128)(2,1)S(1)}, u32[]{:S(2)}, u32[]{:S(2)}) collective-permute-start(bf16[4,128,128]{2,1,0:T(8,128)(2,1)S(1)} %pad_maximum_fusion.1.o0), channel_id=1, source_target_pairs={{0,96},{8,104},{16,112},{24,120},{32,0},{40,8},{48,16},{56,24},{64... | collective-permute-start | bytes 393224 | tf_op jit(solution)/shard_map/ppermute | solution.py:40
  13.4 2.3 %collective-permute-done.5.o3 = bf16[4,128,128]{2,1,0:T(8,128)(2,1)S(1)} collective-permute-done((bf16[4,128,128]{2,1,0:T(8,128)(2,1)S(1)}, bf16[4,128,128]{2,1,0:T(8,128)(2,1)S(1)}, u32[]{:S(2)}, u32[]{:S(2)}) %collective-permute-start.5) | collective-permute-done | bytes 131104 | tf_op jit(solution)/shard_map/ppermute | solution.py:40
  15.8 2.6 %collective-permute-done.4.o2 = bf16[4,128,128]{2,1,0:T(8,128)(2,1)S(1)} collective-permute-done((bf16[4,128,128]{2,1,0:T(8,128)(2,1)S(1)}, bf16[4,128,128]{2,1,0:T(8,128)(2,1)S(1)}, u32[]{:S(2)}, u32[]{:S(2)}) %collective-permute-start.4) | collective-permute-done | bytes 131104 | tf_op jit(solution)/shard_map/ppermute | solution.py:40
  22.8 5.9 %collective-permute-start.18 = (bf16[128,256]{1,0:T(8,128)(2,1)S(1)}, bf16[128,256]{1,0:T(8,128)(2,1)S(1)}, u32[]{:S(2)}, u32[]{:S(2)}) collective-permute-start(bf16[128,256]{1,0:T(8,128)(2,1)S(1)} %key_values.2), channel_id=1, source_target_pairs={{0,7},{1,0},{2,1},{3,2},{4,3},{5,4},{6,5},{7,6},{8,15},{9,8},{10,9... | collective-permute-start | bytes 196616 | tf_op jit(solution)/shard_map/ppermute | solution.py:351
  31.2 4.4 %collective-permute-done.12 = bf16[128,256]{1,0:T(8,128)(2,1)S(1)} collective-permute-done((bf16[128,256]{1,0:T(8,128)(2,1)S(1)}, bf16[128,256]{1,0:T(8,128)(2,1)S(1)}, u32[]{:S(2)}, u32[]{:S(2)}) %collective-permute-start.12) | collective-permute-done | bytes 65568 | tf_op jit(solution)/shard_map/ppermute | solution.py:351
  35.9 7.1 %collective-permute-done.13 = bf16[128,256]{1,0:T(8,128)(2,1)S(1)} collective-permute-done((bf16[128,256]{1,0:T(8,128)(2,1)S(1)}, bf16[128,256]{1,0:T(8,128)(2,1)S(1)}, u32[]{:S(2)}, u32[]{:S(2)}) %collective-permute-start.13) | collective-permute-done | bytes 65568 | tf_op jit(solution)/shard_map/ppermute | solution.py:351
  43.0 7.5 %collective-permute-done.14 = bf16[128,256]{1,0:T(8,128)(2,1)S(1)} collective-permute-done((bf16[128,256]{1,0:T(8,128)(2,1)S(1)}, bf16[128,256]{1,0:T(8,128)(2,1)S(1)}, u32[]{:S(2)}, u32[]{:S(2)}) %collective-permute-start.14) | collective-permute-done | bytes 65568 | tf_op jit(solution)/shard_map/ppermute | solution.py:351
  50.6 8.6 %collective-permute-done.15 = bf16[128,256]{1,0:T(8,128)(2,1)S(1)} collective-permute-done((bf16[128,256]{1,0:T(8,128)(2,1)S(1)}, bf16[128,256]{1,0:T(8,128)(2,1)S(1)}, u32[]{:S(2)}, u32[]{:S(2)}) %collective-permute-start.15) | collective-permute-done | bytes 65568 | tf_op jit(solution)/shard_map/ppermute | solution.py:351
  59.2 6.1 %collective-permute-done.16 = bf16[128,256]{1,0:T(8,128)(2,1)S(1)} collective-permute-done((bf16[128,256]{1,0:T(8,128)(2,1)S(1)}, bf16[128,256]{1,0:T(8,128)(2,1)S(1)}, u32[]{:S(2)}, u32[]{:S(2)}) %collective-permute-start.16) | collective-permute-done | bytes 65568 | tf_op jit(solution)/shard_map/ppermute | solution.py:351
  68.8 3.2 %collective-permute-done.11.x3 = bf16[4,256,128]{2,1,0:T(8,128)(2,1)S(1)} collective-permute-done((bf16[4,256,128]{2,1,0:T(8,128)(2,1)S(1)}, bf16[4,256,128]{2,1,0:T(8,128)(2,1)S(1)}, u32[]{:S(2)}, u32[]{:S(2)}) %collective-permute-start.11) | collective-permute-done | bytes 262176 | tf_op jit(solution)/shard_map/ppermute | solution.py:40
  72.0 1.9 %collective-permute-done.10.x2 = bf16[4,256,128]{2,1,0:T(8,128)(2,1)S(1)} collective-permute-done((bf16[4,256,128]{2,1,0:T(8,128)(2,1)S(1)}, bf16[4,256,128]{2,1,0:T(8,128)(2,1)S(1)}, u32[]{:S(2)}, u32[]{:S(2)}) %collective-permute-start.10) | collective-permute-done | bytes 262176 | tf_op jit(solution)/shard_map/ppermute | solution.py:40
  73.9 2.7 %collective-permute-done.9.x1 = bf16[4,256,128]{2,1,0:T(8,128)(2,1)S(1)} collective-permute-done((bf16[4,256,128]{2,1,0:T(8,128)(2,1)S(1)}, bf16[4,256,128]{2,1,0:T(8,128)(2,1)S(1)}, u32[]{:S(2)}, u32[]{:S(2)}) %collective-permute-start.9) | collective-permute-done | bytes 262176 | tf_op jit(solution)/shard_map/ppermute | solution.py:40
  76.7 4.6 %attend.2 = (bf16[4,256,128]{2,1,0:T(8,128)(2,1)S(1)}, bf16[4,256,128]{2,1,0:T(8,128)(2,1)S(1)}, bf16[4,256,128]{2,1,0:T(8,128)(2,1)S(1)}, bf16[4,256,128]{2,1,0:T(8,128)(2,1)S(1)}, bf16[4,256,128]{2,1,0:T(8,128)(2,1)S(1)}) custom-call(s32[4,8]{1,0:T(4,128)S(1)} %copy-done.7, s32[4]{0:T(128)S(1)} %copy-done.9, f32[4,8]{1,0:T(4,128)S(1)} %copy-done.8, ...), custom_call_target="tpu_custom_call" | custom-call | flops 536870912 | bytes 4194304 | tf_op jit(solution)/shard_map/attend/pallas_call | solution.py:287
  82.5 5.4 %collective-permute-start.34 = (bf16[128,256]{1,0:T(8,128)(2,1)S(1)}, bf16[128,256]{1,0:T(8,128)(2,1)S(1)}, u32[]{:S(2)}, u32[]{:S(2)}) collective-permute-start(bf16[128,256]{1,0:T(8,128)(2,1)S(1)} %key_values.3), channel_id=1, source_target_pairs={{0,4},{1,5},{2,6},{3,7},{4,0},{5,1},{6,2},{7,3},{8,12},{9,13},{10,... | collective-permute-start | bytes 196616 | tf_op jit(solution)/shard_map/ppermute | solution.py:351
  89.0 9.2 %collective-permute-done.31 = bf16[128,256]{1,0:T(8,128)(2,1)S(1)} collective-permute-done((bf16[128,256]{1,0:T(8,128)(2,1)S(1)}, bf16[128,256]{1,0:T(8,128)(2,1)S(1)}, u32[]{:S(2)}, u32[]{:S(2)}) %collective-permute-start.31) | collective-permute-done | bytes 65568 | tf_op jit(solution)/shard_map/ppermute | solution.py:351
  98.2 1.7 %collective-permute-start.32 = (bf16[128,256]{1,0:T(8,128)(2,1)S(1)}, bf16[128,256]{1,0:T(8,128)(2,1)S(1)}, u32[]{:S(2)}, u32[]{:S(2)}) collective-permute-start(bf16[128,256]{1,0:T(8,128)(2,1)S(1)} %key_values.3), channel_id=1, source_target_pairs={{0,2},{1,3},{2,4},{3,5},{4,6},{5,7},{6,0},{7,1},{8,10},{9,11},{10,... | collective-permute-start | bytes 196616 | tf_op jit(solution)/shard_map/ppermute | solution.py:351
  100.0 5.3 %collective-permute-done.32 = bf16[128,256]{1,0:T(8,128)(2,1)S(1)} collective-permute-done((bf16[128,256]{1,0:T(8,128)(2,1)S(1)}, bf16[128,256]{1,0:T(8,128)(2,1)S(1)}, u32[]{:S(2)}, u32[]{:S(2)}) %collective-permute-start.32) | collective-permute-done | bytes 65568 | tf_op jit(solution)/shard_map/ppermute | solution.py:351
  106.7 2.7 %collective-permute-start.24 = (bf16[4,256,128]{2,1,0:T(8,128)(2,1)S(1)}, bf16[4,256,128]{2,1,0:T(8,128)(2,1)S(1)}, u32[]{:S(2)}, u32[]{:S(2)}) collective-permute-start(bf16[4,256,128]{2,1,0:T(8,128)(2,1)S(1)} %get-tuple-element.21), channel_id=1, source_target_pairs={{0,96},{8,104},{16,112},{24,120},{32,0},{40,8},{48,16},{56,24},{64... | collective-permute-start | bytes 786440 | tf_op jit(solution)/shard_map/ppermute | solution.py:40
  109.7 6.0 %collective-permute-done.22 = bf16[4,256,128]{2,1,0:T(8,128)(2,1)S(1)} collective-permute-done((bf16[4,256,128]{2,1,0:T(8,128)(2,1)S(1)}, bf16[4,256,128]{2,1,0:T(8,128)(2,1)S(1)}, u32[]{:S(2)}, u32[]{:S(2)}) %collective-permute-start.22) | collective-permute-done | bytes 262176 | tf_op jit(solution)/shard_map/ppermute | solution.py:40
  116.8 2.9 %collective-permute-start.27 = (bf16[4,256,128]{2,1,0:T(8,128)(2,1)S(1)}, bf16[4,256,128]{2,1,0:T(8,128)(2,1)S(1)}, u32[]{:S(2)}, u32[]{:S(2)}) collective-permute-start(bf16[4,256,128]{2,1,0:T(8,128)(2,1)S(1)} %add_convert_fusion.2), channel_id=1, source_target_pairs={{0,24},{8,0},{16,8},{24,16},{32,56},{40,32},{48,40},{56,48},{64,88... | collective-permute-start | bytes 786440 | tf_op jit(solution)/shard_map/ppermute | solution.py:36
  119.9 2.5 %collective-permute-start.25 = (bf16[4,256,128]{2,1,0:T(8,128)(2,1)S(1)}, bf16[4,256,128]{2,1,0:T(8,128)(2,1)S(1)}, u32[]{:S(2)}, u32[]{:S(2)}) collective-permute-start(bf16[4,256,128]{2,1,0:T(8,128)(2,1)S(1)} %add_convert_fusion.2), channel_id=1, source_target_pairs={{0,8},{8,16},{16,24},{24,0},{32,40},{40,48},{48,56},{56,32},{64,72... | collective-permute-start | bytes 786440 | tf_op jit(solution)/shard_map/ppermute | solution.py:36
  123.6 4.0 %collective-permute-done.26 = bf16[4,256,128]{2,1,0:T(8,128)(2,1)S(1)} collective-permute-done((bf16[4,256,128]{2,1,0:T(8,128)(2,1)S(1)}, bf16[4,256,128]{2,1,0:T(8,128)(2,1)S(1)}, u32[]{:S(2)}, u32[]{:S(2)}) %collective-permute-start.26) | collective-permute-done | bytes 262176 | tf_op jit(solution)/shard_map/ppermute | solution.py:36
  128.4 2.7 %collective-permute-start.30 = (bf16[4,256,128]{2,1,0:T(8,128)(2,1)S(1)}, bf16[4,256,128]{2,1,0:T(8,128)(2,1)S(1)}, u32[]{:S(2)}, u32[]{:S(2)}) collective-permute-start(bf16[4,256,128]{2,1,0:T(8,128)(2,1)S(1)} %add_convert_fusion.1.x0), channel_id=1, source_target_pairs={{0,96},{8,104},{16,112},{24,120},{32,0},{40,8},{48,16},{56,24},{64... | collective-permute-start | bytes 786440 | tf_op jit(solution)/shard_map/ppermute | solution.py:40
  132.5 5.3 %collective-permute-done.30.x3 = bf16[4,256,128]{2,1,0:T(8,128)(2,1)S(1)} collective-permute-done((bf16[4,256,128]{2,1,0:T(8,128)(2,1)S(1)}, bf16[4,256,128]{2,1,0:T(8,128)(2,1)S(1)}, u32[]{:S(2)}, u32[]{:S(2)}) %collective-permute-start.30) | collective-permute-done | bytes 262176 | tf_op jit(solution)/shard_map/ppermute | solution.py:40
  139.0 2.7 %collective-permute-done.28.x1 = bf16[4,256,128]{2,1,0:T(8,128)(2,1)S(1)} collective-permute-done((bf16[4,256,128]{2,1,0:T(8,128)(2,1)S(1)}, bf16[4,256,128]{2,1,0:T(8,128)(2,1)S(1)}, u32[]{:S(2)}, u32[]{:S(2)}) %collective-permute-start.28) | collective-permute-done | bytes 262176 | tf_op jit(solution)/shard_map/ppermute | solution.py:40
  141.7 5.1 %attend.3 = (bf16[4,256,128]{2,1,0:T(8,128)(2,1)S(1)}, bf16[4,256,128]{2,1,0:T(8,128)(2,1)S(1)}, bf16[4,256,128]{2,1,0:T(8,128)(2,1)S(1)}, bf16[4,256,128]{2,1,0:T(8,128)(2,1)S(1)}, bf16[8,128]{1,0:T(8,128)(2,1)}) custom-call(s32[4,8]{1,0:T(4,128)S(1)} %copy-done.7, s32[4]{0:T(128)S(1)} %copy-done.9, f32[4,8]{1,0:T(4,128)S(1)} %copy-done.8, ...), custom_call_target="tpu_custom_call" | custom-call | flops 536870912 | bytes 4194304 | tf_op jit(solution)/shard_map/attend/pallas_call | solution.py:287
  147.0 2.0 %collective-permute-start.40 = (bf16[4,256,128]{2,1,0:T(8,128)(2,1)S(1)}, bf16[4,256,128]{2,1,0:T(8,128)(2,1)S(1)}, u32[]{:S(2)}, u32[]{:S(2)}) collective-permute-start(bf16[4,256,128]{2,1,0:T(8,128)(2,1)S(1)} %get-tuple-element.25), channel_id=1, source_target_pairs={{0,64},{8,72},{16,80},{24,88},{32,96},{40,104},{48,112},{56,120},{... | collective-permute-start | bytes 786440 | tf_op jit(solution)/shard_map/ppermute | solution.py:40
  149.0 2.0 %collective-permute-start.41 = (bf16[4,256,128]{2,1,0:T(8,128)(2,1)S(1)}, bf16[4,256,128]{2,1,0:T(8,128)(2,1)S(1)}, u32[]{:S(2)}, u32[]{:S(2)}) collective-permute-start(bf16[4,256,128]{2,1,0:T(8,128)(2,1)S(1)} %get-tuple-element.26), channel_id=1, source_target_pairs={{0,96},{8,104},{16,112},{24,120},{32,0},{40,8},{48,16},{56,24},{64... | collective-permute-start | bytes 786440 | tf_op jit(solution)/shard_map/ppermute | solution.py:40
  151.0 6.4 %collective-permute-done.39 = bf16[4,256,128]{2,1,0:T(8,128)(2,1)S(1)} collective-permute-done((bf16[4,256,128]{2,1,0:T(8,128)(2,1)S(1)}, bf16[4,256,128]{2,1,0:T(8,128)(2,1)S(1)}, u32[]{:S(2)}, u32[]{:S(2)}) %collective-permute-start.39) | collective-permute-done | bytes 262176 | tf_op jit(solution)/shard_map/ppermute | solution.py:40
  157.4 2.3 %collective-permute-done.41 = bf16[4,256,128]{2,1,0:T(8,128)(2,1)S(1)} collective-permute-done((bf16[4,256,128]{2,1,0:T(8,128)(2,1)S(1)}, bf16[4,256,128]{2,1,0:T(8,128)(2,1)S(1)}, u32[]{:S(2)}, u32[]{:S(2)}) %collective-permute-start.41) | collective-permute-done | bytes 262176 | tf_op jit(solution)/shard_map/ppermute | solution.py:40
  159.9 2.8 %collective-permute-start.42 = (bf16[256,128]{1,0:T(8,128)(2,1)S(1)}, bf16[256,128]{1,0:T(8,128)(2,1)S(1)}, u32[]{:S(2)}, u32[]{:S(2)}) collective-permute-start(bf16[256,128]{1,0:T(8,128)(2,1)S(1)} %get-tuple-element.29), channel_id=1, source_target_pairs={{0,16},{8,24},{16,0},{24,8},{32,48},{40,56},{48,32},{56,40},{64,80... | collective-permute-start | bytes 196616 | tf_op jit(solution)/shard_map/ppermute | solution.py:36
  (117 shorter events, 37.0 us)
Async XLA Ops:
  0.0 19.7 %collective-permute-start.7 = (bf16[2048,128]{1,0:T(8,128)(2,1)}, bf16[2048,128]{1,0:T(8,128)(2,1)S(1)}, u32[]{:S(2)}, u32[]{:S(2)}) collective-permute-start(bf16[2048,128]{1,0:T(8,128)(2,1)} %bitcast.69), channel_id=1, source_target_pairs={{0,128},{128,0},{1,129},{129,1},{2,130},{130,2},{3,131},{131,3},{4... | collective-permute-start | bytes 1572872 | tf_op jit(solution)/shard_map/ppermute | solution.py:54
  0.0 19.7 %collective-permute-start.8 = (bf16[2048,128]{1,0:T(8,128)(2,1)}, bf16[2048,128]{1,0:T(8,128)(2,1)S(1)}, u32[]{:S(2)}, u32[]{:S(2)}) collective-permute-start(bf16[2048,128]{1,0:T(8,128)(2,1)} %bitcast.72), channel_id=1, source_target_pairs={{0,128},{128,0},{1,129},{129,1},{2,130},{130,2},{3,131},{131,3},{4... | collective-permute-start | bytes 1572872 | tf_op jit(solution)/shard_map/ppermute | solution.py:54
  12.5 7.2 %collective-permute-start.3 = (bf16[4,128,128]{2,1,0:T(8,128)(2,1)S(1)}, bf16[4,128,128]{2,1,0:T(8,128)(2,1)S(1)}, u32[]{:S(2)}, u32[]{:S(2)}) collective-permute-start(bf16[4,128,128]{2,1,0:T(8,128)(2,1)S(1)} %pad_maximum_fusion.1.o0), channel_id=1, source_target_pairs={{0,32},{8,40},{16,48},{24,56},{32,64},{40,72},{48,80},{56,88},{64,... | collective-permute-start | bytes 393224 | tf_op jit(solution)/shard_map/ppermute | solution.py:40
  15.8 50.8 %collective-permute-start.20 = (bf16[2048,128]{1,0:T(8,128)(2,1)S(1)}, bf16[2048,128]{1,0:T(8,128)(2,1)S(1)}, u32[]{:S(2)}, u32[]{:S(2)}) collective-permute-start(bf16[2048,128]{1,0:T(8,128)(2,1)S(1)} %bitcast.63), channel_id=1, source_target_pairs={{0,128},{128,0},{1,129},{129,1},{2,130},{130,2},{3,131},{131,3},{4... | collective-permute-start | bytes 1572872 | tf_op jit(solution)/shard_map/ppermute | solution.py:54
  18.4 50.4 %collective-permute-start.21 = (bf16[128,2048]{1,0:T(8,128)(2,1)S(1)}, bf16[128,2048]{1,0:T(8,128)(2,1)S(1)}, u32[]{:S(2)}, u32[]{:S(2)}) collective-permute-start(bf16[128,2048]{1,0:T(8,128)(2,1)S(1)} %bitcast.66), channel_id=1, source_target_pairs={{0,128},{128,0},{1,129},{129,1},{2,130},{130,2},{3,131},{131,3},{4... | collective-permute-start | bytes 1572872 | tf_op jit(solution)/shard_map/ppermute | solution.py:54
  22.8 42.6 %collective-permute-start.18 = (bf16[128,256]{1,0:T(8,128)(2,1)S(1)}, bf16[128,256]{1,0:T(8,128)(2,1)S(1)}, u32[]{:S(2)}, u32[]{:S(2)}) collective-permute-start(bf16[128,256]{1,0:T(8,128)(2,1)S(1)} %key_values.2), channel_id=1, source_target_pairs={{0,7},{1,0},{2,1},{3,2},{4,3},{5,4},{6,5},{7,6},{8,15},{9,8},{10,9... | collective-permute-start | bytes 196616 | tf_op jit(solution)/shard_map/ppermute | solution.py:351
  28.7 36.6 %collective-permute-start.17 = (bf16[128,256]{1,0:T(8,128)(2,1)S(1)}, bf16[128,256]{1,0:T(8,128)(2,1)S(1)}, u32[]{:S(2)}, u32[]{:S(2)}) collective-permute-start(bf16[128,256]{1,0:T(8,128)(2,1)S(1)} %key_values.2), channel_id=1, source_target_pairs={{0,6},{1,7},{2,0},{3,1},{4,2},{5,3},{6,4},{7,5},{8,14},{9,15},{10,... | collective-permute-start | bytes 196616 | tf_op jit(solution)/shard_map/ppermute | solution.py:351
  35.6 7.4 %collective-permute-start.13 = (bf16[128,256]{1,0:T(8,128)(2,1)S(1)}, bf16[128,256]{1,0:T(8,128)(2,1)S(1)}, u32[]{:S(2)}, u32[]{:S(2)}) collective-permute-start(bf16[128,256]{1,0:T(8,128)(2,1)S(1)} %key_values.2), channel_id=1, source_target_pairs={{0,2},{1,3},{2,4},{3,5},{4,6},{5,7},{6,0},{7,1},{8,10},{9,11},{10,... | collective-permute-start | bytes 196616 | tf_op jit(solution)/shard_map/ppermute | solution.py:351
  43.0 7.5 %collective-permute-start.14 = (bf16[128,256]{1,0:T(8,128)(2,1)S(1)}, bf16[128,256]{1,0:T(8,128)(2,1)S(1)}, u32[]{:S(2)}, u32[]{:S(2)}) collective-permute-start(bf16[128,256]{1,0:T(8,128)(2,1)S(1)} %key_values.2), channel_id=1, source_target_pairs={{0,3},{1,4},{2,5},{3,6},{4,7},{5,0},{6,1},{7,2},{8,11},{9,12},{10,... | collective-permute-start | bytes 196616 | tf_op jit(solution)/shard_map/ppermute | solution.py:351
  50.5 8.7 %collective-permute-start.15 = (bf16[128,256]{1,0:T(8,128)(2,1)S(1)}, bf16[128,256]{1,0:T(8,128)(2,1)S(1)}, u32[]{:S(2)}, u32[]{:S(2)}) collective-permute-start(bf16[128,256]{1,0:T(8,128)(2,1)S(1)} %key_values.2), channel_id=1, source_target_pairs={{0,4},{1,5},{2,6},{3,7},{4,0},{5,1},{6,2},{7,3},{8,12},{9,13},{10,... | collective-permute-start | bytes 196616 | tf_op jit(solution)/shard_map/ppermute | solution.py:351
  65.4 11.3 %collective-permute-start.19 = (bf16[8,128,256]{2,1,0:T(8,128)(2,1)S(1)}, bf16[8,128,256]{2,1,0:T(8,128)(2,1)S(1)}, u32[]{:S(2)}, u32[]{:S(2)}) collective-permute-start(bf16[8,128,256]{2,1,0:T(8,128)(2,1)S(1)} %bitcast_dynamic-update-slice_fusion.8.kv_same), channel_id=1, source_target_pairs={{0,128},{128,0},{1,129},{129,1},{2,130},{130,2},{3,131},{131,3},{4... | collective-permute-start | bytes 1572872 | tf_op jit(solution)/shard_map/ppermute | solution.py:54
  66.0 8.0 %collective-permute-start.10 = (bf16[4,256,128]{2,1,0:T(8,128)(2,1)S(1)}, bf16[4,256,128]{2,1,0:T(8,128)(2,1)S(1)}, u32[]{:S(2)}, u32[]{:S(2)}) collective-permute-start(bf16[4,256,128]{2,1,0:T(8,128)(2,1)S(1)} %slice.8.x0), channel_id=1, source_target_pairs={{0,64},{8,72},{16,80},{24,88},{32,96},{40,104},{48,112},{56,120},{... | collective-permute-start | bytes 786440 | tf_op jit(solution)/shard_map/ppermute | solution.py:40
  66.6 10.1 %collective-permute-start.9 = (bf16[4,256,128]{2,1,0:T(8,128)(2,1)S(1)}, bf16[4,256,128]{2,1,0:T(8,128)(2,1)S(1)}, u32[]{:S(2)}, u32[]{:S(2)}) collective-permute-start(bf16[4,256,128]{2,1,0:T(8,128)(2,1)S(1)} %slice.8.x0), channel_id=1, source_target_pairs={{0,32},{8,40},{16,48},{24,56},{32,64},{40,72},{48,80},{56,88},{64,... | collective-permute-start | bytes 786440 | tf_op jit(solution)/shard_map/ppermute | solution.py:40
  81.3 41.2 %collective-permute-start.37 = (bf16[128,256]{1,0:T(8,128)(2,1)S(1)}, bf16[128,256]{1,0:T(8,128)(2,1)S(1)}, u32[]{:S(2)}, u32[]{:S(2)}) collective-permute-start(bf16[128,256]{1,0:T(8,128)(2,1)S(1)} %key_values.3), channel_id=1, source_target_pairs={{0,7},{1,0},{2,1},{3,2},{4,3},{5,4},{6,5},{7,6},{8,15},{9,8},{10,9... | collective-permute-start | bytes 196616 | tf_op jit(solution)/shard_map/ppermute | solution.py:351
  81.4 28.0 %collective-permute-start.35 = (bf16[128,256]{1,0:T(8,128)(2,1)S(1)}, bf16[128,256]{1,0:T(8,128)(2,1)S(1)}, u32[]{:S(2)}, u32[]{:S(2)}) collective-permute-start(bf16[128,256]{1,0:T(8,128)(2,1)S(1)} %key_values.3), channel_id=1, source_target_pairs={{0,5},{1,6},{2,7},{3,0},{4,1},{5,2},{6,3},{7,4},{8,13},{9,14},{10,... | collective-permute-start | bytes 196616 | tf_op jit(solution)/shard_map/ppermute | solution.py:351
  82.5 24.1 %collective-permute-start.34 = (bf16[128,256]{1,0:T(8,128)(2,1)S(1)}, bf16[128,256]{1,0:T(8,128)(2,1)S(1)}, u32[]{:S(2)}, u32[]{:S(2)}) collective-permute-start(bf16[128,256]{1,0:T(8,128)(2,1)S(1)} %key_values.3), channel_id=1, source_target_pairs={{0,4},{1,5},{2,6},{3,7},{4,0},{5,1},{6,2},{7,3},{8,12},{9,13},{10,... | collective-permute-start | bytes 196616 | tf_op jit(solution)/shard_map/ppermute | solution.py:351
  87.9 17.4 %collective-permute-start.33 = (bf16[128,256]{1,0:T(8,128)(2,1)S(1)}, bf16[128,256]{1,0:T(8,128)(2,1)S(1)}, u32[]{:S(2)}, u32[]{:S(2)}) collective-permute-start(bf16[128,256]{1,0:T(8,128)(2,1)S(1)} %key_values.3), channel_id=1, source_target_pairs={{0,3},{1,4},{2,5},{3,6},{4,7},{5,0},{6,1},{7,2},{8,11},{9,12},{10,... | collective-permute-start | bytes 196616 | tf_op jit(solution)/shard_map/ppermute | solution.py:351
  88.0 10.2 %collective-permute-start.31 = (bf16[128,256]{1,0:T(8,128)(2,1)S(1)}, bf16[128,256]{1,0:T(8,128)(2,1)S(1)}, u32[]{:S(2)}, u32[]{:S(2)}) collective-permute-start(bf16[128,256]{1,0:T(8,128)(2,1)S(1)} %key_values.3), channel_id=1, source_target_pairs={{0,1},{1,2},{2,3},{3,4},{4,5},{5,6},{6,7},{7,0},{8,9},{9,10},{10,1... | collective-permute-start | bytes 196616 | tf_op jit(solution)/shard_map/ppermute | solution.py:351
  98.2 7.1 %collective-permute-start.32 = (bf16[128,256]{1,0:T(8,128)(2,1)S(1)}, bf16[128,256]{1,0:T(8,128)(2,1)S(1)}, u32[]{:S(2)}, u32[]{:S(2)}) collective-permute-start(bf16[128,256]{1,0:T(8,128)(2,1)S(1)} %key_values.3), channel_id=1, source_target_pairs={{0,2},{1,3},{2,4},{3,5},{4,6},{5,7},{6,0},{7,1},{8,10},{9,11},{10,... | collective-permute-start | bytes 196616 | tf_op jit(solution)/shard_map/ppermute | solution.py:351
  105.3 10.4 %collective-permute-start.22 = (bf16[4,256,128]{2,1,0:T(8,128)(2,1)S(1)}, bf16[4,256,128]{2,1,0:T(8,128)(2,1)S(1)}, u32[]{:S(2)}, u32[]{:S(2)}) collective-permute-start(bf16[4,256,128]{2,1,0:T(8,128)(2,1)S(1)} %get-tuple-element.19), channel_id=1, source_target_pairs={{0,32},{8,40},{16,48},{24,56},{32,64},{40,72},{48,80},{56,88},{64,... | collective-permute-start | bytes 786440 | tf_op jit(solution)/shard_map/ppermute | solution.py:40
  105.3 10.4 %collective-permute-start.23 = (bf16[4,256,128]{2,1,0:T(8,128)(2,1)S(1)}, bf16[4,256,128]{2,1,0:T(8,128)(2,1)S(1)}, u32[]{:S(2)}, u32[]{:S(2)}) collective-permute-start(bf16[4,256,128]{2,1,0:T(8,128)(2,1)S(1)} %get-tuple-element.20), channel_id=1, source_target_pairs={{0,64},{8,72},{16,80},{24,88},{32,96},{40,104},{48,112},{56,120},{... | collective-permute-start | bytes 786440 | tf_op jit(solution)/shard_map/ppermute | solution.py:40
  106.7 10.0 %collective-permute-start.24 = (bf16[4,256,128]{2,1,0:T(8,128)(2,1)S(1)}, bf16[4,256,128]{2,1,0:T(8,128)(2,1)S(1)}, u32[]{:S(2)}, u32[]{:S(2)}) collective-permute-start(bf16[4,256,128]{2,1,0:T(8,128)(2,1)S(1)} %get-tuple-element.21), channel_id=1, source_target_pairs={{0,96},{8,104},{16,112},{24,120},{32,0},{40,8},{48,16},{56,24},{64... | collective-permute-start | bytes 786440 | tf_op jit(solution)/shard_map/ppermute | solution.py:40
  109.4 13.1 %collective-permute-start.36 = (bf16[128,256]{1,0:T(8,128)(2,1)S(1)}, bf16[128,256]{1,0:T(8,128)(2,1)S(1)}, u32[]{:S(2)}, u32[]{:S(2)}) collective-permute-start(bf16[128,256]{1,0:T(8,128)(2,1)S(1)} %key_values.3), channel_id=1, source_target_pairs={{0,6},{1,7},{2,0},{3,1},{4,2},{5,3},{6,4},{7,5},{8,14},{9,15},{10,... | collective-permute-start | bytes 196616 | tf_op jit(solution)/shard_map/ppermute | solution.py:351
  119.7 7.9 %collective-permute-start.26 = (bf16[4,256,128]{2,1,0:T(8,128)(2,1)S(1)}, bf16[4,256,128]{2,1,0:T(8,128)(2,1)S(1)}, u32[]{:S(2)}, u32[]{:S(2)}) collective-permute-start(bf16[4,256,128]{2,1,0:T(8,128)(2,1)S(1)} %add_convert_fusion.2), channel_id=1, source_target_pairs={{0,16},{8,24},{16,0},{24,8},{32,48},{40,56},{48,32},{56,40},{64,80... | collective-permute-start | bytes 786440 | tf_op jit(solution)/shard_map/ppermute | solution.py:36
  119.9 8.2 %collective-permute-start.25 = (bf16[4,256,128]{2,1,0:T(8,128)(2,1)S(1)}, bf16[4,256,128]{2,1,0:T(8,128)(2,1)S(1)}, u32[]{:S(2)}, u32[]{:S(2)}) collective-permute-start(bf16[4,256,128]{2,1,0:T(8,128)(2,1)S(1)} %add_convert_fusion.2), channel_id=1, source_target_pairs={{0,8},{8,16},{16,24},{24,0},{32,40},{40,48},{48,56},{56,32},{64,72... | collective-permute-start | bytes 786440 | tf_op jit(solution)/shard_map/ppermute | solution.py:36
  122.5 10.0 %collective-permute-start.38 = (bf16[8,128,256]{2,1,0:T(8,128)(2,1)S(1)}, bf16[8,128,256]{2,1,0:T(8,128)(2,1)S(1)}, u32[]{:S(2)}, u32[]{:S(2)}) collective-permute-start(bf16[8,128,256]{2,1,0:T(8,128)(2,1)S(1)} %bitcast_dynamic-update-slice_fusion.kv_same), channel_id=1, source_target_pairs={{0,128},{128,0},{1,129},{129,1},{2,130},{130,2},{3,131},{131,3},{4... | collective-permute-start | bytes 1572872 | tf_op jit(solution)/shard_map/ppermute | solution.py:54
  128.4 9.4 %collective-permute-start.30 = (bf16[4,256,128]{2,1,0:T(8,128)(2,1)S(1)}, bf16[4,256,128]{2,1,0:T(8,128)(2,1)S(1)}, u32[]{:S(2)}, u32[]{:S(2)}) collective-permute-start(bf16[4,256,128]{2,1,0:T(8,128)(2,1)S(1)} %add_convert_fusion.1.x0), channel_id=1, source_target_pairs={{0,96},{8,104},{16,112},{24,120},{32,0},{40,8},{48,16},{56,24},{64... | collective-permute-start | bytes 786440 | tf_op jit(solution)/shard_map/ppermute | solution.py:40
  131.1 8.0 %collective-permute-start.29 = (bf16[4,256,128]{2,1,0:T(8,128)(2,1)S(1)}, bf16[4,256,128]{2,1,0:T(8,128)(2,1)S(1)}, u32[]{:S(2)}, u32[]{:S(2)}) collective-permute-start(bf16[4,256,128]{2,1,0:T(8,128)(2,1)S(1)} %add_convert_fusion.1.x0), channel_id=1, source_target_pairs={{0,64},{8,72},{16,80},{24,88},{32,96},{40,104},{48,112},{56,120},{... | collective-permute-start | bytes 786440 | tf_op jit(solution)/shard_map/ppermute | solution.py:40
  132.5 9.3 %collective-permute-start.28 = (bf16[4,256,128]{2,1,0:T(8,128)(2,1)S(1)}, bf16[4,256,128]{2,1,0:T(8,128)(2,1)S(1)}, u32[]{:S(2)}, u32[]{:S(2)}) collective-permute-start(bf16[4,256,128]{2,1,0:T(8,128)(2,1)S(1)} %add_convert_fusion.1.x0), channel_id=1, source_target_pairs={{0,32},{8,40},{16,48},{24,56},{32,64},{40,72},{48,80},{56,88},{64,... | collective-permute-start | bytes 786440 | tf_op jit(solution)/shard_map/ppermute | solution.py:40
  146.9 10.5 %collective-permute-start.39 = (bf16[4,256,128]{2,1,0:T(8,128)(2,1)S(1)}, bf16[4,256,128]{2,1,0:T(8,128)(2,1)S(1)}, u32[]{:S(2)}, u32[]{:S(2)}) collective-permute-start(bf16[4,256,128]{2,1,0:T(8,128)(2,1)S(1)} %get-tuple-element.24), channel_id=1, source_target_pairs={{0,32},{8,40},{16,48},{24,56},{32,64},{40,72},{48,80},{56,88},{64,... | collective-permute-start | bytes 786440 | tf_op jit(solution)/shard_map/ppermute | solution.py:40
  147.0 10.4 %collective-permute-start.40 = (bf16[4,256,128]{2,1,0:T(8,128)(2,1)S(1)}, bf16[4,256,128]{2,1,0:T(8,128)(2,1)S(1)}, u32[]{:S(2)}, u32[]{:S(2)}) collective-permute-start(bf16[4,256,128]{2,1,0:T(8,128)(2,1)S(1)} %get-tuple-element.25), channel_id=1, source_target_pairs={{0,64},{8,72},{16,80},{24,88},{32,96},{40,104},{48,112},{56,120},{... | collective-permute-start | bytes 786440 | tf_op jit(solution)/shard_map/ppermute | solution.py:40
  149.0 10.6 %collective-permute-start.41 = (bf16[4,256,128]{2,1,0:T(8,128)(2,1)S(1)}, bf16[4,256,128]{2,1,0:T(8,128)(2,1)S(1)}, u32[]{:S(2)}, u32[]{:S(2)}) collective-permute-start(bf16[4,256,128]{2,1,0:T(8,128)(2,1)S(1)} %get-tuple-element.26), channel_id=1, source_target_pairs={{0,96},{8,104},{16,112},{24,120},{32,0},{40,8},{48,16},{56,24},{64... | collective-permute-start | bytes 786440 | tf_op jit(solution)/shard_map/ppermute | solution.py:40
  (25 other events, 148.4 us)

commit v4 on v3

--- a/solution.py
+++ b/solution.py
@@ -102,8 +102,8 @@
     return block
 
 
-def normed_into(block_of, pieces, gain, normed):
-    rows = normed.shape[0]
+def normed_into(block_of, pieces, gains, targets):
+    rows = targets[0].shape[0]
 
     def add_squares(part, squares):
         for piece in pieces:
@@ -119,8 +119,11 @@
     def _(part):
         for step, piece in enumerate(pieces):
             block = block_of(step, part)
-            scaled = (piece[part].astype(jnp.float32) * inverse) * gain[pl.ds(block, 1), :]
-            normed[:, tile_cols(block)] = scaled.astype(jnp.bfloat16)
+            scaled = piece[part].astype(jnp.float32) * inverse
+            for gain, target in zip(gains, targets):
+                target[:, tile_cols(block)] = (scaled * gain[pl.ds(block, 1), :]).astype(
+                    jnp.bfloat16
+                )
 
 
 def chosen_gain(core, section, mine, theirs, index, gain):
@@ -128,7 +131,6 @@
 
 
 def key_value_kernel(
-    section,
     o0,
     o1,
     o2,
@@ -139,24 +141,33 @@
     key_theirs,
     value_mine,
     value_theirs,
-    out,
+    out_zero,
+    out_one,
     normed,
     weight,
-    gain,
     sems,
 ):
+    sources = ((key_mine, value_mine), (key_theirs, value_theirs))
+    copies = [
+        pltpu.make_async_copy(
+            source, weight.at[whose, :, half * HS : (half + 1) * HS], sems.at[whose * 2 + half]
+        )
+        for whose, pair in enumerate(sources)
+        for half, source in enumerate(pair)
+    ]
+    for copy in copies:
+        copy.start()
+    gains = (gain_mine.at[1], gain_theirs.at[1])
+    targets = (normed.at[0], normed.at[1])
     where = position()
-    core = where[0]
-    key_at, value_at = weight.at[:, :HS], weight.at[:, HS:]
-    fetch(core, section, key_mine, key_theirs, key_at, sems.at[0], start)
-    fetch(core, section, value_mine, value_theirs, value_at, sems.at[1], start)
-    chosen_gain(core, section, gain_mine, gain_theirs, 1, gain)
-    normed_into(placed(where, True), (o0, o1, o2, o3), gain, normed)
-    fetch(core, section, key_mine, key_theirs, key_at, sems.at[0], wait)
-    fetch(core, section, value_mine, value_theirs, value_at, sems.at[1], wait)
-    out[...] = jnp.dot(
-        normed[...], weight[...], preferred_element_type=jnp.float32
-    ).astype(jnp.bfloat16)
+    normed_into(placed(where, True), (o0, o1, o2, o3), gains, targets)
+    for copy in copies:
+        copy.wait()
+    for section, out in enumerate((out_zero, out_one)):
+        whose = lax.rem(where[0] + section, 2)
+        out[...] = jnp.dot(
+            normed[whose], weight[whose], preferred_element_type=jnp.float32
+        ).astype(jnp.bfloat16)
 
 
 def attend_kernel(
@@ -197,7 +208,7 @@
     fetch(core, section, query_mine, query_theirs, w_query, sems.at[0], start)
     fetch(core, section, out_mine, out_theirs, w_out, sems.at[1], start)
     chosen_gain(core, section, gain_mine, gain_theirs, 0, gain)
-    normed_into(placed(where, section == 0), (x0, x1, x2, x3), gain, normed)
+    normed_into(placed(where, section == 0), (x0, x1, x2, x3), (gain,), (normed,))
     if section == 0:
 
         @pl.loop(0, SIDE)
@@ -257,24 +268,23 @@
             out[part] = normed[:, tile_cols(block)]
 
 
-def key_values(section, pieces, gains, w_key, w_value):
+def key_values(pieces, gains, w_key, w_value):
     rows = pieces[0].shape[1]
     features = w_key[0].shape[0]
     return pl.pallas_call(
-        functools.partial(key_value_kernel, section),
-        out_shape=jax.ShapeDtypeStruct((rows, 2 * HS), jnp.bfloat16),
+        key_value_kernel,
+        out_shape=[jax.ShapeDtypeStruct((rows, 2 * HS), jnp.bfloat16)] * 2,
         in_specs=[VMEM] * 6 + [ANY] * 4,
-        out_specs=VMEM,
+        out_specs=[VMEM] * 2,
         scratch_shapes=[
-            pltpu.VMEM((rows, features), jnp.bfloat16),
-            pltpu.VMEM((features, 2 * HS), jnp.bfloat16),
-            pltpu.VMEM(gains[0].shape[1:], jnp.float32),
-            pltpu.SemaphoreType.DMA((2,)),
+            pltpu.VMEM((2, rows, features), jnp.bfloat16),
+            pltpu.VMEM((2, features, 2 * HS), jnp.bfloat16),
+            pltpu.SemaphoreType.DMA((4,)),
         ],
         cost_estimate=pl.CostEstimate(
-            flops=4 * rows * features * HS, bytes_accessed=6 * features * HS, transcendentals=0
+            flops=8 * rows * features * HS, bytes_accessed=10 * features * HS, transcendentals=0
         ),
-        compiler_params=pltpu.CompilerParams(vmem_limit_bytes=8 << 20),
+        compiler_params=pltpu.CompilerParams(vmem_limit_bytes=12 << 20),
         name="key_values",
     )(*pieces, *gains, *w_key, *w_value)
 
@@ -339,12 +349,14 @@
     obs_group, patch_group = group[:, :obs_rows], group[:, obs_rows:]
 
     gains = jnp.concatenate([patch_gain, obs_gain], axis=0).reshape(2, SIDE * SIDE, HS)
-    gains, keys, values, queries, outs = [
-        (mine, swapped(mine)) for mine in (gains, w_key[0], w_value[0], w_query[0], w_out[0])
-    ]
-
-    obs_pieces = all_far(obs_group)
-    mine = key_values(0, obs_pieces, gains, keys, values)
+    gains, keys, values = [(mine, swapped(mine)) for mine in (gains, w_key[0], w_value[0])]
+    queries, outs = [(mine, swapped(mine)) for mine in (w_query[0], w_out[0])]
+
+    obs_far = {}
+    for step in AROUND:
+        obs_far[step] = far(obs_group, step)
+    obs_pieces = [obs_group] + [obs_far[step] for step in range(1, SIDE)]
+    kv_first, kv_second = key_values(obs_pieces, gains, keys, values)
 
     def to_patch(value, steps):
         return {
@@ -354,22 +366,20 @@
             for step in steps
         }
 
-    arrived = to_patch(mine, (4, 3, 5)) | to_patch(mine, (2, 6, 1, 7))
-    same = jnp.stack([mine] + [arrived[step] for step in range(1, patch_count)])
+    arrived = to_patch(kv_first, (4, 3, 5)) | to_patch(kv_first, (2, 6, 1, 7))
+    same = jnp.stack([kv_first] + [arrived[step] for step in range(1, patch_count)])
     kv_zero = (same, swapped(same))
-    patch_group, mine = lax.optimization_barrier((patch_group, mine))
     patch_pieces = all_far(patch_group)
-    mine = key_values(1, obs_pieces, gains, keys, values)
 
     def reduced(parts):
         arrived = {step: far(parts[step], step) for step in AROUND}
         return added(parts[0], [arrived[step] for step in range(1, SIDE)]).astype(jnp.bfloat16)
 
     *parts, kept = attend(0, lists, patch_pieces, kv_zero, gains, queries, outs)
-    mine, _ = lax.optimization_barrier((mine, kept))
-    arrived = to_patch(mine, (4, 1)) | to_patch(mine, (3, 5))
-    arrived |= to_patch(mine, (2, 6, 7))
-    same = jnp.stack([mine] + [arrived[step] for step in range(1, patch_count)])
+    kv_second, _ = lax.optimization_barrier((kv_second, kept))
+    arrived = to_patch(kv_second, (1, 7)) | to_patch(kv_second, (4, 3, 5))
+    arrived |= to_patch(kv_second, (2, 6))
+    same = jnp.stack([kv_second] + [arrived[step] for step in range(1, patch_count)])
     kv_one = (same, swapped(same))
 
     total = reduced(parts)

time: 173 us -> 147 us (0.85)
  the two profiles are of different devices: /device:TPU:2 before, /device:TPU:15 now
where the time goes in v4:
time: 147 us
  starting transfers between devices  84 us (57%)
  waiting for transfers between devices  49.1 us (33%)
  Pallas kernels  11.3 us (8%)
    ppermute x14, starting transfers between devices, to_patch(): lax.ppermute(value, 'patch', [(at, (at + step) % patch_count) for at in r...  31.9 us
    ppermute x8, starting transfers between devices, swapped(): return lax.ppermute(value, 'pipe', [(0, 1), (1, 0)])  31.1 us
    ppermute x15, waiting for transfers between devices, far(): return lax.ppermute(value, ('pipe', 'obs'), square_shift(False, step))  28 us
    ppermute x14, waiting for transfers between devices, to_patch(): lax.ppermute(value, 'patch', [(at, (at + step) % patch_count) for at in r...  12.6 us
    ppermute x9, starting transfers between devices, near(): return lax.ppermute(value, ('pipe', 'obs'), square_shift(True, step))  11.7 us
    pallas_call x2, Pallas kernels, attend(): pl.pallas_call(functools.partial(attend_kernel, section), out_shape=[piec...  9.78 us
    ppermute x15, starting transfers between devices, far(): return lax.ppermute(value, ('pipe', 'obs'), square_shift(False, step))  9.25 us
    ppermute x9, waiting for transfers between devices, near(): return lax.ppermute(value, ('pipe', 'obs'), square_shift(True, step))  7.66 us
  transfers between devices with their start and end apart: 46, of which 24 were waited for; matrix products, arithmetic and copies ran while one was open for 0% of the time, Pallas kernels for 1%

profile of v4, /device:TPU:15, one launch (start us, length us, event | category | flops | bytes accessed | tf_op | source)
XLA Modules:
  0.0 147.2 jit_solution(11640566824529441745)
XLA Ops:
  4.0 2.0 %collective-permute-start.2 = (bf16[384,128]{1,0:T(8,128)(2,1)S(1)}, bf16[384,128]{1,0:T(8,128)(2,1)S(1)}, u32[]{:S(2)}, u32[]{:S(2)}) collective-permute-start(bf16[384,128]{1,0:T(8,128)(2,1)S(1)} %get-tuple-element.35), channel_id=1, source_target_pairs={{0,24},{8,0},{16,8},{24,16},{32,56},{40,32},{48,40},{56,48},{64,88... | collective-permute-start | bytes 294920 | tf_op jit(solution)/shard_map/ppermute | solution.py:36
  12.7 3.8 %collective-permute-start.20 = (bf16[2048,128]{1,0:T(8,128)(2,1)S(1)}, bf16[2048,128]{1,0:T(8,128)(2,1)S(1)}, u32[]{:S(2)}, u32[]{:S(2)}) collective-permute-start(bf16[2048,128]{1,0:T(8,128)(2,1)S(1)} %bitcast.63), channel_id=1, source_target_pairs={{0,128},{128,0},{1,129},{129,1},{2,130},{130,2},{3,131},{131,3},{4... | collective-permute-start | bytes 1572872 | tf_op jit(solution)/shard_map/ppermute | solution.py:54
  16.5 3.0 %collective-permute-start.21 = (bf16[128,2048]{1,0:T(8,128)(2,1)S(1)}, bf16[128,2048]{1,0:T(8,128)(2,1)S(1)}, u32[]{:S(2)}, u32[]{:S(2)}) collective-permute-start(bf16[128,2048]{1,0:T(8,128)(2,1)S(1)} %bitcast.66), channel_id=1, source_target_pairs={{0,128},{128,0},{1,129},{129,1},{2,130},{130,2},{3,131},{131,3},{4... | collective-permute-start | bytes 1572872 | tf_op jit(solution)/shard_map/ppermute | solution.py:54
  23.1 3.0 %collective-permute-start.13 = (bf16[128,256]{1,0:T(8,128)(2,1)S(1)}, bf16[128,256]{1,0:T(8,128)(2,1)S(1)}, u32[]{:S(2)}, u32[]{:S(2)}) collective-permute-start(bf16[128,256]{1,0:T(8,128)(2,1)S(1)} %get-tuple-element.17), channel_id=1, source_target_pairs={{0,2},{1,3},{2,4},{3,5},{4,6},{5,7},{6,0},{7,1},{8,10},{9,11},{10,... | collective-permute-start | bytes 196616 | tf_op jit(solution)/shard_map/ppermute | solution.py:363
  26.1 2.6 %collective-permute-done.12 = bf16[128,256]{1,0:T(8,128)(2,1)S(1)} collective-permute-done((bf16[128,256]{1,0:T(8,128)(2,1)S(1)}, bf16[128,256]{1,0:T(8,128)(2,1)S(1)}, u32[]{:S(2)}, u32[]{:S(2)}) %collective-permute-start.12) | collective-permute-done | bytes 65568 | tf_op jit(solution)/shard_map/ppermute | solution.py:363
  31.3 3.7 %collective-permute-start.15 = (bf16[128,256]{1,0:T(8,128)(2,1)S(1)}, bf16[128,256]{1,0:T(8,128)(2,1)S(1)}, u32[]{:S(2)}, u32[]{:S(2)}) collective-permute-start(bf16[128,256]{1,0:T(8,128)(2,1)S(1)} %get-tuple-element.17), channel_id=1, source_target_pairs={{0,4},{1,5},{2,6},{3,7},{4,0},{5,1},{6,2},{7,3},{8,12},{9,13},{10,... | collective-permute-start | bytes 196616 | tf_op jit(solution)/shard_map/ppermute | solution.py:363
  35.7 3.8 %collective-permute-start.16 = (bf16[128,256]{1,0:T(8,128)(2,1)S(1)}, bf16[128,256]{1,0:T(8,128)(2,1)S(1)}, u32[]{:S(2)}, u32[]{:S(2)}) collective-permute-start(bf16[128,256]{1,0:T(8,128)(2,1)S(1)} %get-tuple-element.17), channel_id=1, source_target_pairs={{0,5},{1,6},{2,7},{3,0},{4,1},{5,2},{6,3},{7,4},{8,13},{9,14},{10,... | collective-permute-start | bytes 196616 | tf_op jit(solution)/shard_map/ppermute | solution.py:363
  39.6 2.4 %collective-permute-done.15 = bf16[128,256]{1,0:T(8,128)(2,1)S(1)} collective-permute-done((bf16[128,256]{1,0:T(8,128)(2,1)S(1)}, bf16[128,256]{1,0:T(8,128)(2,1)S(1)}, u32[]{:S(2)}, u32[]{:S(2)}) %collective-permute-start.15) | collective-permute-done | bytes 65568 | tf_op jit(solution)/shard_map/ppermute | solution.py:363
  42.0 2.1 %collective-permute-start.18 = (bf16[128,256]{1,0:T(8,128)(2,1)S(1)}, bf16[128,256]{1,0:T(8,128)(2,1)S(1)}, u32[]{:S(2)}, u32[]{:S(2)}) collective-permute-start(bf16[128,256]{1,0:T(8,128)(2,1)S(1)} %get-tuple-element.17), channel_id=1, source_target_pairs={{0,7},{1,0},{2,1},{3,2},{4,3},{5,4},{6,5},{7,6},{8,15},{9,8},{10,9... | collective-permute-start | bytes 196616 | tf_op jit(solution)/shard_map/ppermute | solution.py:363
  44.1 3.2 %collective-permute-done.17 = bf16[128,256]{1,0:T(8,128)(2,1)S(1)} collective-permute-done((bf16[128,256]{1,0:T(8,128)(2,1)S(1)}, bf16[128,256]{1,0:T(8,128)(2,1)S(1)}, u32[]{:S(2)}, u32[]{:S(2)}) %collective-permute-start.17) | collective-permute-done | bytes 65568 | tf_op jit(solution)/shard_map/ppermute | solution.py:363
  47.4 7.1 %collective-permute-start.19 = (bf16[8,128,256]{2,1,0:T(8,128)(2,1)S(1)}, bf16[8,128,256]{2,1,0:T(8,128)(2,1)S(1)}, u32[]{:S(2)}, u32[]{:S(2)}) collective-permute-start(bf16[8,128,256]{2,1,0:T(8,128)(2,1)S(1)} %bitcast_dynamic-update-slice_fusion.8.kv_same), channel_id=1, source_target_pairs={{0,128},{128,0},{1,129},{129,1},{2,130},{130,2},{3,131},{131,3},{4... | collective-permute-start | bytes 1572872 | tf_op jit(solution)/shard_map/ppermute | solution.py:54
  54.8 6.5 %collective-permute-done.4.x2 = bf16[4,256,128]{2,1,0:T(8,128)(2,1)S(1)} collective-permute-done((bf16[4,256,128]{2,1,0:T(8,128)(2,1)S(1)}, bf16[4,256,128]{2,1,0:T(8,128)(2,1)S(1)}, u32[]{:S(2)}, u32[]{:S(2)}) %collective-permute-start.4) | collective-permute-done | bytes 262176 | tf_op jit(solution)/shard_map/ppermute | solution.py:40
  61.3 2.6 %collective-permute-done.5.x3 = bf16[4,256,128]{2,1,0:T(8,128)(2,1)S(1)} collective-permute-done((bf16[4,256,128]{2,1,0:T(8,128)(2,1)S(1)}, bf16[4,256,128]{2,1,0:T(8,128)(2,1)S(1)}, u32[]{:S(2)}, u32[]{:S(2)}) %collective-permute-start.5) | collective-permute-done | bytes 262176 | tf_op jit(solution)/shard_map/ppermute | solution.py:40
  63.9 4.6 %attend.2 = (bf16[4,256,128]{2,1,0:T(8,128)(2,1)S(1)}, bf16[4,256,128]{2,1,0:T(8,128)(2,1)S(1)}, bf16[4,256,128]{2,1,0:T(8,128)(2,1)S(1)}, bf16[4,256,128]{2,1,0:T(8,128)(2,1)S(1)}, bf16[4,256,128]{2,1,0:T(8,128)(2,1)S(1)}) custom-call(s32[4,8]{1,0:T(4,128)S(1)} %copy-done.5, s32[4]{0:T(128)S(1)} %copy-done.7, f32[4,8]{1,0:T(4,128)S(1)} %copy-done.6, ...), custom_call_target="tpu_custom_call" | custom-call | flops 536870912 | bytes 4194304 | tf_op jit(solution)/shard_map/attend/pallas_call | solution.py:297
  68.7 2.4 %collective-permute-start.32 = (bf16[128,256]{1,0:T(8,128)(2,1)S(1)}, bf16[128,256]{1,0:T(8,128)(2,1)S(1)}, u32[]{:S(2)}, u32[]{:S(2)}) collective-permute-start(bf16[128,256]{1,0:T(8,128)(2,1)S(1)} %get-tuple-element.24), channel_id=1, source_target_pairs={{0,2},{1,3},{2,4},{3,5},{4,6},{5,7},{6,0},{7,1},{8,10},{9,11},{10,... | collective-permute-start | bytes 196616 | tf_op jit(solution)/shard_map/ppermute | solution.py:363
  74.4 3.0 %collective-permute-start.35 = (bf16[128,256]{1,0:T(8,128)(2,1)S(1)}, bf16[128,256]{1,0:T(8,128)(2,1)S(1)}, u32[]{:S(2)}, u32[]{:S(2)}) collective-permute-start(bf16[128,256]{1,0:T(8,128)(2,1)S(1)} %get-tuple-element.24), channel_id=1, source_target_pairs={{0,5},{1,6},{2,7},{3,0},{4,1},{5,2},{6,3},{7,4},{8,13},{9,14},{10,... | collective-permute-start | bytes 196616 | tf_op jit(solution)/shard_map/ppermute | solution.py:363
  77.5 2.9 %collective-permute-start.36 = (bf16[128,256]{1,0:T(8,128)(2,1)S(1)}, bf16[128,256]{1,0:T(8,128)(2,1)S(1)}, u32[]{:S(2)}, u32[]{:S(2)}) collective-permute-start(bf16[128,256]{1,0:T(8,128)(2,1)S(1)} %get-tuple-element.24), channel_id=1, source_target_pairs={{0,6},{1,7},{2,0},{3,1},{4,2},{5,3},{6,4},{7,5},{8,14},{9,15},{10,... | collective-permute-start | bytes 196616 | tf_op jit(solution)/shard_map/ppermute | solution.py:363
  81.7 2.3 %collective-permute-done.34 = bf16[128,256]{1,0:T(8,128)(2,1)S(1)} collective-permute-done((bf16[128,256]{1,0:T(8,128)(2,1)S(1)}, bf16[128,256]{1,0:T(8,128)(2,1)S(1)}, u32[]{:S(2)}, u32[]{:S(2)}) %collective-permute-start.34) | collective-permute-done | bytes 65568 | tf_op jit(solution)/shard_map/ppermute | solution.py:363
  84.0 4.5 %collective-permute-start.37 = (bf16[128,256]{1,0:T(8,128)(2,1)S(1)}, bf16[128,256]{1,0:T(8,128)(2,1)S(1)}, u32[]{:S(2)}, u32[]{:S(2)}) collective-permute-start(bf16[128,256]{1,0:T(8,128)(2,1)S(1)} %get-tuple-element.24), channel_id=1, source_target_pairs={{0,7},{1,0},{2,1},{3,2},{4,3},{5,4},{6,5},{7,6},{8,15},{9,8},{10,9... | collective-permute-start | bytes 196616 | tf_op jit(solution)/shard_map/ppermute | solution.py:363
  88.6 2.1 %collective-permute-done.24 = bf16[4,256,128]{2,1,0:T(8,128)(2,1)S(1)} collective-permute-done((bf16[4,256,128]{2,1,0:T(8,128)(2,1)S(1)}, bf16[4,256,128]{2,1,0:T(8,128)(2,1)S(1)}, u32[]{:S(2)}, u32[]{:S(2)}) %collective-permute-start.24) | collective-permute-done | bytes 262176 | tf_op jit(solution)/shard_map/ppermute | solution.py:40
  91.7 2.0 %collective-permute-start.26 = (bf16[4,256,128]{2,1,0:T(8,128)(2,1)S(1)}, bf16[4,256,128]{2,1,0:T(8,128)(2,1)S(1)}, u32[]{:S(2)}, u32[]{:S(2)}) collective-permute-start(bf16[4,256,128]{2,1,0:T(8,128)(2,1)S(1)} %add_convert_fusion.2), channel_id=1, source_target_pairs={{0,16},{8,24},{16,0},{24,8},{32,48},{40,56},{48,32},{56,40},{64,80... | collective-permute-start | bytes 786440 | tf_op jit(solution)/shard_map/ppermute | solution.py:36
  94.4 3.9 %collective-permute-start.38 = (bf16[8,128,256]{2,1,0:T(8,128)(2,1)S(1)}, bf16[8,128,256]{2,1,0:T(8,128)(2,1)S(1)}, u32[]{:S(2)}, u32[]{:S(2)}) collective-permute-start(bf16[8,128,256]{2,1,0:T(8,128)(2,1)S(1)} %bitcast_dynamic-update-slice_fusion.kv_same), channel_id=1, source_target_pairs={{0,128},{128,0},{1,129},{129,1},{2,130},{130,2},{3,131},{131,3},{4... | collective-permute-start | bytes 1572872 | tf_op jit(solution)/shard_map/ppermute | solution.py:54
  98.5 3.0 %collective-permute-done.27 = bf16[4,256,128]{2,1,0:T(8,128)(2,1)S(1)} collective-permute-done((bf16[4,256,128]{2,1,0:T(8,128)(2,1)S(1)}, bf16[4,256,128]{2,1,0:T(8,128)(2,1)S(1)}, u32[]{:S(2)}, u32[]{:S(2)}) %collective-permute-start.27) | collective-permute-done | bytes 262176 | tf_op jit(solution)/shard_map/ppermute | solution.py:36
  104.1 2.9 %collective-permute-done.28.x1 = bf16[4,256,128]{2,1,0:T(8,128)(2,1)S(1)} collective-permute-done((bf16[4,256,128]{2,1,0:T(8,128)(2,1)S(1)}, bf16[4,256,128]{2,1,0:T(8,128)(2,1)S(1)}, u32[]{:S(2)}, u32[]{:S(2)}) %collective-permute-start.28) | collective-permute-done | bytes 262176 | tf_op jit(solution)/shard_map/ppermute | solution.py:40
  107.0 2.0 %collective-permute-done.29.x2 = bf16[4,256,128]{2,1,0:T(8,128)(2,1)S(1)} collective-permute-done((bf16[4,256,128]{2,1,0:T(8,128)(2,1)S(1)}, bf16[4,256,128]{2,1,0:T(8,128)(2,1)S(1)}, u32[]{:S(2)}, u32[]{:S(2)}) %collective-permute-start.29) | collective-permute-done | bytes 262176 | tf_op jit(solution)/shard_map/ppermute | solution.py:40
  109.0 2.8 %collective-permute-done.30.x3 = bf16[4,256,128]{2,1,0:T(8,128)(2,1)S(1)} collective-permute-done((bf16[4,256,128]{2,1,0:T(8,128)(2,1)S(1)}, bf16[4,256,128]{2,1,0:T(8,128)(2,1)S(1)}, u32[]{:S(2)}, u32[]{:S(2)}) %collective-permute-start.30) | collective-permute-done | bytes 262176 | tf_op jit(solution)/shard_map/ppermute | solution.py:40
  111.9 5.1 %attend.3 = (bf16[4,256,128]{2,1,0:T(8,128)(2,1)S(1)}, bf16[4,256,128]{2,1,0:T(8,128)(2,1)S(1)}, bf16[4,256,128]{2,1,0:T(8,128)(2,1)S(1)}, bf16[4,256,128]{2,1,0:T(8,128)(2,1)S(1)}, bf16[8,128]{1,0:T(8,128)(2,1)}) custom-call(s32[4,8]{1,0:T(4,128)S(1)} %copy-done.5, s32[4]{0:T(128)S(1)} %copy-done.7, f32[4,8]{1,0:T(4,128)S(1)} %copy-done.6, ...), custom_call_target="tpu_custom_call" | custom-call | flops 536870912 | bytes 4194304 | tf_op jit(solution)/shard_map/attend/pallas_call | solution.py:297
  119.5 2.8 %collective-permute-done.39 = bf16[4,256,128]{2,1,0:T(8,128)(2,1)S(1)} collective-permute-done((bf16[4,256,128]{2,1,0:T(8,128)(2,1)S(1)}, bf16[4,256,128]{2,1,0:T(8,128)(2,1)S(1)}, u32[]{:S(2)}, u32[]{:S(2)}) %collective-permute-start.39) | collective-permute-done | bytes 262176 | tf_op jit(solution)/shard_map/ppermute | solution.py:40
  122.3 2.1 %collective-permute-done.40 = bf16[4,256,128]{2,1,0:T(8,128)(2,1)S(1)} collective-permute-done((bf16[4,256,128]{2,1,0:T(8,128)(2,1)S(1)}, bf16[4,256,128]{2,1,0:T(8,128)(2,1)S(1)}, u32[]{:S(2)}, u32[]{:S(2)}) %collective-permute-start.40) | collective-permute-done | bytes 262176 | tf_op jit(solution)/shard_map/ppermute | solution.py:40
  124.4 2.7 %collective-permute-done.41 = bf16[4,256,128]{2,1,0:T(8,128)(2,1)S(1)} collective-permute-done((bf16[4,256,128]{2,1,0:T(8,128)(2,1)S(1)}, bf16[4,256,128]{2,1,0:T(8,128)(2,1)S(1)}, u32[]{:S(2)}, u32[]{:S(2)}) %collective-permute-start.41) | collective-permute-done | bytes 262176 | tf_op jit(solution)/shard_map/ppermute | solution.py:40
  127.3 2.5 %collective-permute-start.42 = (bf16[256,128]{1,0:T(8,128)(2,1)S(1)}, bf16[256,128]{1,0:T(8,128)(2,1)S(1)}, u32[]{:S(2)}, u32[]{:S(2)}) collective-permute-start(bf16[256,128]{1,0:T(8,128)(2,1)S(1)} %get-tuple-element.31), channel_id=1, source_target_pairs={{0,16},{8,24},{16,0},{24,8},{32,48},{40,56},{48,32},{56,40},{64,80... | collective-permute-start | bytes 196616 | tf_op jit(solution)/shard_map/ppermute | solution.py:36
  134.2 11.4 %collective-permute-start.45 = (bf16[256,128]{1,0:T(8,128)(2,1)S(1)}, bf16[256,128]{1,0:T(8,128)(2,1)S(1)}, u32[]{:S(2)}, u32[]{:S(2)}) collective-permute-start(bf16[256,128]{1,0:T(8,128)(2,1)S(1)} %get-tuple-element.29), channel_id=1, source_target_pairs={{0,128},{128,0},{1,129},{129,1},{2,130},{130,2},{3,131},{131,3},{4... | collective-permute-start | bytes 196616 | tf_op jit(solution)/shard_map/ppermute | solution.py:54
  (116 shorter events, 35.7 us)
Async XLA Ops:
  0.0 19.8 %collective-permute-start.10 = (bf16[2048,128]{1,0:T(8,128)(2,1)}, bf16[2048,128]{1,0:T(8,128)(2,1)S(1)}, u32[]{:S(2)}, u32[]{:S(2)}) collective-permute-start(bf16[2048,128]{1,0:T(8,128)(2,1)} %bitcast.69), channel_id=1, source_target_pairs={{0,128},{128,0},{1,129},{129,1},{2,130},{130,2},{3,131},{131,3},{4... | collective-permute-start | bytes 1572872 | tf_op jit(solution)/shard_map/ppermute | solution.py:54
  0.7 19.2 %collective-permute-start.11 = (bf16[2048,128]{1,0:T(8,128)(2,1)}, bf16[2048,128]{1,0:T(8,128)(2,1)S(1)}, u32[]{:S(2)}, u32[]{:S(2)}) collective-permute-start(bf16[2048,128]{1,0:T(8,128)(2,1)} %bitcast.71), channel_id=1, source_target_pairs={{0,128},{128,0},{1,129},{129,1},{2,130},{130,2},{3,131},{131,3},{4... | collective-permute-start | bytes 1572872 | tf_op jit(solution)/shard_map/ppermute | solution.py:54
  9.8 6.7 %collective-permute-start.7 = (bf16[4,128,128]{2,1,0:T(8,128)(2,1)S(1)}, bf16[4,128,128]{2,1,0:T(8,128)(2,1)S(1)}, u32[]{:S(2)}, u32[]{:S(2)}) collective-permute-start(bf16[4,128,128]{2,1,0:T(8,128)(2,1)S(1)} %pad_maximum_fusion.1.o0), channel_id=1, source_target_pairs={{0,64},{8,72},{16,80},{24,88},{32,96},{40,104},{48,112},{56,120},{... | collective-permute-start | bytes 393224 | tf_op jit(solution)/shard_map/ppermute | solution.py:40
  11.3 8.3 %collective-permute-start.8 = (bf16[4,128,128]{2,1,0:T(8,128)(2,1)S(1)}, bf16[4,128,128]{2,1,0:T(8,128)(2,1)S(1)}, u32[]{:S(2)}, u32[]{:S(2)}) collective-permute-start(bf16[4,128,128]{2,1,0:T(8,128)(2,1)S(1)} %pad_maximum_fusion.1.o0), channel_id=1, source_target_pairs={{0,96},{8,104},{16,112},{24,120},{32,0},{40,8},{48,16},{56,24},{64... | collective-permute-start | bytes 393224 | tf_op jit(solution)/shard_map/ppermute | solution.py:40
  12.7 51.2 %collective-permute-start.20 = (bf16[2048,128]{1,0:T(8,128)(2,1)S(1)}, bf16[2048,128]{1,0:T(8,128)(2,1)S(1)}, u32[]{:S(2)}, u32[]{:S(2)}) collective-permute-start(bf16[2048,128]{1,0:T(8,128)(2,1)S(1)} %bitcast.63), channel_id=1, source_target_pairs={{0,128},{128,0},{1,129},{129,1},{2,130},{130,2},{3,131},{131,3},{4... | collective-permute-start | bytes 1572872 | tf_op jit(solution)/shard_map/ppermute | solution.py:54
  16.5 47.4 %collective-permute-start.21 = (bf16[128,2048]{1,0:T(8,128)(2,1)S(1)}, bf16[128,2048]{1,0:T(8,128)(2,1)S(1)}, u32[]{:S(2)}, u32[]{:S(2)}) collective-permute-start(bf16[128,2048]{1,0:T(8,128)(2,1)S(1)} %bitcast.66), channel_id=1, source_target_pairs={{0,128},{128,0},{1,129},{129,1},{2,130},{130,2},{3,131},{131,3},{4... | collective-permute-start | bytes 1572872 | tf_op jit(solution)/shard_map/ppermute | solution.py:54
  19.5 35.1 %collective-permute-start.3 = (bf16[4,256,128]{2,1,0:T(8,128)(2,1)S(1)}, bf16[4,256,128]{2,1,0:T(8,128)(2,1)S(1)}, u32[]{:S(2)}, u32[]{:S(2)}) collective-permute-start(bf16[4,256,128]{2,1,0:T(8,128)(2,1)S(1)} %slice.8.x0), channel_id=1, source_target_pairs={{0,32},{8,40},{16,48},{24,56},{32,64},{40,72},{48,80},{56,88},{64,... | collective-permute-start | bytes 786440 | tf_op jit(solution)/shard_map/ppermute | solution.py:40
  21.4 7.3 %collective-permute-start.12 = (bf16[128,256]{1,0:T(8,128)(2,1)S(1)}, bf16[128,256]{1,0:T(8,128)(2,1)S(1)}, u32[]{:S(2)}, u32[]{:S(2)}) collective-permute-start(bf16[128,256]{1,0:T(8,128)(2,1)S(1)} %get-tuple-element.17), channel_id=1, source_target_pairs={{0,1},{1,2},{2,3},{3,4},{4,5},{5,6},{6,7},{7,0},{8,9},{9,10},{10,1... | collective-permute-start | bytes 196616 | tf_op jit(solution)/shard_map/ppermute | solution.py:363
  23.1 8.2 %collective-permute-start.13 = (bf16[128,256]{1,0:T(8,128)(2,1)S(1)}, bf16[128,256]{1,0:T(8,128)(2,1)S(1)}, u32[]{:S(2)}, u32[]{:S(2)}) collective-permute-start(bf16[128,256]{1,0:T(8,128)(2,1)S(1)} %get-tuple-element.17), channel_id=1, source_target_pairs={{0,2},{1,3},{2,4},{3,5},{4,6},{5,7},{6,0},{7,1},{8,10},{9,11},{10,... | collective-permute-start | bytes 196616 | tf_op jit(solution)/shard_map/ppermute | solution.py:363
  28.7 7.0 %collective-permute-start.14 = (bf16[128,256]{1,0:T(8,128)(2,1)S(1)}, bf16[128,256]{1,0:T(8,128)(2,1)S(1)}, u32[]{:S(2)}, u32[]{:S(2)}) collective-permute-start(bf16[128,256]{1,0:T(8,128)(2,1)S(1)} %get-tuple-element.17), channel_id=1, source_target_pairs={{0,3},{1,4},{2,5},{3,6},{4,7},{5,0},{6,1},{7,2},{8,11},{9,12},{10,... | collective-permute-start | bytes 196616 | tf_op jit(solution)/shard_map/ppermute | solution.py:363
  31.3 10.7 %collective-permute-start.15 = (bf16[128,256]{1,0:T(8,128)(2,1)S(1)}, bf16[128,256]{1,0:T(8,128)(2,1)S(1)}, u32[]{:S(2)}, u32[]{:S(2)}) collective-permute-start(bf16[128,256]{1,0:T(8,128)(2,1)S(1)} %get-tuple-element.17), channel_id=1, source_target_pairs={{0,4},{1,5},{2,6},{3,7},{4,0},{5,1},{6,2},{7,3},{8,12},{9,13},{10,... | collective-permute-start | bytes 196616 | tf_op jit(solution)/shard_map/ppermute | solution.py:363
  47.4 16.5 %collective-permute-start.19 = (bf16[8,128,256]{2,1,0:T(8,128)(2,1)S(1)}, bf16[8,128,256]{2,1,0:T(8,128)(2,1)S(1)}, u32[]{:S(2)}, u32[]{:S(2)}) collective-permute-start(bf16[8,128,256]{2,1,0:T(8,128)(2,1)S(1)} %bitcast_dynamic-update-slice_fusion.8.kv_same), channel_id=1, source_target_pairs={{0,128},{128,0},{1,129},{129,1},{2,130},{130,2},{3,131},{131,3},{4... | collective-permute-start | bytes 1572872 | tf_op jit(solution)/shard_map/ppermute | solution.py:54
  54.5 6.8 %collective-permute-start.4 = (bf16[4,256,128]{2,1,0:T(8,128)(2,1)S(1)}, bf16[4,256,128]{2,1,0:T(8,128)(2,1)S(1)}, u32[]{:S(2)}, u32[]{:S(2)}) collective-permute-start(bf16[4,256,128]{2,1,0:T(8,128)(2,1)S(1)} %slice.8.x0), channel_id=1, source_target_pairs={{0,64},{8,72},{16,80},{24,88},{32,96},{40,104},{48,112},{56,120},{... | collective-permute-start | bytes 786440 | tf_op jit(solution)/shard_map/ppermute | solution.py:40
  54.6 9.2 %collective-permute-start.5 = (bf16[4,256,128]{2,1,0:T(8,128)(2,1)S(1)}, bf16[4,256,128]{2,1,0:T(8,128)(2,1)S(1)}, u32[]{:S(2)}, u32[]{:S(2)}) collective-permute-start(bf16[4,256,128]{2,1,0:T(8,128)(2,1)S(1)} %slice.8.x0), channel_id=1, source_target_pairs={{0,96},{8,104},{16,112},{24,120},{32,0},{40,8},{48,16},{56,24},{64... | collective-permute-start | bytes 786440 | tf_op jit(solution)/shard_map/ppermute | solution.py:40
  68.6 8.9 %collective-permute-start.31 = (bf16[128,256]{1,0:T(8,128)(2,1)S(1)}, bf16[128,256]{1,0:T(8,128)(2,1)S(1)}, u32[]{:S(2)}, u32[]{:S(2)}) collective-permute-start(bf16[128,256]{1,0:T(8,128)(2,1)S(1)} %get-tuple-element.24), channel_id=1, source_target_pairs={{0,1},{1,2},{2,3},{3,4},{4,5},{5,6},{6,7},{7,0},{8,9},{9,10},{10,1... | collective-permute-start | bytes 196616 | tf_op jit(solution)/shard_map/ppermute | solution.py:363
  68.7 11.7 %collective-permute-start.32 = (bf16[128,256]{1,0:T(8,128)(2,1)S(1)}, bf16[128,256]{1,0:T(8,128)(2,1)S(1)}, u32[]{:S(2)}, u32[]{:S(2)}) collective-permute-start(bf16[128,256]{1,0:T(8,128)(2,1)S(1)} %get-tuple-element.24), channel_id=1, source_target_pairs={{0,2},{1,3},{2,4},{3,5},{4,6},{5,7},{6,0},{7,1},{8,10},{9,11},{10,... | collective-permute-start | bytes 196616 | tf_op jit(solution)/shard_map/ppermute | solution.py:363
  71.1 9.8 %collective-permute-start.33 = (bf16[128,256]{1,0:T(8,128)(2,1)S(1)}, bf16[128,256]{1,0:T(8,128)(2,1)S(1)}, u32[]{:S(2)}, u32[]{:S(2)}) collective-permute-start(bf16[128,256]{1,0:T(8,128)(2,1)S(1)} %get-tuple-element.24), channel_id=1, source_target_pairs={{0,3},{1,4},{2,5},{3,6},{4,7},{5,0},{6,1},{7,2},{8,11},{9,12},{10,... | collective-permute-start | bytes 196616 | tf_op jit(solution)/shard_map/ppermute | solution.py:363
  72.6 11.4 %collective-permute-start.34 = (bf16[128,256]{1,0:T(8,128)(2,1)S(1)}, bf16[128,256]{1,0:T(8,128)(2,1)S(1)}, u32[]{:S(2)}, u32[]{:S(2)}) collective-permute-start(bf16[128,256]{1,0:T(8,128)(2,1)S(1)} %get-tuple-element.24), channel_id=1, source_target_pairs={{0,4},{1,5},{2,6},{3,7},{4,0},{5,1},{6,2},{7,3},{8,12},{9,13},{10,... | collective-permute-start | bytes 196616 | tf_op jit(solution)/shard_map/ppermute | solution.py:363
  74.4 9.6 %collective-permute-start.35 = (bf16[128,256]{1,0:T(8,128)(2,1)S(1)}, bf16[128,256]{1,0:T(8,128)(2,1)S(1)}, u32[]{:S(2)}, u32[]{:S(2)}) collective-permute-start(bf16[128,256]{1,0:T(8,128)(2,1)S(1)} %get-tuple-element.24), channel_id=1, source_target_pairs={{0,5},{1,6},{2,7},{3,0},{4,1},{5,2},{6,3},{7,4},{8,13},{9,14},{10,... | collective-permute-start | bytes 196616 | tf_op jit(solution)/shard_map/ppermute | solution.py:363
  77.5 16.9 %collective-permute-start.36 = (bf16[128,256]{1,0:T(8,128)(2,1)S(1)}, bf16[128,256]{1,0:T(8,128)(2,1)S(1)}, u32[]{:S(2)}, u32[]{:S(2)}) collective-permute-start(bf16[128,256]{1,0:T(8,128)(2,1)S(1)} %get-tuple-element.24), channel_id=1, source_target_pairs={{0,6},{1,7},{2,0},{3,1},{4,2},{5,3},{6,4},{7,5},{8,14},{9,15},{10,... | collective-permute-start | bytes 196616 | tf_op jit(solution)/shard_map/ppermute | solution.py:363
  80.4 8.1 %collective-permute-start.22 = (bf16[4,256,128]{2,1,0:T(8,128)(2,1)S(1)}, bf16[4,256,128]{2,1,0:T(8,128)(2,1)S(1)}, u32[]{:S(2)}, u32[]{:S(2)}) collective-permute-start(bf16[4,256,128]{2,1,0:T(8,128)(2,1)S(1)} %get-tuple-element.20), channel_id=1, source_target_pairs={{0,32},{8,40},{16,48},{24,56},{32,64},{40,72},{48,80},{56,88},{64,... | collective-permute-start | bytes 786440 | tf_op jit(solution)/shard_map/ppermute | solution.py:40
  80.9 7.6 %collective-permute-start.23 = (bf16[4,256,128]{2,1,0:T(8,128)(2,1)S(1)}, bf16[4,256,128]{2,1,0:T(8,128)(2,1)S(1)}, u32[]{:S(2)}, u32[]{:S(2)}) collective-permute-start(bf16[4,256,128]{2,1,0:T(8,128)(2,1)S(1)} %get-tuple-element.21), channel_id=1, source_target_pairs={{0,64},{8,72},{16,80},{24,88},{32,96},{40,104},{48,112},{56,120},{... | collective-permute-start | bytes 786440 | tf_op jit(solution)/shard_map/ppermute | solution.py:40
  84.0 10.4 %collective-permute-start.37 = (bf16[128,256]{1,0:T(8,128)(2,1)S(1)}, bf16[128,256]{1,0:T(8,128)(2,1)S(1)}, u32[]{:S(2)}, u32[]{:S(2)}) collective-permute-start(bf16[128,256]{1,0:T(8,128)(2,1)S(1)} %get-tuple-element.24), channel_id=1, source_target_pairs={{0,7},{1,0},{2,1},{3,2},{4,3},{5,4},{6,5},{7,6},{8,15},{9,8},{10,9... | collective-permute-start | bytes 196616 | tf_op jit(solution)/shard_map/ppermute | solution.py:363
  90.8 7.5 %collective-permute-start.25 = (bf16[4,256,128]{2,1,0:T(8,128)(2,1)S(1)}, bf16[4,256,128]{2,1,0:T(8,128)(2,1)S(1)}, u32[]{:S(2)}, u32[]{:S(2)}) collective-permute-start(bf16[4,256,128]{2,1,0:T(8,128)(2,1)S(1)} %add_convert_fusion.2), channel_id=1, source_target_pairs={{0,8},{8,16},{16,24},{24,0},{32,40},{40,48},{48,56},{56,32},{64,72... | collective-permute-start | bytes 786440 | tf_op jit(solution)/shard_map/ppermute | solution.py:36
  91.7 6.8 %collective-permute-start.26 = (bf16[4,256,128]{2,1,0:T(8,128)(2,1)S(1)}, bf16[4,256,128]{2,1,0:T(8,128)(2,1)S(1)}, u32[]{:S(2)}, u32[]{:S(2)}) collective-permute-start(bf16[4,256,128]{2,1,0:T(8,128)(2,1)S(1)} %add_convert_fusion.2), channel_id=1, source_target_pairs={{0,16},{8,24},{16,0},{24,8},{32,48},{40,56},{48,32},{56,40},{64,80... | collective-permute-start | bytes 786440 | tf_op jit(solution)/shard_map/ppermute | solution.py:36
  93.7 7.8 %collective-permute-start.27 = (bf16[4,256,128]{2,1,0:T(8,128)(2,1)S(1)}, bf16[4,256,128]{2,1,0:T(8,128)(2,1)S(1)}, u32[]{:S(2)}, u32[]{:S(2)}) collective-permute-start(bf16[4,256,128]{2,1,0:T(8,128)(2,1)S(1)} %add_convert_fusion.2), channel_id=1, source_target_pairs={{0,24},{8,0},{16,8},{24,16},{32,56},{40,32},{48,40},{56,48},{64,88... | collective-permute-start | bytes 786440 | tf_op jit(solution)/shard_map/ppermute | solution.py:36
  94.4 9.7 %collective-permute-start.38 = (bf16[8,128,256]{2,1,0:T(8,128)(2,1)S(1)}, bf16[8,128,256]{2,1,0:T(8,128)(2,1)S(1)}, u32[]{:S(2)}, u32[]{:S(2)}) collective-permute-start(bf16[8,128,256]{2,1,0:T(8,128)(2,1)S(1)} %bitcast_dynamic-update-slice_fusion.kv_same), channel_id=1, source_target_pairs={{0,128},{128,0},{1,129},{129,1},{2,130},{130,2},{3,131},{131,3},{4... | collective-permute-start | bytes 1572872 | tf_op jit(solution)/shard_map/ppermute | solution.py:54
  102.2 6.8 %collective-permute-start.29 = (bf16[4,256,128]{2,1,0:T(8,128)(2,1)S(1)}, bf16[4,256,128]{2,1,0:T(8,128)(2,1)S(1)}, u32[]{:S(2)}, u32[]{:S(2)}) collective-permute-start(bf16[4,256,128]{2,1,0:T(8,128)(2,1)S(1)} %add_convert_fusion.1.x0), channel_id=1, source_target_pairs={{0,64},{8,72},{16,80},{24,88},{32,96},{40,104},{48,112},{56,120},{... | collective-permute-start | bytes 786440 | tf_op jit(solution)/shard_map/ppermute | solution.py:40
  103.5 8.4 %collective-permute-start.30 = (bf16[4,256,128]{2,1,0:T(8,128)(2,1)S(1)}, bf16[4,256,128]{2,1,0:T(8,128)(2,1)S(1)}, u32[]{:S(2)}, u32[]{:S(2)}) collective-permute-start(bf16[4,256,128]{2,1,0:T(8,128)(2,1)S(1)} %add_convert_fusion.1.x0), channel_id=1, source_target_pairs={{0,96},{8,104},{16,112},{24,120},{32,0},{40,8},{48,16},{56,24},{64... | collective-permute-start | bytes 786440 | tf_op jit(solution)/shard_map/ppermute | solution.py:40
  117.6 6.8 %collective-permute-start.40 = (bf16[4,256,128]{2,1,0:T(8,128)(2,1)S(1)}, bf16[4,256,128]{2,1,0:T(8,128)(2,1)S(1)}, u32[]{:S(2)}, u32[]{:S(2)}) collective-permute-start(bf16[4,256,128]{2,1,0:T(8,128)(2,1)S(1)} %get-tuple-element.27), channel_id=1, source_target_pairs={{0,64},{8,72},{16,80},{24,88},{32,96},{40,104},{48,112},{56,120},{... | collective-permute-start | bytes 786440 | tf_op jit(solution)/shard_map/ppermute | solution.py:40
  119.4 7.7 %collective-permute-start.41 = (bf16[4,256,128]{2,1,0:T(8,128)(2,1)S(1)}, bf16[4,256,128]{2,1,0:T(8,128)(2,1)S(1)}, u32[]{:S(2)}, u32[]{:S(2)}) collective-permute-start(bf16[4,256,128]{2,1,0:T(8,128)(2,1)S(1)} %get-tuple-element.28), channel_id=1, source_target_pairs={{0,96},{8,104},{16,112},{24,120},{32,0},{40,8},{48,16},{56,24},{64... | collective-permute-start | bytes 786440 | tf_op jit(solution)/shard_map/ppermute | solution.py:40
  134.2 12.3 %collective-permute-start.45 = (bf16[256,128]{1,0:T(8,128)(2,1)S(1)}, bf16[256,128]{1,0:T(8,128)(2,1)S(1)}, u32[]{:S(2)}, u32[]{:S(2)}) collective-permute-start(bf16[256,128]{1,0:T(8,128)(2,1)S(1)} %get-tuple-element.29), channel_id=1, source_target_pairs={{0,128},{128,0},{1,129},{129,1},{2,130},{130,2},{3,131},{131,3},{4... | collective-permute-start | bytes 196616 | tf_op jit(solution)/shard_map/ppermute | solution.py:54
  (25 other events, 171.6 us)

commit v5 on v4

--- a/solution.py
+++ b/solution.py
@@ -138,16 +138,15 @@
     gain_mine,
     gain_theirs,
     key_mine,
-    key_theirs,
     value_mine,
-    value_theirs,
+    theirs,
     out_zero,
     out_one,
     normed,
     weight,
     sems,
 ):
-    sources = ((key_mine, value_mine), (key_theirs, value_theirs))
+    sources = ((key_mine, value_mine), (theirs.at[0], theirs.at[1]))
     copies = [
         pltpu.make_async_copy(
             source, weight.at[whose, :, half * HS : (half + 1) * HS], sems.at[whose * 2 + half]
@@ -205,7 +204,7 @@
     core, near_at, far_at, near_stride, far_stride = where
     place = lax.axis_index("patch")
     patch_count = kv_same.shape[0]
-    fetch(core, section, query_mine, query_theirs, w_query, sems.at[0], start)
+    fetch(core, section, query_mine, query_theirs.at[2], w_query, sems.at[0], start)
     fetch(core, section, out_mine, out_theirs, w_out, sems.at[1], start)
     chosen_gain(core, section, gain_mine, gain_theirs, 0, gain)
     normed_into(placed(where, section == 0), (x0, x1, x2, x3), (gain,), (normed,))
@@ -215,15 +214,14 @@
         def _(part):
             kept[part] = x0[wrapped(near_at - part)]
 
-    fetch(core, section, query_mine, query_theirs, w_query, sems.at[0], wait)
+    fetch(core, section, query_mine, query_theirs.at[2], w_query, sems.at[0], wait)
     context[...] = (
         jnp.dot(normed[...], w_query[...], preferred_element_type=jnp.float32) * HS ** (-0.5)
     ).astype(jnp.bfloat16)
     blocks_here = rows // BLK
 
-    @pl.loop(0, blocks_here)
-    def _(block):
-        here = pl.ds(pl.multiple_of(block * BLK, BLK), BLK)
+    for block in range(blocks_here):
+        here = slice(block * BLK, (block + 1) * BLK)
         query = context[here, :]
         row = core * blocks_here + block
         live = counts[row]
@@ -268,13 +266,13 @@
             out[part] = normed[:, tile_cols(block)]
 
 
-def key_values(pieces, gains, w_key, w_value):
+def key_values(pieces, gains, weights):
     rows = pieces[0].shape[1]
-    features = w_key[0].shape[0]
+    features = weights[0].shape[0]
     return pl.pallas_call(
         key_value_kernel,
         out_shape=[jax.ShapeDtypeStruct((rows, 2 * HS), jnp.bfloat16)] * 2,
-        in_specs=[VMEM] * 6 + [ANY] * 4,
+        in_specs=[VMEM] * 6 + [ANY] * 3,
         out_specs=[VMEM] * 2,
         scratch_shapes=[
             pltpu.VMEM((2, rows, features), jnp.bfloat16),
@@ -286,7 +284,7 @@
         ),
         compiler_params=pltpu.CompilerParams(vmem_limit_bytes=12 << 20),
         name="key_values",
-    )(*pieces, *gains, *w_key, *w_value)
+    )(*pieces, *gains, *weights)
 
 
 def attend(section, lists, pieces, kv, gains, w_query, w_out):
@@ -349,14 +347,15 @@
     obs_group, patch_group = group[:, :obs_rows], group[:, obs_rows:]
 
     gains = jnp.concatenate([patch_gain, obs_gain], axis=0).reshape(2, SIDE * SIDE, HS)
-    gains, keys, values = [(mine, swapped(mine)) for mine in (gains, w_key[0], w_value[0])]
-    queries, outs = [(mine, swapped(mine)) for mine in (w_query[0], w_out[0])]
+    gains = (gains, swapped(gains))
+    theirs = swapped(jnp.stack([w_key[0], w_value[0], w_query[0]]))
+    outs = (w_out[0], swapped(w_out[0]))
 
     obs_far = {}
     for step in AROUND:
         obs_far[step] = far(obs_group, step)
     obs_pieces = [obs_group] + [obs_far[step] for step in range(1, SIDE)]
-    kv_first, kv_second = key_values(obs_pieces, gains, keys, values)
+    kv_first, kv_second = key_values(obs_pieces, gains, (w_key[0], w_value[0], theirs))
 
     def to_patch(value, steps):
         return {
@@ -375,10 +374,10 @@
         arrived = {step: far(parts[step], step) for step in AROUND}
         return added(parts[0], [arrived[step] for step in range(1, SIDE)]).astype(jnp.bfloat16)
 
-    *parts, kept = attend(0, lists, patch_pieces, kv_zero, gains, queries, outs)
+    *parts, kept = attend(0, lists, patch_pieces, kv_zero, gains, (w_query[0], theirs), outs)
     kv_second, _ = lax.optimization_barrier((kv_second, kept))
-    arrived = to_patch(kv_second, (1, 7)) | to_patch(kv_second, (4, 3, 5))
-    arrived |= to_patch(kv_second, (2, 6))
+    arrived = to_patch(kv_second, (2, 6, 1, 7))
+    arrived |= to_patch(kv_second, (4, 3, 5))
     same = jnp.stack([kv_second] + [arrived[step] for step in range(1, patch_count)])
     kv_one = (same, swapped(same))
 
@@ -387,7 +386,7 @@
     after_zero = (kept.astype(jnp.float32) + added(first, others)).astype(jnp.bfloat16)
 
     pieces = all_far(after_zero)
-    *parts, _ = attend(1, lists, pieces, kv_one, gains, queries, outs)
+    *parts, _ = attend(1, lists, pieces, kv_one, gains, (w_query[0], theirs), outs)
     total = reduced(parts)
     own_zero = lax.dynamic_index_in_dim(after_zero, near_at, 0, keepdims=False)
     own_total = lax.dynamic_index_in_dim(total, near_at, 0, keepdims=False)

time: 147 us -> 139 us (0.946)
  the two profiles are of different devices: /device:TPU:15 before, /device:TPU:2 now
where the time goes in v5:
time: 139 us; the launch traced here: 137 us
  starting transfers between devices  71.7 us (52%)
  waiting for transfers between devices  49.7 us (36%)
  Pallas kernels  10.7 us (8%)
  other arithmetic  4.13 us (3%)
    ppermute x14, starting transfers between devices, to_patch(): lax.ppermute(value, 'patch', [(at, (at + step) % patch_count) for at in r...  33.4 us
    ppermute x15, waiting for transfers between devices, far(): return lax.ppermute(value, ('pipe', 'obs'), square_shift(False, step))  28.8 us
    ppermute x15, starting transfers between devices, far(): return lax.ppermute(value, ('pipe', 'obs'), square_shift(False, step))  23.5 us
    ppermute x9, starting transfers between devices, near(): return lax.ppermute(value, ('pipe', 'obs'), square_shift(True, step))  14.3 us
    ppermute x9, waiting for transfers between devices, near(): return lax.ppermute(value, ('pipe', 'obs'), square_shift(True, step))  13.2 us
    pallas_call x2, Pallas kernels, attend(): pl.pallas_call(functools.partial(attend_kernel, section), out_shape=[piec...  9.19 us
    ppermute x14, waiting for transfers between devices, to_patch(): lax.ppermute(value, 'patch', [(at, (at + step) % patch_count) for at in r...  5.23 us
    another operation x1, other arithmetic, on_device(): theirs = swapped(jnp.stack([w_key[0], w_value[0], w_query[0]]))  2.83 us
  transfers between devices with their start and end apart: 44, of which 26 were waited for; matrix products, arithmetic and copies ran while one was open for 0% of the time, Pallas kernels for 1%

profile of v5, /device:TPU:2, one launch (start us, length us, event | category | flops | bytes accessed | tf_op | source)
XLA Modules:
  0.0 136.8 jit_solution(1609762146867708262)
XLA Ops:
  0.1 2.8 %pad_maximum_fusion = bf16[3,2048,128]{2,1,0:T(8,128)(2,1)} fusion(bf16[1,2048,128]{2,1,0:T(8,128)(2,1)} %param.16, bf16[1,2048,128]{2,1,0:T(8,128)(2,1)} %param.18, bf16[1,2048,128]{2,1,0:T(8,128)(2,1)} %param.17), kind=kLoop, calls=%fused_computation | loop fusion | flops 1572864 | bytes 3145728 | tf_op jit(solution)/shard_map/stack | solution.py:351
  4.5 2.8 %collective-permute-start.1 = (bf16[384,128]{1,0:T(8,128)(2,1)S(1)}, bf16[384,128]{1,0:T(8,128)(2,1)S(1)}, u32[]{:S(2)}, u32[]{:S(2)}) collective-permute-start(bf16[384,128]{1,0:T(8,128)(2,1)S(1)} %get-tuple-element.35), channel_id=1, source_target_pairs={{0,16},{8,24},{16,0},{24,8},{32,48},{40,56},{48,32},{56,40},{64,80... | collective-permute-start | bytes 294920 | tf_op jit(solution)/shard_map/ppermute | solution.py:36
  7.9 2.8 %collective-permute-done.1 = bf16[384,128]{1,0:T(8,128)(2,1)S(1)} collective-permute-done((bf16[384,128]{1,0:T(8,128)(2,1)S(1)}, bf16[384,128]{1,0:T(8,128)(2,1)S(1)}, u32[]{:S(2)}, u32[]{:S(2)}) %collective-permute-start.1) | collective-permute-done | bytes 98336 | tf_op jit(solution)/shard_map/ppermute | solution.py:36
  13.0 2.9 %collective-permute-start.7 = (bf16[4,128,128]{2,1,0:T(8,128)(2,1)S(1)}, bf16[4,128,128]{2,1,0:T(8,128)(2,1)S(1)}, u32[]{:S(2)}, u32[]{:S(2)}) collective-permute-start(bf16[4,128,128]{2,1,0:T(8,128)(2,1)S(1)} %pad_maximum_fusion.2.o0), channel_id=1, source_target_pairs={{0,64},{8,72},{16,80},{24,88},{32,96},{40,104},{48,112},{56,120},{... | collective-permute-start | bytes 393224 | tf_op jit(solution)/shard_map/ppermute | solution.py:40
  22.4 2.0 %collective-permute-start.11 = (bf16[128,256]{1,0:T(8,128)(2,1)S(1)}, bf16[128,256]{1,0:T(8,128)(2,1)S(1)}, u32[]{:S(2)}, u32[]{:S(2)}) collective-permute-start(bf16[128,256]{1,0:T(8,128)(2,1)S(1)} %get-tuple-element.17), channel_id=1, source_target_pairs={{0,1},{1,2},{2,3},{3,4},{4,5},{5,6},{6,7},{7,0},{8,9},{9,10},{10,1... | collective-permute-start | bytes 196616 | tf_op jit(solution)/shard_map/ppermute | solution.py:362
  24.4 3.3 %collective-permute-start.12 = (bf16[128,256]{1,0:T(8,128)(2,1)S(1)}, bf16[128,256]{1,0:T(8,128)(2,1)S(1)}, u32[]{:S(2)}, u32[]{:S(2)}) collective-permute-start(bf16[128,256]{1,0:T(8,128)(2,1)S(1)} %get-tuple-element.17), channel_id=1, source_target_pairs={{0,2},{1,3},{2,4},{3,5},{4,6},{5,7},{6,0},{7,1},{8,10},{9,11},{10,... | collective-permute-start | bytes 196616 | tf_op jit(solution)/shard_map/ppermute | solution.py:362
  27.7 4.0 %collective-permute-start.13 = (bf16[128,256]{1,0:T(8,128)(2,1)S(1)}, bf16[128,256]{1,0:T(8,128)(2,1)S(1)}, u32[]{:S(2)}, u32[]{:S(2)}) collective-permute-start(bf16[128,256]{1,0:T(8,128)(2,1)S(1)} %get-tuple-element.17), channel_id=1, source_target_pairs={{0,3},{1,4},{2,5},{3,6},{4,7},{5,0},{6,1},{7,2},{8,11},{9,12},{10,... | collective-permute-start | bytes 196616 | tf_op jit(solution)/shard_map/ppermute | solution.py:362
  32.2 5.0 %collective-permute-start.15 = (bf16[128,256]{1,0:T(8,128)(2,1)S(1)}, bf16[128,256]{1,0:T(8,128)(2,1)S(1)}, u32[]{:S(2)}, u32[]{:S(2)}) collective-permute-start(bf16[128,256]{1,0:T(8,128)(2,1)S(1)} %get-tuple-element.17), channel_id=1, source_target_pairs={{0,5},{1,6},{2,7},{3,0},{4,1},{5,2},{6,3},{7,4},{8,13},{9,14},{10,... | collective-permute-start | bytes 196616 | tf_op jit(solution)/shard_map/ppermute | solution.py:362
  41.3 2.4 %collective-permute-done.15 = bf16[128,256]{1,0:T(8,128)(2,1)S(1)} collective-permute-done((bf16[128,256]{1,0:T(8,128)(2,1)S(1)}, bf16[128,256]{1,0:T(8,128)(2,1)S(1)}, u32[]{:S(2)}, u32[]{:S(2)}) %collective-permute-start.15) | collective-permute-done | bytes 65568 | tf_op jit(solution)/shard_map/ppermute | solution.py:362
  43.7 2.0 %collective-permute-done.16 = bf16[128,256]{1,0:T(8,128)(2,1)S(1)} collective-permute-done((bf16[128,256]{1,0:T(8,128)(2,1)S(1)}, bf16[128,256]{1,0:T(8,128)(2,1)S(1)}, u32[]{:S(2)}, u32[]{:S(2)}) %collective-permute-start.16) | collective-permute-done | bytes 65568 | tf_op jit(solution)/shard_map/ppermute | solution.py:362
  46.7 2.9 %collective-permute-start.4 = (bf16[4,256,128]{2,1,0:T(8,128)(2,1)S(1)}, bf16[4,256,128]{2,1,0:T(8,128)(2,1)S(1)}, u32[]{:S(2)}, u32[]{:S(2)}) collective-permute-start(bf16[4,256,128]{2,1,0:T(8,128)(2,1)S(1)} %slice.8.x0), channel_id=1, source_target_pairs={{0,64},{8,72},{16,80},{24,88},{32,96},{40,104},{48,112},{56,120},{... | collective-permute-start | bytes 786440 | tf_op jit(solution)/shard_map/ppermute | solution.py:40
  50.3 3.3 %collective-permute-done.3.x1 = bf16[4,256,128]{2,1,0:T(8,128)(2,1)S(1)} collective-permute-done((bf16[4,256,128]{2,1,0:T(8,128)(2,1)S(1)}, bf16[4,256,128]{2,1,0:T(8,128)(2,1)S(1)}, u32[]{:S(2)}, u32[]{:S(2)}) %collective-permute-start.3) | collective-permute-done | bytes 262176 | tf_op jit(solution)/shard_map/ppermute | solution.py:40
  53.5 3.2 %collective-permute-done.4.x2 = bf16[4,256,128]{2,1,0:T(8,128)(2,1)S(1)} collective-permute-done((bf16[4,256,128]{2,1,0:T(8,128)(2,1)S(1)}, bf16[4,256,128]{2,1,0:T(8,128)(2,1)S(1)}, u32[]{:S(2)}, u32[]{:S(2)}) %collective-permute-start.4) | collective-permute-done | bytes 262176 | tf_op jit(solution)/shard_map/ppermute | solution.py:40
  57.3 4.4 %attend.2 = (bf16[4,256,128]{2,1,0:T(8,128)(2,1)S(1)}, bf16[4,256,128]{2,1,0:T(8,128)(2,1)S(1)}, bf16[4,256,128]{2,1,0:T(8,128)(2,1)S(1)}, bf16[4,256,128]{2,1,0:T(8,128)(2,1)S(1)}, bf16[4,256,128]{2,1,0:T(8,128)(2,1)S(1)}) custom-call(s32[4,8]{1,0:T(4,128)S(1)} %copy-done.5, s32[4]{0:T(128)S(1)} %copy-done.7, f32[4,8]{1,0:T(4,128)S(1)} %copy-done.6, ...), custom_call_target="tpu_custom_call" | custom-call | flops 536870912 | bytes 4194304 | tf_op jit(solution)/shard_map/attend/pallas_call | solution.py:295
  62.9 2.0 %collective-permute-start.30 = (bf16[128,256]{1,0:T(8,128)(2,1)S(1)}, bf16[128,256]{1,0:T(8,128)(2,1)S(1)}, u32[]{:S(2)}, u32[]{:S(2)}) collective-permute-start(bf16[128,256]{1,0:T(8,128)(2,1)S(1)} %get-tuple-element.24), channel_id=1, source_target_pairs={{0,2},{1,3},{2,4},{3,5},{4,6},{5,7},{6,0},{7,1},{8,10},{9,11},{10,... | collective-permute-start | bytes 196616 | tf_op jit(solution)/shard_map/ppermute | solution.py:362
  64.9 2.6 %collective-permute-start.31 = (bf16[128,256]{1,0:T(8,128)(2,1)S(1)}, bf16[128,256]{1,0:T(8,128)(2,1)S(1)}, u32[]{:S(2)}, u32[]{:S(2)}) collective-permute-start(bf16[128,256]{1,0:T(8,128)(2,1)S(1)} %get-tuple-element.24), channel_id=1, source_target_pairs={{0,3},{1,4},{2,5},{3,6},{4,7},{5,0},{6,1},{7,2},{8,11},{9,12},{10,... | collective-permute-start | bytes 196616 | tf_op jit(solution)/shard_map/ppermute | solution.py:362
  67.5 2.4 %collective-permute-start.32 = (bf16[128,256]{1,0:T(8,128)(2,1)S(1)}, bf16[128,256]{1,0:T(8,128)(2,1)S(1)}, u32[]{:S(2)}, u32[]{:S(2)}) collective-permute-start(bf16[128,256]{1,0:T(8,128)(2,1)S(1)} %get-tuple-element.24), channel_id=1, source_target_pairs={{0,4},{1,5},{2,6},{3,7},{4,0},{5,1},{6,2},{7,3},{8,12},{9,13},{10,... | collective-permute-start | bytes 196616 | tf_op jit(solution)/shard_map/ppermute | solution.py:362
  69.9 3.3 %collective-permute-start.33 = (bf16[128,256]{1,0:T(8,128)(2,1)S(1)}, bf16[128,256]{1,0:T(8,128)(2,1)S(1)}, u32[]{:S(2)}, u32[]{:S(2)}) collective-permute-start(bf16[128,256]{1,0:T(8,128)(2,1)S(1)} %get-tuple-element.24), channel_id=1, source_target_pairs={{0,5},{1,6},{2,7},{3,0},{4,1},{5,2},{6,3},{7,4},{8,13},{9,14},{10,... | collective-permute-start | bytes 196616 | tf_op jit(solution)/shard_map/ppermute | solution.py:362
  75.8 3.1 %collective-permute-start.21 = (bf16[4,256,128]{2,1,0:T(8,128)(2,1)S(1)}, bf16[4,256,128]{2,1,0:T(8,128)(2,1)S(1)}, u32[]{:S(2)}, u32[]{:S(2)}) collective-permute-start(bf16[4,256,128]{2,1,0:T(8,128)(2,1)S(1)} %get-tuple-element.21), channel_id=1, source_target_pairs={{0,64},{8,72},{16,80},{24,88},{32,96},{40,104},{48,112},{56,120},{... | collective-permute-start | bytes 786440 | tf_op jit(solution)/shard_map/ppermute | solution.py:40
  80.0 2.3 %collective-permute-start.35 = (bf16[128,256]{1,0:T(8,128)(2,1)S(1)}, bf16[128,256]{1,0:T(8,128)(2,1)S(1)}, u32[]{:S(2)}, u32[]{:S(2)}) collective-permute-start(bf16[128,256]{1,0:T(8,128)(2,1)S(1)} %get-tuple-element.24), channel_id=1, source_target_pairs={{0,7},{1,0},{2,1},{3,2},{4,3},{5,4},{6,5},{7,6},{8,15},{9,8},{10,9... | collective-permute-start | bytes 196616 | tf_op jit(solution)/shard_map/ppermute | solution.py:362
  82.4 3.7 %collective-permute-done.21 = bf16[4,256,128]{2,1,0:T(8,128)(2,1)S(1)} collective-permute-done((bf16[4,256,128]{2,1,0:T(8,128)(2,1)S(1)}, bf16[4,256,128]{2,1,0:T(8,128)(2,1)S(1)}, u32[]{:S(2)}, u32[]{:S(2)}) %collective-permute-start.21) | collective-permute-done | bytes 262176 | tf_op jit(solution)/shard_map/ppermute | solution.py:40
  87.5 2.3 %collective-permute-start.24 = (bf16[4,256,128]{2,1,0:T(8,128)(2,1)S(1)}, bf16[4,256,128]{2,1,0:T(8,128)(2,1)S(1)}, u32[]{:S(2)}, u32[]{:S(2)}) collective-permute-start(bf16[4,256,128]{2,1,0:T(8,128)(2,1)S(1)} %add_convert_fusion.2), channel_id=1, source_target_pairs={{0,16},{8,24},{16,0},{24,8},{32,48},{40,56},{48,32},{56,40},{64,80... | collective-permute-start | bytes 786440 | tf_op jit(solution)/shard_map/ppermute | solution.py:36
  89.8 2.0 %collective-permute-start.25 = (bf16[4,256,128]{2,1,0:T(8,128)(2,1)S(1)}, bf16[4,256,128]{2,1,0:T(8,128)(2,1)S(1)}, u32[]{:S(2)}, u32[]{:S(2)}) collective-permute-start(bf16[4,256,128]{2,1,0:T(8,128)(2,1)S(1)} %add_convert_fusion.2), channel_id=1, source_target_pairs={{0,24},{8,0},{16,8},{24,16},{32,56},{40,32},{48,40},{56,48},{64,88... | collective-permute-start | bytes 786440 | tf_op jit(solution)/shard_map/ppermute | solution.py:36
  92.9 2.6 %collective-permute-done.24 = bf16[4,256,128]{2,1,0:T(8,128)(2,1)S(1)} collective-permute-done((bf16[4,256,128]{2,1,0:T(8,128)(2,1)S(1)}, bf16[4,256,128]{2,1,0:T(8,128)(2,1)S(1)}, u32[]{:S(2)}, u32[]{:S(2)}) %collective-permute-start.24) | collective-permute-done | bytes 262176 | tf_op jit(solution)/shard_map/ppermute | solution.py:36
  95.5 2.8 %collective-permute-done.25 = bf16[4,256,128]{2,1,0:T(8,128)(2,1)S(1)} collective-permute-done((bf16[4,256,128]{2,1,0:T(8,128)(2,1)S(1)}, bf16[4,256,128]{2,1,0:T(8,128)(2,1)S(1)}, u32[]{:S(2)}, u32[]{:S(2)}) %collective-permute-start.25) | collective-permute-done | bytes 262176 | tf_op jit(solution)/shard_map/ppermute | solution.py:36
  99.9 3.3 %collective-permute-start.27 = (bf16[4,256,128]{2,1,0:T(8,128)(2,1)S(1)}, bf16[4,256,128]{2,1,0:T(8,128)(2,1)S(1)}, u32[]{:S(2)}, u32[]{:S(2)}) collective-permute-start(bf16[4,256,128]{2,1,0:T(8,128)(2,1)S(1)} %add_convert_fusion.1.x0), channel_id=1, source_target_pairs={{0,64},{8,72},{16,80},{24,88},{32,96},{40,104},{48,112},{56,120},{... | collective-permute-start | bytes 786440 | tf_op jit(solution)/shard_map/ppermute | solution.py:40
  103.2 3.0 %collective-permute-done.26.x1 = bf16[4,256,128]{2,1,0:T(8,128)(2,1)S(1)} collective-permute-done((bf16[4,256,128]{2,1,0:T(8,128)(2,1)S(1)}, bf16[4,256,128]{2,1,0:T(8,128)(2,1)S(1)}, u32[]{:S(2)}, u32[]{:S(2)}) %collective-permute-start.26) | collective-permute-done | bytes 262176 | tf_op jit(solution)/shard_map/ppermute | solution.py:40
  106.2 4.1 %collective-permute-done.27.x2 = bf16[4,256,128]{2,1,0:T(8,128)(2,1)S(1)} collective-permute-done((bf16[4,256,128]{2,1,0:T(8,128)(2,1)S(1)}, bf16[4,256,128]{2,1,0:T(8,128)(2,1)S(1)}, u32[]{:S(2)}, u32[]{:S(2)}) %collective-permute-start.27) | collective-permute-done | bytes 262176 | tf_op jit(solution)/shard_map/ppermute | solution.py:40
  110.3 4.8 %attend.3 = (bf16[4,256,128]{2,1,0:T(8,128)(2,1)S(1)}, bf16[4,256,128]{2,1,0:T(8,128)(2,1)S(1)}, bf16[4,256,128]{2,1,0:T(8,128)(2,1)S(1)}, bf16[4,256,128]{2,1,0:T(8,128)(2,1)S(1)}, bf16[8,128]{1,0:T(8,128)(2,1)}) custom-call(s32[4,8]{1,0:T(4,128)S(1)} %copy-done.5, s32[4]{0:T(128)S(1)} %copy-done.7, f32[4,8]{1,0:T(4,128)S(1)} %copy-done.6, ...), custom_call_target="tpu_custom_call" | custom-call | flops 536870912 | bytes 4194304 | tf_op jit(solution)/shard_map/attend/pallas_call | solution.py:295
  115.9 3.0 %collective-permute-start.38 = (bf16[4,256,128]{2,1,0:T(8,128)(2,1)S(1)}, bf16[4,256,128]{2,1,0:T(8,128)(2,1)S(1)}, u32[]{:S(2)}, u32[]{:S(2)}) collective-permute-start(bf16[4,256,128]{2,1,0:T(8,128)(2,1)S(1)} %get-tuple-element.27), channel_id=1, source_target_pairs={{0,64},{8,72},{16,80},{24,88},{32,96},{40,104},{48,112},{56,120},{... | collective-permute-start | bytes 786440 | tf_op jit(solution)/shard_map/ppermute | solution.py:40
  119.2 3.6 %collective-permute-done.37 = bf16[4,256,128]{2,1,0:T(8,128)(2,1)S(1)} collective-permute-done((bf16[4,256,128]{2,1,0:T(8,128)(2,1)S(1)}, bf16[4,256,128]{2,1,0:T(8,128)(2,1)S(1)}, u32[]{:S(2)}, u32[]{:S(2)}) %collective-permute-start.37) | collective-permute-done | bytes 262176 | tf_op jit(solution)/shard_map/ppermute | solution.py:40
  122.8 4.6 %collective-permute-done.38 = bf16[4,256,128]{2,1,0:T(8,128)(2,1)S(1)} collective-permute-done((bf16[4,256,128]{2,1,0:T(8,128)(2,1)S(1)}, bf16[4,256,128]{2,1,0:T(8,128)(2,1)S(1)}, u32[]{:S(2)}, u32[]{:S(2)}) %collective-permute-start.38) | collective-permute-done | bytes 262176 | tf_op jit(solution)/shard_map/ppermute | solution.py:40
  (113 shorter events, 37.1 us)
Async XLA Ops:
  2.9 18.0 %collective-permute-start.10 = (bf16[3,2048,128]{2,1,0:T(8,128)(2,1)}, bf16[3,2048,128]{2,1,0:T(8,128)(2,1)S(1)}, u32[]{:S(2)}, u32[]{:S(2)}) collective-permute-start(bf16[3,2048,128]{2,1,0:T(8,128)(2,1)} %pad_maximum_fusion), channel_id=1, source_target_pairs={{0,128},{128,0},{1,129},{129,1},{2,130},{130,2},{3,131},{131,3},{4... | collective-permute-start | bytes 4718600 | tf_op jit(solution)/shard_map/ppermute | solution.py:54
  13.0 7.2 %collective-permute-start.7 = (bf16[4,128,128]{2,1,0:T(8,128)(2,1)S(1)}, bf16[4,128,128]{2,1,0:T(8,128)(2,1)S(1)}, u32[]{:S(2)}, u32[]{:S(2)}) collective-permute-start(bf16[4,128,128]{2,1,0:T(8,128)(2,1)S(1)} %pad_maximum_fusion.2.o0), channel_id=1, source_target_pairs={{0,64},{8,72},{16,80},{24,88},{32,96},{40,104},{48,112},{56,120},{... | collective-permute-start | bytes 393224 | tf_op jit(solution)/shard_map/ppermute | solution.py:40
  18.5 38.7 %collective-permute-start.19 = (bf16[128,2048]{1,0:T(8,128)(2,1)S(1)}, bf16[128,2048]{1,0:T(8,128)(2,1)S(1)}, u32[]{:S(2)}, u32[]{:S(2)}) collective-permute-start(bf16[128,2048]{1,0:T(8,128)(2,1)S(1)} %bitcast.65), channel_id=1, source_target_pairs={{0,128},{128,0},{1,129},{129,1},{2,130},{130,2},{3,131},{131,3},{4... | collective-permute-start | bytes 1572872 | tf_op jit(solution)/shard_map/ppermute | solution.py:54
  22.4 9.8 %collective-permute-start.11 = (bf16[128,256]{1,0:T(8,128)(2,1)S(1)}, bf16[128,256]{1,0:T(8,128)(2,1)S(1)}, u32[]{:S(2)}, u32[]{:S(2)}) collective-permute-start(bf16[128,256]{1,0:T(8,128)(2,1)S(1)} %get-tuple-element.17), channel_id=1, source_target_pairs={{0,1},{1,2},{2,3},{3,4},{4,5},{5,6},{6,7},{7,0},{8,9},{9,10},{10,1... | collective-permute-start | bytes 196616 | tf_op jit(solution)/shard_map/ppermute | solution.py:362
  24.4 13.6 %collective-permute-start.12 = (bf16[128,256]{1,0:T(8,128)(2,1)S(1)}, bf16[128,256]{1,0:T(8,128)(2,1)S(1)}, u32[]{:S(2)}, u32[]{:S(2)}) collective-permute-start(bf16[128,256]{1,0:T(8,128)(2,1)S(1)} %get-tuple-element.17), channel_id=1, source_target_pairs={{0,2},{1,3},{2,4},{3,5},{4,6},{5,7},{6,0},{7,1},{8,10},{9,11},{10,... | collective-permute-start | bytes 196616 | tf_op jit(solution)/shard_map/ppermute | solution.py:362
  27.7 12.3 %collective-permute-start.13 = (bf16[128,256]{1,0:T(8,128)(2,1)S(1)}, bf16[128,256]{1,0:T(8,128)(2,1)S(1)}, u32[]{:S(2)}, u32[]{:S(2)}) collective-permute-start(bf16[128,256]{1,0:T(8,128)(2,1)S(1)} %get-tuple-element.17), channel_id=1, source_target_pairs={{0,3},{1,4},{2,5},{3,6},{4,7},{5,0},{6,1},{7,2},{8,11},{9,12},{10,... | collective-permute-start | bytes 196616 | tf_op jit(solution)/shard_map/ppermute | solution.py:362
  31.7 9.5 %collective-permute-start.14 = (bf16[128,256]{1,0:T(8,128)(2,1)S(1)}, bf16[128,256]{1,0:T(8,128)(2,1)S(1)}, u32[]{:S(2)}, u32[]{:S(2)}) collective-permute-start(bf16[128,256]{1,0:T(8,128)(2,1)S(1)} %get-tuple-element.17), channel_id=1, source_target_pairs={{0,4},{1,5},{2,6},{3,7},{4,0},{5,1},{6,2},{7,3},{8,12},{9,13},{10,... | collective-permute-start | bytes 196616 | tf_op jit(solution)/shard_map/ppermute | solution.py:362
  32.2 11.4 %collective-permute-start.15 = (bf16[128,256]{1,0:T(8,128)(2,1)S(1)}, bf16[128,256]{1,0:T(8,128)(2,1)S(1)}, u32[]{:S(2)}, u32[]{:S(2)}) collective-permute-start(bf16[128,256]{1,0:T(8,128)(2,1)S(1)} %get-tuple-element.17), channel_id=1, source_target_pairs={{0,5},{1,6},{2,7},{3,0},{4,1},{5,2},{6,3},{7,4},{8,13},{9,14},{10,... | collective-permute-start | bytes 196616 | tf_op jit(solution)/shard_map/ppermute | solution.py:362
  38.0 7.7 %collective-permute-start.16 = (bf16[128,256]{1,0:T(8,128)(2,1)S(1)}, bf16[128,256]{1,0:T(8,128)(2,1)S(1)}, u32[]{:S(2)}, u32[]{:S(2)}) collective-permute-start(bf16[128,256]{1,0:T(8,128)(2,1)S(1)} %get-tuple-element.17), channel_id=1, source_target_pairs={{0,6},{1,7},{2,0},{3,1},{4,2},{5,3},{6,4},{7,5},{8,14},{9,15},{10,... | collective-permute-start | bytes 196616 | tf_op jit(solution)/shard_map/ppermute | solution.py:362
  45.7 11.6 %collective-permute-start.18 = (bf16[8,128,256]{2,1,0:T(8,128)(2,1)S(1)}, bf16[8,128,256]{2,1,0:T(8,128)(2,1)S(1)}, u32[]{:S(2)}, u32[]{:S(2)}) collective-permute-start(bf16[8,128,256]{2,1,0:T(8,128)(2,1)S(1)} %bitcast_dynamic-update-slice_fusion.8.kv_same), channel_id=1, source_target_pairs={{0,128},{128,0},{1,129},{129,1},{2,130},{130,2},{3,131},{131,3},{4... | collective-permute-start | bytes 1572872 | tf_op jit(solution)/shard_map/ppermute | solution.py:54
  45.9 7.7 %collective-permute-start.3 = (bf16[4,256,128]{2,1,0:T(8,128)(2,1)S(1)}, bf16[4,256,128]{2,1,0:T(8,128)(2,1)S(1)}, u32[]{:S(2)}, u32[]{:S(2)}) collective-permute-start(bf16[4,256,128]{2,1,0:T(8,128)(2,1)S(1)} %slice.8.x0), channel_id=1, source_target_pairs={{0,32},{8,40},{16,48},{24,56},{32,64},{40,72},{48,80},{56,88},{64,... | collective-permute-start | bytes 786440 | tf_op jit(solution)/shard_map/ppermute | solution.py:40
  46.7 10.1 %collective-permute-start.4 = (bf16[4,256,128]{2,1,0:T(8,128)(2,1)S(1)}, bf16[4,256,128]{2,1,0:T(8,128)(2,1)S(1)}, u32[]{:S(2)}, u32[]{:S(2)}) collective-permute-start(bf16[4,256,128]{2,1,0:T(8,128)(2,1)S(1)} %slice.8.x0), channel_id=1, source_target_pairs={{0,64},{8,72},{16,80},{24,88},{32,96},{40,104},{48,112},{56,120},{... | collective-permute-start | bytes 786440 | tf_op jit(solution)/shard_map/ppermute | solution.py:40
  49.6 7.7 %collective-permute-start.5 = (bf16[4,256,128]{2,1,0:T(8,128)(2,1)S(1)}, bf16[4,256,128]{2,1,0:T(8,128)(2,1)S(1)}, u32[]{:S(2)}, u32[]{:S(2)}) collective-permute-start(bf16[4,256,128]{2,1,0:T(8,128)(2,1)S(1)} %slice.8.x0), channel_id=1, source_target_pairs={{0,96},{8,104},{16,112},{24,120},{32,0},{40,8},{48,16},{56,24},{64... | collective-permute-start | bytes 786440 | tf_op jit(solution)/shard_map/ppermute | solution.py:40
  61.7 11.5 %collective-permute-start.29 = (bf16[128,256]{1,0:T(8,128)(2,1)S(1)}, bf16[128,256]{1,0:T(8,128)(2,1)S(1)}, u32[]{:S(2)}, u32[]{:S(2)}) collective-permute-start(bf16[128,256]{1,0:T(8,128)(2,1)S(1)} %get-tuple-element.24), channel_id=1, source_target_pairs={{0,1},{1,2},{2,3},{3,4},{4,5},{5,6},{6,7},{7,0},{8,9},{9,10},{10,1... | collective-permute-start | bytes 196616 | tf_op jit(solution)/shard_map/ppermute | solution.py:362
  62.9 11.8 %collective-permute-start.30 = (bf16[128,256]{1,0:T(8,128)(2,1)S(1)}, bf16[128,256]{1,0:T(8,128)(2,1)S(1)}, u32[]{:S(2)}, u32[]{:S(2)}) collective-permute-start(bf16[128,256]{1,0:T(8,128)(2,1)S(1)} %get-tuple-element.24), channel_id=1, source_target_pairs={{0,2},{1,3},{2,4},{3,5},{4,6},{5,7},{6,0},{7,1},{8,10},{9,11},{10,... | collective-permute-start | bytes 196616 | tf_op jit(solution)/shard_map/ppermute | solution.py:362
  64.9 10.9 %collective-permute-start.31 = (bf16[128,256]{1,0:T(8,128)(2,1)S(1)}, bf16[128,256]{1,0:T(8,128)(2,1)S(1)}, u32[]{:S(2)}, u32[]{:S(2)}) collective-permute-start(bf16[128,256]{1,0:T(8,128)(2,1)S(1)} %get-tuple-element.24), channel_id=1, source_target_pairs={{0,3},{1,4},{2,5},{3,6},{4,7},{5,0},{6,1},{7,2},{8,11},{9,12},{10,... | collective-permute-start | bytes 196616 | tf_op jit(solution)/shard_map/ppermute | solution.py:362
  67.5 11.4 %collective-permute-start.32 = (bf16[128,256]{1,0:T(8,128)(2,1)S(1)}, bf16[128,256]{1,0:T(8,128)(2,1)S(1)}, u32[]{:S(2)}, u32[]{:S(2)}) collective-permute-start(bf16[128,256]{1,0:T(8,128)(2,1)S(1)} %get-tuple-element.24), channel_id=1, source_target_pairs={{0,4},{1,5},{2,6},{3,7},{4,0},{5,1},{6,2},{7,3},{8,12},{9,13},{10,... | collective-permute-start | bytes 196616 | tf_op jit(solution)/shard_map/ppermute | solution.py:362
  69.9 10.1 %collective-permute-start.33 = (bf16[128,256]{1,0:T(8,128)(2,1)S(1)}, bf16[128,256]{1,0:T(8,128)(2,1)S(1)}, u32[]{:S(2)}, u32[]{:S(2)}) collective-permute-start(bf16[128,256]{1,0:T(8,128)(2,1)S(1)} %get-tuple-element.24), channel_id=1, source_target_pairs={{0,5},{1,6},{2,7},{3,0},{4,1},{5,2},{6,3},{7,4},{8,13},{9,14},{10,... | collective-permute-start | bytes 196616 | tf_op jit(solution)/shard_map/ppermute | solution.py:362
  73.2 18.6 %collective-permute-start.34 = (bf16[128,256]{1,0:T(8,128)(2,1)S(1)}, bf16[128,256]{1,0:T(8,128)(2,1)S(1)}, u32[]{:S(2)}, u32[]{:S(2)}) collective-permute-start(bf16[128,256]{1,0:T(8,128)(2,1)S(1)} %get-tuple-element.24), channel_id=1, source_target_pairs={{0,6},{1,7},{2,0},{3,1},{4,2},{5,3},{6,4},{7,5},{8,14},{9,15},{10,... | collective-permute-start | bytes 196616 | tf_op jit(solution)/shard_map/ppermute | solution.py:362
  74.7 7.7 %collective-permute-start.20 = (bf16[4,256,128]{2,1,0:T(8,128)(2,1)S(1)}, bf16[4,256,128]{2,1,0:T(8,128)(2,1)S(1)}, u32[]{:S(2)}, u32[]{:S(2)}) collective-permute-start(bf16[4,256,128]{2,1,0:T(8,128)(2,1)S(1)} %get-tuple-element.20), channel_id=1, source_target_pairs={{0,32},{8,40},{16,48},{24,56},{32,64},{40,72},{48,80},{56,88},{64,... | collective-permute-start | bytes 786440 | tf_op jit(solution)/shard_map/ppermute | solution.py:40
  75.8 10.2 %collective-permute-start.21 = (bf16[4,256,128]{2,1,0:T(8,128)(2,1)S(1)}, bf16[4,256,128]{2,1,0:T(8,128)(2,1)S(1)}, u32[]{:S(2)}, u32[]{:S(2)}) collective-permute-start(bf16[4,256,128]{2,1,0:T(8,128)(2,1)S(1)} %get-tuple-element.21), channel_id=1, source_target_pairs={{0,64},{8,72},{16,80},{24,88},{32,96},{40,104},{48,112},{56,120},{... | collective-permute-start | bytes 786440 | tf_op jit(solution)/shard_map/ppermute | solution.py:40
  79.0 7.1 %collective-permute-start.22 = (bf16[4,256,128]{2,1,0:T(8,128)(2,1)S(1)}, bf16[4,256,128]{2,1,0:T(8,128)(2,1)S(1)}, u32[]{:S(2)}, u32[]{:S(2)}) collective-permute-start(bf16[4,256,128]{2,1,0:T(8,128)(2,1)S(1)} %get-tuple-element.22), channel_id=1, source_target_pairs={{0,96},{8,104},{16,112},{24,120},{32,0},{40,8},{48,16},{56,24},{64... | collective-permute-start | bytes 786440 | tf_op jit(solution)/shard_map/ppermute | solution.py:40
  80.0 11.9 %collective-permute-start.35 = (bf16[128,256]{1,0:T(8,128)(2,1)S(1)}, bf16[128,256]{1,0:T(8,128)(2,1)S(1)}, u32[]{:S(2)}, u32[]{:S(2)}) collective-permute-start(bf16[128,256]{1,0:T(8,128)(2,1)S(1)} %get-tuple-element.24), channel_id=1, source_target_pairs={{0,7},{1,0},{2,1},{3,2},{4,3},{5,4},{6,5},{7,6},{8,15},{9,8},{10,9... | collective-permute-start | bytes 196616 | tf_op jit(solution)/shard_map/ppermute | solution.py:362
  87.5 8.0 %collective-permute-start.24 = (bf16[4,256,128]{2,1,0:T(8,128)(2,1)S(1)}, bf16[4,256,128]{2,1,0:T(8,128)(2,1)S(1)}, u32[]{:S(2)}, u32[]{:S(2)}) collective-permute-start(bf16[4,256,128]{2,1,0:T(8,128)(2,1)S(1)} %add_convert_fusion.2), channel_id=1, source_target_pairs={{0,16},{8,24},{16,0},{24,8},{32,48},{40,56},{48,32},{56,40},{64,80... | collective-permute-start | bytes 786440 | tf_op jit(solution)/shard_map/ppermute | solution.py:36
  89.8 8.6 %collective-permute-start.25 = (bf16[4,256,128]{2,1,0:T(8,128)(2,1)S(1)}, bf16[4,256,128]{2,1,0:T(8,128)(2,1)S(1)}, u32[]{:S(2)}, u32[]{:S(2)}) collective-permute-start(bf16[4,256,128]{2,1,0:T(8,128)(2,1)S(1)} %add_convert_fusion.2), channel_id=1, source_target_pairs={{0,24},{8,0},{16,8},{24,16},{32,56},{40,32},{48,40},{56,48},{64,88... | collective-permute-start | bytes 786440 | tf_op jit(solution)/shard_map/ppermute | solution.py:36
  91.9 11.3 %collective-permute-start.36 = (bf16[8,128,256]{2,1,0:T(8,128)(2,1)S(1)}, bf16[8,128,256]{2,1,0:T(8,128)(2,1)S(1)}, u32[]{:S(2)}, u32[]{:S(2)}) collective-permute-start(bf16[8,128,256]{2,1,0:T(8,128)(2,1)S(1)} %bitcast_dynamic-update-slice_fusion.kv_same), channel_id=1, source_target_pairs={{0,128},{128,0},{1,129},{129,1},{2,130},{130,2},{3,131},{131,3},{4... | collective-permute-start | bytes 1572872 | tf_op jit(solution)/shard_map/ppermute | solution.py:54
  98.5 7.7 %collective-permute-start.26 = (bf16[4,256,128]{2,1,0:T(8,128)(2,1)S(1)}, bf16[4,256,128]{2,1,0:T(8,128)(2,1)S(1)}, u32[]{:S(2)}, u32[]{:S(2)}) collective-permute-start(bf16[4,256,128]{2,1,0:T(8,128)(2,1)S(1)} %add_convert_fusion.1.x0), channel_id=1, source_target_pairs={{0,32},{8,40},{16,48},{24,56},{32,64},{40,72},{48,80},{56,88},{64,... | collective-permute-start | bytes 786440 | tf_op jit(solution)/shard_map/ppermute | solution.py:40
  99.9 10.4 %collective-permute-start.27 = (bf16[4,256,128]{2,1,0:T(8,128)(2,1)S(1)}, bf16[4,256,128]{2,1,0:T(8,128)(2,1)S(1)}, u32[]{:S(2)}, u32[]{:S(2)}) collective-permute-start(bf16[4,256,128]{2,1,0:T(8,128)(2,1)S(1)} %add_convert_fusion.1.x0), channel_id=1, source_target_pairs={{0,64},{8,72},{16,80},{24,88},{32,96},{40,104},{48,112},{56,120},{... | collective-permute-start | bytes 786440 | tf_op jit(solution)/shard_map/ppermute | solution.py:40
  103.2 7.2 %collective-permute-start.28 = (bf16[4,256,128]{2,1,0:T(8,128)(2,1)S(1)}, bf16[4,256,128]{2,1,0:T(8,128)(2,1)S(1)}, u32[]{:S(2)}, u32[]{:S(2)}) collective-permute-start(bf16[4,256,128]{2,1,0:T(8,128)(2,1)S(1)} %add_convert_fusion.1.x0), channel_id=1, source_target_pairs={{0,96},{8,104},{16,112},{24,120},{32,0},{40,8},{48,16},{56,24},{64... | collective-permute-start | bytes 786440 | tf_op jit(solution)/shard_map/ppermute | solution.py:40
  115.2 7.7 %collective-permute-start.37 = (bf16[4,256,128]{2,1,0:T(8,128)(2,1)S(1)}, bf16[4,256,128]{2,1,0:T(8,128)(2,1)S(1)}, u32[]{:S(2)}, u32[]{:S(2)}) collective-permute-start(bf16[4,256,128]{2,1,0:T(8,128)(2,1)S(1)} %get-tuple-element.26), channel_id=1, source_target_pairs={{0,32},{8,40},{16,48},{24,56},{32,64},{40,72},{48,80},{56,88},{64,... | collective-permute-start | bytes 786440 | tf_op jit(solution)/shard_map/ppermute | solution.py:40
  115.9 11.6 %collective-permute-start.38 = (bf16[4,256,128]{2,1,0:T(8,128)(2,1)S(1)}, bf16[4,256,128]{2,1,0:T(8,128)(2,1)S(1)}, u32[]{:S(2)}, u32[]{:S(2)}) collective-permute-start(bf16[4,256,128]{2,1,0:T(8,128)(2,1)S(1)} %get-tuple-element.27), channel_id=1, source_target_pairs={{0,64},{8,72},{16,80},{24,88},{32,96},{40,104},{48,112},{56,120},{... | collective-permute-start | bytes 786440 | tf_op jit(solution)/shard_map/ppermute | solution.py:40
  118.9 9.0 %collective-permute-start.39 = (bf16[4,256,128]{2,1,0:T(8,128)(2,1)S(1)}, bf16[4,256,128]{2,1,0:T(8,128)(2,1)S(1)}, u32[]{:S(2)}, u32[]{:S(2)}) collective-permute-start(bf16[4,256,128]{2,1,0:T(8,128)(2,1)S(1)} %get-tuple-element.28), channel_id=1, source_target_pairs={{0,96},{8,104},{16,112},{24,120},{32,0},{40,8},{48,16},{56,24},{64... | collective-permute-start | bytes 786440 | tf_op jit(solution)/shard_map/ppermute | solution.py:40
  (23 other events, 297.1 us)
